TPU v7x, 32 devices: a whole 2x2x4 slice. The times are simulated.
32 devices in a mesh: dp: 16 (over z, y, x), head: 2 (over core).
Axes of the slice: x: 2, y: 2, z: 4, core: 2. Of those that a mesh axis runs over, the one named last changes fastest.
Arguments:
- tokens: bfloat16 [96, 197, 768], P(('dp', 'head')), may hold values from -6 to 6
- kept_index: int32 [96, 98], P(('dp', 'head')), may hold values from 0 to 196, as said below
- kept_count: int32 [96], P(('dp', 'head')), may hold values from 49 to 98, as said below
- ln1_gain: float32 [768], replicated, may hold values from 0.5 to 1.5
- ln1_bias: float32 [768], replicated, may hold values from -1 to 1
- w_qkv: bfloat16 [3, 768, 768], P(None, None, 'head'), may hold values from -0.3125 to 0.3125
- w_proj: bfloat16 [768, 768], P('head'), may hold values from -0.875 to 0.875
- proj_bias: float32 [768], replicated, may hold values from -1 to 1
- ln2_gain: float32 [768], replicated, may hold values from 0.5 to 1.5
- ln2_bias: float32 [768], replicated, may hold values from -1 to 1
- w_fc1: bfloat16 [768, 3072], P(None, 'head'), may hold values from -0.21875 to 0.21875
- fc1_bias: float32 [3072], P('head'), may hold values from -1 to 1
- w_fc2: bfloat16 [3072, 768], P('head'), may hold values from -0.15625 to 0.15625
- fc2_bias: float32 [768], replicated, may hold values from -1 to 1
- w_router: float32 [768], replicated, may hold values from -0.4375 to 0.4375
- cotangent: bfloat16 [96, 197, 768], P(('dp', 'head')), may hold values from -6 to 6
Outputs:
- out: bfloat16 [96, 197, 768], P(('dp', 'head'))
- input_grad: bfloat16 [96, 197, 768], P(('dp', 'head'))
- ln1_gain_grad: float32 [768], replicated
- ln1_bias_grad: float32 [768], replicated
- qkv_grad: float32 [3, 768, 768], P(None, 'dp', 'head')
- proj_grad: float32 [768, 768], P('head', 'dp')
- proj_bias_grad: float32 [768], replicated
- ln2_gain_grad: float32 [768], replicated
- ln2_bias_grad: float32 [768], replicated
- fc1_grad: float32 [768, 3072], P('dp', 'head')
- fc1_bias_grad: float32 [3072], P('head')
- fc2_grad: float32 [3072, 768], P('head', 'dp')
- fc2_bias_grad: float32 [768], replicated
- router_grad: float32 [768], replicated
Inputs may be any that keep to these rules, and one draw needn't show every extreme that they name: `kept_index`: each row holds 98 distinct slot numbers of its image in ascending order; the first kept_count of them are the image's kept slots, the rest pass unchanged like the slots not named. `kept_count`: some image keeps all 98 in every draw.
All inputs are finite; a program needn't handle non-finite values.
Results may differ from a plain program's by a relative error of at most 0.012.
The roundings to bfloat16 on the way count: a program that leaves them out, or rounds other values in their place, can miss the bound.
Values may be sent and summed in bfloat16 or wider, within the bound.
No kernel may reach another device: no remote copies, remote signals or barrier semaphores. Data moves between devices by JAX's collectives and lax.ppermute only.
A program may use at most 128 MiB of HBM per device.

v0:
```python
import functools

import jax
import jax.numpy as jnp
from jax import lax
from jax.experimental import pallas as pl
from jax.experimental.pallas import tpu as pltpu
from jax.sharding import PartitionSpec as P

HEAD_DIM = 64
norm_eps = 1e-06
root_half = 0.7071067811865476
inv_root_two_pi = 0.3989422804014327
f32, bf16 = jnp.float32, jnp.bfloat16


MIB = 1024 * 1024
SIDES = 2
COST_RATE = 1_100_000_000
UNIT_BLOCK = 512


def rows_of(count):
    return -(-count // 16) * 16


def norm_stats(values):
    row_mean = jnp.mean(values, axis=-1, keepdims=True)
    centered = values - row_mean
    inv_std = lax.rsqrt(jnp.mean(centered * centered, axis=-1, keepdims=True) + norm_eps)
    return centered * inv_std, inv_std


def norm_back(grad_normed, gain, normed, inv_std):
    unit = grad_normed * gain
    return inv_std * (
        unit
        - jnp.mean(unit, axis=-1, keepdims=True)
        - normed * jnp.mean(unit * normed, axis=-1, keepdims=True)
    )


def dot(a, b, over=((1,), (0,))):
    return lax.dot_general(a, b, (over, ((), ())), preferred_element_type=f32)


def dot_turned(a, b):
    return dot(a, b, ((1,), (1,)))


def column_sum(values):
    return jnp.sum(values, axis=0, keepdims=True)


class Held:
    def __init__(self, ref, copy):
        self.ref, self.copy, self.shape = ref, copy, ref.shape

    def ready(self):
        if self.copy is not None:
            self.copy.wait()
            self.copy = None
        return self.ref

    def __getitem__(self, at):
        return self.ready()[at]


class Made:
    def __init__(self, ref, copy):
        self.ref, self.copy, self.shape, self.left = ref, copy, ref.shape, False

    def __getitem__(self, at):
        return self.ref[at]

    def __setitem__(self, at, value):
        self.ref[at] = value

    def leave(self):
        if not self.left:
            self.copy.start()
            self.left = True


class Far:
    def __init__(self, value):
        self.value = value


def call(kernel, out_shape, inputs, scalars=0, scratch=(), us=1, room=14):
    values = [x.value if isinstance(x, Far) else x for x in inputs]
    shapes = [x.value if isinstance(x, Far) else x for x in out_shape]
    far_in = [i for i, x in enumerate(inputs) if isinstance(x, Far)]
    far_out = [i for i, x in enumerate(out_shape) if isinstance(x, Far)]
    n_in, n_out = len(inputs), len(out_shape)
    near, away = pl.BlockSpec(memory_space=pltpu.VMEM), pl.BlockSpec(memory_space=pltpu.HBM)
    in_specs = [pl.BlockSpec(memory_space=pltpu.SMEM)] * scalars
    in_specs += [away if i in far_in else near for i in range(scalars, n_in)]

    def body(*refs):
        ins, outs, refs = list(refs[:n_in]), list(refs[n_in : n_in + n_out]), refs[n_in + n_out :]
        in_refs, refs = refs[: len(far_in)], refs[len(far_in) :]
        out_refs, refs = refs[: len(far_out)], refs[len(far_out) :]
        sems, extra = (refs[0], refs[1:]) if far_in or far_out else (None, refs)
        for n, i in enumerate(far_in):
            copy = pltpu.make_async_copy(ins[i], in_refs[n], sems.at[n])
            copy.start()
            ins[i] = Held(in_refs[n], copy)
        for n, i in enumerate(far_out):
            copy = pltpu.make_async_copy(out_refs[n], outs[i], sems.at[len(far_in) + n])
            outs[i] = Made(out_refs[n], copy)
        kernel(*ins, *outs, *extra)
        for i in far_in:
            ins[i].ready()
        for i in far_out:
            outs[i].leave()
        for i in far_out:
            outs[i].copy.wait()

    moved = sum(i.size * i.dtype.itemsize for i in values)
    moved += sum(o.size * o.dtype.itemsize for o in shapes)
    far_scratch = [pltpu.VMEM(values[i].shape, values[i].dtype) for i in far_in]
    far_scratch += [pltpu.VMEM(shapes[i].shape, shapes[i].dtype) for i in far_out]
    if far_scratch:
        far_scratch.append(pltpu.SemaphoreType.DMA((len(far_in) + len(far_out),)))
    values = [
        x if i < scalars else pltpu.with_memory_space_constraint(x, pltpu.HBM if i in far_in else pltpu.VMEM)
        for i, x in enumerate(values)
    ]
    return pl.pallas_call(
        body,
        out_shape=[
            (pltpu.HBM if i in far_out else pltpu.VMEM)(o.shape, o.dtype)
            for i, o in enumerate(shapes)
        ],
        in_specs=in_specs,
        out_specs=[away if i in far_out else near for i in range(n_out)],
        scratch_shapes=[*far_scratch, *scratch],
        compiler_params=pltpu.CompilerParams(vmem_limit_bytes=room * MIB),
        cost_estimate=pl.CostEstimate(flops=us * COST_RATE, bytes_accessed=moved, transcendentals=0),
    )(*values)


def line(ref):
    return ref[...].reshape(1, -1)


def shape(dims, kind):
    return jax.ShapeDtypeStruct(dims, kind)


def live_column(count_ref, images, padded):
    rows = lax.broadcasted_iota(jnp.int32, (padded, 1), 0)
    return jnp.concatenate(
        [jnp.where(rows < count_ref[b], 1.0, 0.0).astype(f32) for b in range(images)], axis=0
    )


def turned_hot(index_ref, padded_ref, image, slots, padded):
    wide = padded_ref[image : image + 1, :padded]
    place = lax.broadcasted_iota(jnp.int32, (slots, padded), 0)
    return jnp.where(place == wide, 1.0, 0.0).astype(bf16)


def fill_index(index_ref, padded_ref):
    padded_ref[...] = jnp.full(padded_ref.shape, -1, jnp.int32)
    padded_ref[: index_ref.shape[0], : index_ref.shape[1]] = index_ref[...]


def front_kernel(
    count_ref,
    index_ref,
    tokens_ref,
    cotangent_ref,
    router_w_ref,
    gain_ref,
    shift_ref,
    picked_ref,
    grad_picked_ref,
    first_ref,
    grad_mlp_ref,
    router_ref,
    fc2_bias_grad_ref,
    padded_ref,
):
    images, slots, _ = tokens_ref.shape
    padded = picked_ref.shape[0] // images
    fill_index(index_ref, padded_ref)
    for b in range(images):
        hot = turned_hot(index_ref, padded_ref, b, slots, padded)
        rows = slice(b * padded, (b + 1) * padded)
        picked_ref[rows, :] = dot(hot, tokens_ref[b], ((0,), (0,))).astype(bf16)
        grad_picked_ref[rows, :] = dot(hot, cotangent_ref[b], ((0,), (0,))).astype(bf16)
    picked = picked_ref[...].astype(f32)
    router = jax.nn.sigmoid(jnp.sum(picked * line(router_w_ref), axis=-1, keepdims=True))
    router_ref[...] = router
    normed, _ = norm_stats(picked)
    first_ref[...] = (normed * line(gain_ref) + line(shift_ref)).astype(bf16)
    scale = live_column(count_ref, images, padded) * router
    grad_branch = scale * grad_picked_ref[...].astype(f32)
    grad_mlp_ref[...] = grad_branch.astype(bf16)
    fc2_bias_grad_ref[...] = column_sum(grad_branch)


def stacked_heads(pair):
    lane = lax.broadcasted_iota(jnp.int32, pair.shape, 1)
    zero = jnp.zeros_like(pair)
    return jnp.concatenate(
        [jnp.where(lane < HEAD_DIM, pair, zero), jnp.where(lane < HEAD_DIM, zero, pair)], axis=0
    )


def joined_heads(stacked):
    half = stacked.shape[0] // 2
    lane = lax.broadcasted_iota(jnp.int32, (half, stacked.shape[1]), 1)
    return jnp.where(lane < HEAD_DIM, stacked[:half], stacked[half:])


def pair_probs(queries, keys, count):
    scores = dot_turned(queries, keys) * HEAD_DIM ** (-0.5)
    lane = lax.broadcasted_iota(jnp.int32, scores.shape, 1)
    scores = jnp.where(lane < count, scores, -1e30)
    raised = jnp.exp(scores - jnp.max(scores, axis=-1, keepdims=True))
    return raised * (1.0 / jnp.sum(raised, axis=-1, keepdims=True))


def attention_kernel(
    count_ref,
    first_ref,
    qkv_own_ref,
    qkv_other_ref,
    proj_own_ref,
    proj_other_ref,
    picked_ref,
    proj_bias_ref,
    gain_ref,
    shift_ref,
    made_own_ref,
    made_other_ref,
    mixed_own_ref,
    mixed_other_ref,
    attention_ref,
    second_ref,
):
    images = count_ref.shape[0]
    padded = first_ref.shape[0] // images
    local = qkv_own_ref.shape[2]
    total = line(proj_bias_ref)
    for side in range(SIDES):
        w_ref = (qkv_own_ref, qkv_other_ref)[side]
        made_ref = (made_own_ref, made_other_ref)[side]
        mixed_ref = (mixed_own_ref, mixed_other_ref)[side]
        for t in range(3):
            made_ref[:, t * local : (t + 1) * local] = dot(first_ref[...], w_ref[t]).astype(
                bf16
            )
        for b in range(images):
            rows = slice(b * padded, (b + 1) * padded)
            for at in range(0, local, 2 * HEAD_DIM):
                q, k, v = (
                    made_ref[rows, t * local + at : t * local + at + 2 * HEAD_DIM]
                    for t in range(3)
                )
                probs = pair_probs(stacked_heads(q), k, count_ref[b]).astype(bf16)
                mixed_ref[rows, at : at + 2 * HEAD_DIM] = joined_heads(dot(probs, v)).astype(bf16)
        total = total + dot(mixed_ref[...], (proj_own_ref, proj_other_ref)[side][...])
    attention_ref[...] = total
    normed, _ = norm_stats(picked_ref[...].astype(f32) + total)
    second_ref[...] = (normed * line(gain_ref) + line(shift_ref)).astype(bf16)


def mlp_kernel(second_ref, w_fc1_ref, bias_ref, grad_mlp_ref, w_fc2_ref, *refs):
    begin_refs, (both_ref, unit_sum_ref, mlp_ref, grad_second_ref) = refs[:-4], refs[-4:]
    units = w_fc1_ref.shape[1]
    for at in range(0, units, UNIT_BLOCK):
        block = slice(at, at + UNIT_BLOCK)
        pre = dot(second_ref[...], w_fc1_ref[:, block]) + bias_ref[block].reshape(1, -1)
        half = 0.5 * (1.0 + lax.erf(pre * root_half))
        act = (pre * half).astype(bf16)
        both_ref[0, :, block] = act
        slope = half + pre * inv_root_two_pi * jnp.exp(-0.5 * pre * pre)
        grad_pre = dot_turned(grad_mlp_ref[...], w_fc2_ref[block, :]) * slope
        unit_sum_ref[block] = column_sum(grad_pre).reshape(UNIT_BLOCK)
        both_ref[1, :, block] = grad_pre.astype(bf16)
    mlp_out = dot(both_ref[0], w_fc2_ref[...])
    grad_second = dot_turned(both_ref[1], w_fc1_ref[...])
    if len(begin_refs) == 1:
        mlp_ref[...] = mlp_out + line(begin_refs[0])
        grad_second_ref[...] = grad_second
    else:
        mlp_ref[...] = mlp_out + begin_refs[0][...]
        grad_second_ref[...] = grad_second + begin_refs[1][...]


def mlp(second, grad_mlp, w_fc1, bias, w_fc2, begin):
    rows, width = second.shape
    units = (w_fc1.value if isinstance(w_fc1, Far) else w_fc1).shape[1]
    return call(
        mlp_kernel,
        [
            shape((2, rows, units), bf16),
            shape((units,), f32),
            shape((rows, width), f32),
            shape((rows, width), f32),
        ],
        (second, w_fc1, bias, grad_mlp, w_fc2, *begin),
        us=6,
    )


TOP_BITS = 4
UNITS = 1 << TOP_BITS


def my_bits():
    place = lax.axis_index("dp") >> (lax.axis_size("dp").bit_length() - 1 - TOP_BITS)
    return [(place >> bit) & 1 for bit in range(TOP_BITS)]


def order_of(part):
    return [(part + j) % 3 for j in range(3)] + [3]


def bits_left(part, step):
    return [bit for bit in range(TOP_BITS - 1, -1, -1) if bit not in order_of(part)[:step]]


def unit_rows(ref, spread, chosen, unit):
    place = 0
    for bit in spread:
        place = place * 2 + chosen[bit]
    return ref[pl.ds(pl.multiple_of(place * unit, 16), unit), :]


def every_choice(bits):
    for j in range(1 << len(bits)):
        yield j, {bit: (j >> (len(bits) - 1 - i)) & 1 for i, bit in enumerate(bits)}


def arrange_rows(turned_ref, mine, part, arranged_ref):
    unit = turned_ref.shape[0] // UNITS
    bit = order_of(part)[0]
    for side, value in enumerate((1 - mine[bit], mine[bit])):
        for j, chosen in every_choice(bits_left(part, 1)):
            chosen[bit] = value
            to = (side * UNITS // 2 + j) * unit
            arranged_ref[to : to + unit, :] = unit_rows(
                turned_ref, bits_left(part, 0), chosen, unit
            )


def term_sum(terms, part, chosen, unit):
    total = 0.0
    for n, ref in enumerate(terms):
        total = total + unit_rows(ref, bits_left(part, max(n, 1)), chosen, unit).astype(f32)
    return total


def step_kernel(step, unit, *refs):
    mine = my_bits()
    for part in range(3):
        terms = refs[part * (step + 1) : (part + 1) * (step + 1)]
        outs = refs[3 * (step + 1) :]
        order = order_of(part)
        for j, chosen in every_choice(bits_left(part, step + 1)):
            for bit in order[1:step]:
                chosen[bit] = mine[bit]
            chosen[order[step]] = 1 - mine[order[step]]
            value = term_sum(terms, part, chosen, unit).astype(bf16)
            if len(outs) == 1:
                outs[0][part * unit : (part + 1) * unit, :] = value
            else:
                outs[part][j * unit : (j + 1) * unit, :] = value


def joined_sums(refs, unit):
    mine = my_bits()
    last = refs[3 * TOP_BITS]
    for part in range(3):
        terms = refs[part * TOP_BITS : (part + 1) * TOP_BITS]
        chosen = {bit: mine[bit] for bit in range(TOP_BITS)}
        total = term_sum(terms, part, chosen, unit)
        yield part, total + last[part * unit : (part + 1) * unit, :].astype(f32)


def mlp_finish_kernel(*refs):
    fc2_ref, fc1_ref = refs[-2:]
    for part, total in joined_sums(refs, fc1_ref.shape[0]):
        at = slice(part * UNIT_BLOCK, (part + 1) * UNIT_BLOCK)
        fc2_ref[:, at] = total[:, :UNIT_BLOCK]
        fc1_ref[:, at] = total[:, UNIT_BLOCK:]


def attn_finish_kernel(*refs):
    qkv_ref, proj_ref = refs[-2:]
    local = qkv_ref.shape[2]
    third = local // 3
    for part, total in joined_sums(refs, proj_ref.shape[0]):
        qkv_ref[part] = total[:, :local]
        proj_ref[:, part * third : (part + 1) * third] = total[:, local:]


def both_rows(own, other):
    return jnp.concatenate([own, other], axis=0)


def weight_tile(arranged_ref, right, away_ref, kept_ref, columns):
    half = away_ref.shape[0]
    away_ref[:, columns] = dot(arranged_ref[:half, :], right).astype(bf16)
    kept_ref[:, columns] = dot(arranged_ref[half:, :], right)


def mlp_weights_kernel(
    grad_mlp_own_ref,
    grad_mlp_par_ref,
    second_own_ref,
    second_par_ref,
    both_own_ref,
    both_par_ref,
    *outs,
):
    away_refs, kept_refs, (turned_ref, arranged_ref) = outs[:3], outs[3:6], outs[6:]
    mine = my_bits()
    for which, (own_ref, par_ref) in enumerate(
        ((grad_mlp_own_ref, grad_mlp_par_ref), (second_own_ref, second_par_ref))
    ):
        turned_ref[...] = both_rows(own_ref[...], par_ref[...]).T
        for part in range(3):
            at = slice(part * UNIT_BLOCK, (part + 1) * UNIT_BLOCK)
            right = both_rows(both_own_ref[which, :, at], both_par_ref[which, :, at])
            arrange_rows(turned_ref, mine, part, arranged_ref)
            columns = slice(which * UNIT_BLOCK, (which + 1) * UNIT_BLOCK)
            weight_tile(arranged_ref, right, away_refs[part], kept_refs[part], columns)


def attn_weights_kernel(
    first_own_ref,
    first_par_ref,
    grad_attn_own_ref,
    grad_attn_par_ref,
    qkv_own_ref,
    qkv_par_ref,
    mixed_own_ref,
    mixed_par_ref,
    *outs,
):
    away_refs, kept_refs, (turned_ref, arranged_ref) = outs[:3], outs[3:6], outs[6:]
    mine = my_bits()
    local = mixed_own_ref.shape[1]
    third = local // 3
    turned_ref[...] = both_rows(first_own_ref[...], first_par_ref[...]).T
    for part in range(3):
        at = slice(part * local, (part + 1) * local)
        right = both_rows(qkv_own_ref[:, at], qkv_par_ref[:, at])
        arrange_rows(turned_ref, mine, part, arranged_ref)
        weight_tile(arranged_ref, right, away_refs[part], kept_refs[part], slice(0, local))
    turned_ref[...] = both_rows(grad_attn_own_ref[...], grad_attn_par_ref[...]).T
    for part in range(3):
        at = slice(part * third, (part + 1) * third)
        right = both_rows(mixed_own_ref[:, at], mixed_par_ref[:, at])
        arrange_rows(turned_ref, mine, part, arranged_ref)
        weight_tile(
            arranged_ref, right, away_refs[part], kept_refs[part], slice(local, local + third)
        )


def weights(kernel, arrays, width, depth, columns, us):
    half = width // 2
    return call(
        kernel,
        [shape((half, columns), bf16)] * 3 + [shape((half, columns), f32)] * 3,
        arrays,
        scratch=[pltpu.VMEM((width, depth), bf16), pltpu.VMEM((width, depth), bf16)],
        us=us,
    )


def small_finish_kernel(left_ref, right_ref, *outs):
    total = left_ref[...] + right_ref[...]
    width = total.shape[1]
    for i, out_ref in enumerate(outs[:-1]):
        out_ref[...] = total[i : i + 1, :].reshape(width)
    for i in range(total.shape[0] - 7):
        outs[-1][i * width : (i + 1) * width] = total[7 + i : 8 + i, :].reshape(width)


def heads_back(count_ref, grad_attn_ref, proj_ref, made_ref, out_ref, mixed_scratch):
    images = count_ref.shape[0]
    padded = made_ref.shape[0] // images
    local = proj_ref.shape[0]
    factor = HEAD_DIM ** (-0.5)
    mixed_scratch[...] = dot_turned(grad_attn_ref[...], proj_ref[...]).astype(bf16)
    for b in range(images):
        rows = slice(b * padded, (b + 1) * padded)
        for at in range(0, local, 2 * HEAD_DIM):
            q, k, v = (
                made_ref[rows, t * local + at : t * local + at + 2 * HEAD_DIM] for t in range(3)
            )
            q = stacked_heads(q)
            grad_mixed = stacked_heads(mixed_scratch[rows, at : at + 2 * HEAD_DIM])
            probs = pair_probs(q, k, count_ref[b])
            grad_probs = dot_turned(grad_mixed, v)
            row_dot = jnp.sum(probs * grad_probs, axis=-1, keepdims=True)
            grad_scores = (probs * (grad_probs - row_dot)).astype(bf16)
            found = (
                joined_heads(dot(grad_scores, k)) * factor,
                dot(grad_scores, q, ((0,), (0,))) * factor,
                dot(probs.astype(bf16), grad_mixed, ((0,), (0,))),
            )
            for t in range(3):
                to = slice(t * local + at, t * local + at + 2 * HEAD_DIM)
                out_ref[rows, to] = found[t].astype(bf16)


def back_other_kernel(
    count_ref,
    grad_second_ref,
    picked_ref,
    attention_ref,
    grad_picked_ref,
    router_ref,
    gain_ref,
    made_ref,
    proj_ref,
    grad_attn_ref,
    grad_hidden_ref,
    out_ref,
    sums_ref,
    mixed_scratch,
):
    images = count_ref.shape[0]
    padded = picked_ref.shape[0] // images
    normed, inv_std = norm_stats(picked_ref[...].astype(f32) + attention_ref[...])
    grad_second = grad_second_ref[...]
    grad_hidden = norm_back(grad_second, line(gain_ref), normed, inv_std)
    grad_hidden_ref[...] = grad_hidden
    scale = live_column(count_ref, images, padded) * router_ref[...]
    grad_attention = scale * grad_picked_ref[...].astype(f32) + grad_hidden
    grad_attn_ref[...] = grad_attention.astype(bf16)
    sums_ref[0:1, :] = column_sum(grad_attention)
    sums_ref[1:2, :] = column_sum(grad_second * normed)
    sums_ref[2:3, :] = column_sum(grad_second)
    heads_back(count_ref, grad_attn_ref, proj_ref, made_ref, out_ref, mixed_scratch)


def last_kernel(
    count_ref,
    index_ref,
    tokens_ref,
    cotangent_ref,
    picked_ref,
    grad_picked_ref,
    router_ref,
    attention_ref,
    mlp_ref,
    grad_hidden_ref,
    grad_qkv_own_ref,
    grad_qkv_other_ref,
    qkv_own_ref,
    qkv_other_ref,
    gain_ref,
    router_w_ref,
    fc2_bias_grad_ref,
    back_sums_ref,
    unit_own_ref,
    unit_other_ref,
    output_ref,
    input_grad_ref,
    keep_ref,
    send_ref,
    padded_ref,
):
    images, slots, width = tokens_ref.shape
    padded = picked_ref.shape[0] // images
    local = qkv_own_ref.shape[2]
    fill_index(index_ref, padded_ref)
    grad_first = jnp.zeros(picked_ref.shape, f32)
    for side in range(SIDES):
        for t in range(3):
            grad_first = grad_first + dot_turned(
                (grad_qkv_own_ref, grad_qkv_other_ref)[side][:, t * local : (t + 1) * local],
                (qkv_own_ref, qkv_other_ref)[side][t],
            )
    picked = picked_ref[...].astype(f32)
    router = router_ref[...]
    scale = live_column(count_ref, images, padded) * router
    branch = attention_ref[...] + mlp_ref[...]
    grad_logit = (
        scale
        * (1.0 - router)
        * jnp.sum(grad_picked_ref[...].astype(f32) * branch, axis=-1, keepdims=True)
    )
    normed, inv_std = norm_stats(picked)
    grad_kept = (
        norm_back(grad_first, line(gain_ref), normed, inv_std)
        + grad_hidden_ref[...]
        + grad_logit * line(router_w_ref)
    )
    sums = (
        column_sum(grad_first * normed),
        column_sum(grad_first),
        back_sums_ref[0:1, :],
        back_sums_ref[1:2, :],
        back_sums_ref[2:3, :],
        fc2_bias_grad_ref[...],
        column_sum(grad_logit * picked),
    )
    for i, values in enumerate(sums):
        keep_ref[i : i + 1, :] = values
        send_ref[i : i + 1, :] = values
    for i in range(unit_own_ref.shape[0] // width):
        at = slice(i * width, (i + 1) * width)
        keep_ref[7 + i : 8 + i, :] = unit_own_ref[at].reshape(1, width)
        send_ref[7 + i : 8 + i, :] = unit_other_ref[at].reshape(1, width)
    for update, base_ref, out_ref in (
        (scale * branch, tokens_ref, output_ref),
        (grad_kept, cotangent_ref, input_grad_ref),
    ):
        high = update.astype(bf16)
        low = (update - high.astype(f32)).astype(bf16)
        for b in range(images):
            hot = turned_hot(index_ref, padded_ref, b, slots, padded)
            rows = slice(b * padded, (b + 1) * padded)
            updated = base_ref[b].astype(f32) + (dot(hot, high[rows]) + dot(hot, low[rows]))
            out_ref[b] = updated.astype(bf16)
        out_ref.leave()


def other_core(value):
    return lax.ppermute(value, "head", [(0, 1), (1, 0)])


def partners(count, bit):
    return [(i, i ^ (1 << bit)) for i in range(count)]


class Halving:
    def __init__(self, halves, count):
        self.shift, self.count = count.bit_length() - 1 - TOP_BITS, count
        self.unit = halves[0].shape[0] * 2 // UNITS
        self.columns = halves[0].shape[1]
        self.terms = [[kept] for kept in halves[3:]]
        self.away, self.step, self.last = list(halves[:3]), 0, None

    def swap(self, part):
        bit = order_of(part)[self.step] + self.shift
        return partners(self.count, bit)

    def send(self):
        if self.step == 3:
            self.last = lax.ppermute(self.away[0], "dp", self.swap(0))
        else:
            for part in range(3):
                got = lax.ppermute(self.away[part], "dp", self.swap(part))
                self.terms[part].append(got)
        self.step += 1

    def flat(self):
        return tuple(term for terms in self.terms for term in terms)

    def next(self, after):
        flat, after = lax.optimization_barrier((self.flat(), after))
        rows = self.unit * UNITS >> (self.step + 1)
        outs = [shape((rows, self.columns), bf16)] * 3
        if self.step == 3:
            outs = [shape((3 * self.unit, self.columns), bf16)]
        self.away = call(
            functools.partial(step_kernel, self.step, self.unit), outs, flat, us=1
        )
        self.away, after = lax.optimization_barrier((self.away, after))
        self.send()
        return after

    def finish(self, kernel, outs):
        return call(kernel, [Far(out) for out in outs], (*self.flat(), self.last), us=1)


def fewer_rows(grad, count, axis):
    place = lax.axis_index("dp")
    for bit in range(count.bit_length() - 2 - TOP_BITS, -1, -1):
        half = grad.shape[axis] // 2
        mine = (place >> bit) & 1
        away = lax.dynamic_slice_in_dim(grad, (1 - mine) * half, half, axis).astype(bf16)
        kept = lax.dynamic_slice_in_dim(grad, mine * half, half, axis)
        grad = kept + lax.ppermute(away, "dp", partners(count, bit)).astype(f32)
    return grad


def on_device(
    tokens,
    kept_index,
    kept_count,
    ln1_gain,
    ln1_bias,
    w_qkv,
    w_proj,
    proj_bias,
    ln2_gain,
    ln2_bias,
    w_fc1,
    fc1_bias,
    w_fc2,
    fc2_bias,
    w_router,
    cotangent,
):
    images, slots, width = tokens.shape
    padded = rows_of(kept_index.shape[1])
    rows = images * padded
    local = w_qkv.shape[2]
    units = w_fc1.shape[1]
    count = lax.axis_size("dp")

    w_qkv_other = other_core(w_qkv)
    w_proj_other = other_core(w_proj)
    w_fc1_other = other_core(w_fc1)
    bias_other = other_core(fc1_bias)
    w_fc2_other = other_core(w_fc2)
    index_scratch = pltpu.VMEM((8, 128), jnp.int32)

    picked, grad_picked, first, grad_mlp, router, fc2_bias_sum = call(
        front_kernel,
        [
            shape((rows, width), bf16),
            shape((rows, width), bf16),
            shape((rows, width), bf16),
            shape((rows, width), bf16),
            shape((rows, 1), f32),
            shape((1, width), f32),
        ],
        (kept_count, Far(kept_index), Far(tokens), Far(cotangent), Far(w_router), Far(ln1_gain), Far(ln1_bias)),
        scalars=1,
        scratch=[index_scratch],
        us=3,
    )
    first_par = other_core(first)
    grad_mlp_par = other_core(grad_mlp)

    made, made_other, mixed, mixed_other, attention, second = call(
        attention_kernel,
        [
            shape((rows, 3 * local), bf16),
            shape((rows, 3 * local), bf16),
            shape((rows, local), bf16),
            shape((rows, local), bf16),
            shape((rows, width), f32),
            shape((rows, width), bf16),
        ],
        (
            kept_count,
            first,
            Far(w_qkv),
            w_qkv_other,
            Far(w_proj),
            w_proj_other,
            picked,
            Far(proj_bias),
            Far(ln2_gain),
            Far(ln2_bias),
        ),
        scalars=1,
        us=7,
    )
    mixed_par = other_core(mixed_other)
    second_par = other_core(second)

    both_other, unit_other, mlp_out, grad_second = mlp(
        second, grad_mlp, w_fc1_other, bias_other, w_fc2_other, (Far(fc2_bias),)
    )
    both_par = other_core(both_other)
    both_own, unit_own, mlp_out, grad_second = mlp(
        second, grad_mlp, Far(w_fc1), Far(fc1_bias), Far(w_fc2), (mlp_out, grad_second)
    )
    mlp_halves = weights(
        mlp_weights_kernel,
        (grad_mlp, grad_mlp_par, second, second_par, both_own, both_par),
        width,
        2 * rows,
        2 * UNIT_BLOCK,
        8,
    )
    mlp_halves, grad_second = lax.optimization_barrier((mlp_halves, grad_second))
    mlp_sums = Halving(mlp_halves, count)
    mlp_sums.send()

    grad_attn, grad_hidden, grad_qkv_other, back_sums = call(
        back_other_kernel,
        [
            shape((rows, width), bf16),
            shape((rows, width), f32),
            shape((rows, 3 * local), bf16),
            shape((8, width), f32),
        ],
        (
            kept_count,
            grad_second,
            picked,
            attention,
            grad_picked,
            router,
            Far(ln2_gain),
            made_other,
            w_proj_other,
        ),
        scalars=1,
        scratch=[pltpu.VMEM((rows, local), bf16)],
        us=7,
    )
    grad_attn_par = other_core(grad_attn)
    grad_qkv_par = other_core(grad_qkv_other)
    (grad_qkv,) = call(
        heads_back,
        [shape((rows, 3 * local), bf16)],
        (kept_count, grad_attn, Far(w_proj), made),
        scalars=1,
        scratch=[pltpu.VMEM((rows, local), bf16)],
        us=6,
    )
    grad_qkv = mlp_sums.next(grad_qkv)
    attn_halves = weights(
        attn_weights_kernel,
        (first, first_par, grad_attn, grad_attn_par, grad_qkv, grad_qkv_par, mixed, mixed_par),
        width,
        2 * rows,
        local + local // 3,
        5,
    )
    attn_halves, grad_qkv = lax.optimization_barrier((attn_halves, grad_qkv))
    attn_sums = Halving(attn_halves, count)
    attn_sums.send()

    sum_rows = 7 + units // width
    output, input_grad, keep, send = call(
        last_kernel,
        [
            Far(shape(tokens.shape, bf16)),
            Far(shape(tokens.shape, bf16)),
            shape((sum_rows, width), f32),
            shape((sum_rows, width), f32),
        ],
        (
            kept_count,
            Far(kept_index),
            Far(tokens),
            Far(cotangent),
            picked,
            grad_picked,
            router,
            attention,
            mlp_out,
            grad_hidden,
            grad_qkv,
            grad_qkv_other,
            Far(w_qkv),
            w_qkv_other,
            Far(ln1_gain),
            Far(w_router),
            fc2_bias_sum,
            back_sums,
            unit_own,
            unit_other,
        ),
        scalars=1,
        scratch=[index_scratch],
        us=7,
    )
    keep = mlp_sums.next(keep)
    keep = attn_sums.next(keep)
    keep = mlp_sums.next(keep)
    keep = attn_sums.next(keep)
    keep = attn_sums.next(keep)
    small = keep + other_core(send)
    steps = count.bit_length() - 1
    for bit in range(steps - 1):
        small = small + lax.ppermute(small, "dp", partners(count, bit))
    sums = call(
        small_finish_kernel,
        [Far(shape((width,), f32))] * 7 + [Far(shape((units,), f32))],
        (small, lax.ppermute(small, "dp", partners(count, steps - 1))),
    )
    unit = width // UNITS
    fc2_turned, fc1_grad = mlp_sums.finish(
        mlp_finish_kernel, [shape((unit, units), f32), shape((unit, units), f32)]
    )
    qkv_grad, proj_turned = attn_sums.finish(
        attn_finish_kernel, [shape((3, unit, local), f32), shape((unit, local), f32)]
    )
    fc2_turned, fc1_grad, proj_turned = (
        fewer_rows(grad, count, 0) for grad in (fc2_turned, fc1_grad, proj_turned)
    )
    qkv_grad = fewer_rows(qkv_grad, count, 1)
    return (
        output,
        input_grad,
        sums[0],
        sums[1],
        qkv_grad,
        proj_turned.T,
        sums[2],
        sums[3],
        sums[4],
        fc1_grad,
        sums[7],
        fc2_turned.T,
        sums[5],
        sums[6],
    )


def solution(mesh):
    batch = ("dp", "head")
    return jax.shard_map(
        on_device,
        mesh=mesh,
        in_specs=(
            P(batch, None, None),
            P(batch, None),
            P(batch),
            P(),
            P(),
            P(None, None, "head"),
            P("head", None),
            P(),
            P(),
            P(),
            P(None, "head"),
            P("head"),
            P("head", None),
            P(),
            P(),
            P(batch, None, None),
        ),
        out_specs=(
            P(batch, None, None),
            P(batch, None, None),
            P(),
            P(),
            P(None, "dp", "head"),
            P("head", "dp"),
            P(),
            P(),
            P(),
            P("dp", "head"),
            P("head"),
            P("head", "dp"),
            P(),
            P(),
        ),
        check_vma=False,
    )
```

profile of v0, /device:TPU:0, one launch (start us, length us, event | category | flops | bytes accessed | tf_op | source)
XLA Modules:
  0.0 133.1 jit_solution(11322824233835481206)
XLA Ops:
  2.8 3.3 %shard_map.263 = (bf16[336,768]{1,0:T(8,128)(2,1)S(1)}, bf16[336,768]{1,0:T(8,128)(2,1)S(1)}, bf16[336,768]{1,0:T(8,128)(2,1)S(1)}, bf16[336,768]{1,0:T(8,128)(2...) custom-call(s32[3]{0:T(128)S(1)} %copy-done, s32[3,98]{1,0:T(4,128)} %refs_1_.5, bf16[3,197,768]{2,1,0:T(8,128)(2,1)} %refs_2_.9, ...), custom_call_target="tpu_custom_call" | custom-call | flops 3300000000 | bytes 3894756 | tf_op jit(solution)/shard_map/pallas_call | solution.py:130
  6.1 6.1 %collective-permute-done.1.refs_5_.refs_8_ = bf16[384,768]{1,0:T(8,128)(2,1)S(1)} collective-permute-done((bf16[384,768]{1,0:T(8,128)(2,1)}, bf16[384,768]{1,0:T(8,128)(2,1)S(1)}, u32[]{:S(2)}, u32[]{:S(2)}) %collective-permute-start.1) | collective-permute-done | bytes 589856 | tf_op jit(solution)/shard_map/ppermute | solution.py:630
  12.3 7.0 %shard_map.264 = (bf16[336,1152]{1,0:T(8,128)(2,1)S(1)}, bf16[336,1152]{1,0:T(8,128)(2,1)S(1)}, bf16[336,384]{1,0:T(8,128)(2,1)S(1)}, bf16[336,384]{1,0:T(8,128)...) custom-call(s32[3]{0:T(128)S(1)} %copy-done, bf16[336,768]{1,0:T(8,128)(2,1)S(1)} %get-tuple-element.175.refs_1_.refs_0_, ...), custom_call_target="tpu_custom_call" | custom-call | flops 7699999744 | bytes 9372684 | tf_op jit(solution)/shard_map/pallas_call | solution.py:130
  19.3 5.0 %shard_map.265 = (bf16[2,336,1536]{2,1,0:T(8,128)(2,1)S(1)}, f32[1536]{0:T(1024)S(1)}, f32[336,768]{1,0:T(8,128)S(1)}, f32[336,768]{1,0:T(8,128)S(1)}) custom-call(bf16[336,768]{1,0:T(8,128)(2,1)S(1)} %get-tuple-element.177.refs_0_.refs_2_, bf16[768,1536]{1,0:T(8,128)(2,1)S(1)} %collective-permute-done.2.refs_1_, f32[1536]{0:T(1024)S(1)} %collective-permute-done.3.refs_2_, ...), custom_call_target="tpu_custom_call" | custom-call | flops 6600000000 | bytes 9894912 | tf_op jit(solution)/shard_map/pallas_call | solution.py:130
  25.3 6.0 %shard_map.266 = (bf16[2,336,1536]{2,1,0:T(8,128)(2,1)S(1)}, f32[1536]{0:T(1024)S(1)}, f32[336,768]{1,0:T(8,128)S(1)}, f32[336,768]{1,0:T(8,128)S(1)}) custom-call(bf16[336,768]{1,0:T(8,128)(2,1)S(1)} %get-tuple-element.177.refs_0_.refs_2_, bf16[768,1536]{1,0:T(8,128)(2,1)} %refs_1_.4, f32[1536]{0:T(1024)} %refs_2_.7, ...), custom_call_target="tpu_custom_call" | custom-call | flops 6600000000 | bytes 11956224 | tf_op jit(solution)/shard_map/pallas_call | solution.py:130
  31.3 4.5 %shard_map.267 = (bf16[384,1024]{1,0:T(8,128)(2,1)S(1)}, bf16[384,1024]{1,0:T(8,128)(2,1)S(1)}, bf16[384,1024]{1,0:T(8,128)(2,1)S(1)}, f32[384,1024]{1,0:T(8,128...) custom-call(bf16[336,768]{1,0:T(8,128)(2,1)S(1)} %get-tuple-element.178.refs_3_.refs_0_, ...), custom_call_target="tpu_custom_call" | custom-call | flops 8800000000 | bytes 13271040 | tf_op jit(solution)/shard_map/pallas_call | solution.py:130
  35.8 2.7 %collective-permute-start.10 = (bf16[384,1024]{1,0:T(8,128)(2,1)S(1)}, bf16[384,1024]{1,0:T(8,128)(2,1)S(1)}, u32[]{:S(2)}, u32[]{:S(2)}) collective-permute-start(bf16[384,1024]{1,0:T(8,128)(2,1)S(1)} %get-tuple-element.196), channel_id=1, source_target_pairs={{0,2},{2,0},{4,6},{6,4},{8,10},{10,8},{12,14},{14,12},{16,18},{18,... | collective-permute-start | bytes 2359304 | tf_op jit(solution)/shard_map/ppermute | solution.py:654
  41.6 6.7 %shard_map.268 = (bf16[336,768]{1,0:T(8,128)(2,1)S(1)}, f32[336,768]{1,0:T(8,128)S(1)}, bf16[336,1152]{1,0:T(8,128)(2,1)S(1)}, f32[8,768]{1,0:T(8,128)S(1)}) custom-call(s32[3]{0:T(128)S(1)} %copy-done, f32[336,768]{1,0:T(8,128)S(1)} %get-tuple-element.191.refs_1_, bf16[336,768]{1,0:T(8,128)(2,1)S(1)} %get-tuple-element.172.refs_6_.refs_2_.refs_4_, ...), custom_call_target="tpu_custom_call" | custom-call | flops 7699999744 | bytes 6811980 | tf_op jit(solution)/shard_map/pallas_call | solution.py:130
  49.0 7.7 %collective-permute-done.10.refs_1_ = bf16[384,1024]{1,0:T(8,128)(2,1)S(1)} collective-permute-done((bf16[384,1024]{1,0:T(8,128)(2,1)S(1)}, bf16[384,1024]{1,0:T(8,128)(2,1)S(1)}, u32[]{:S(2)}, u32[]{:S(2)}) %collective-permute-start.10) | collective-permute-done | bytes 786464 | tf_op jit(solution)/shard_map/ppermute | solution.py:654
  58.1 6.3 %shard_map.269.refs_4_.refs_10_ = bf16[336,1152]{1,0:T(8,128)(2,1)S(1)} custom-call(s32[3]{0:T(128)S(1)} %copy-done, bf16[336,768]{1,0:T(8,128)(2,1)S(1)} %get-tuple-element.194.refs_1_.refs_2_, bf16[384,768]{1,0:T(8,128)(2,1)} %refs_2_.8, bf16[336,1152]{1,0:T(8,128)(2,1)S(1)} %get-tuple-element.201.refs_3_), custom_call_target="tpu_custom_call" | custom-call | flops 6600000000 | bytes 2654220 | tf_op jit(solution)/shard_map/pallas_call | solution.py:130
  66.3 3.9 %shard_map.271 = (bf16[384,512]{1,0:T(8,128)(2,1)S(1)}, bf16[384,512]{1,0:T(8,128)(2,1)S(1)}, bf16[384,512]{1,0:T(8,128)(2,1)S(1)}, f32[384,512]{1,0:T(8,128)S(1...) custom-call(bf16[336,768]{1,0:T(8,128)(2,1)S(1)} %get-tuple-element.175.refs_1_.refs_0_, ...), custom_call_target="tpu_custom_call" | custom-call | flops 5500000256 | bytes 7667712 | tf_op jit(solution)/shard_map/pallas_call | solution.py:130
  70.2 1.6 %collective-permute-start.19 = (bf16[192,1024]{1,0:T(8,128)(2,1)S(1)}, bf16[192,1024]{1,0:T(8,128)(2,1)S(1)}, u32[]{:S(2)}, u32[]{:S(2)}) collective-permute-start(bf16[192,1024]{1,0:T(8,128)(2,1)S(1)} %get-tuple-element.236), channel_id=1, source_target_pairs={{0,8},{2,10},{4,12},{6,14},{8,0},{10,2},{12,4},{14,6},{16,24},{18,... | collective-permute-start | bytes 1179656 | tf_op jit(solution)/shard_map/ppermute | solution.py:654
  74.4 2.3 %collective-permute-done.18.refs_2_ = bf16[192,1024]{1,0:T(8,128)(2,1)S(1)} collective-permute-done((bf16[192,1024]{1,0:T(8,128)(2,1)S(1)}, bf16[192,1024]{1,0:T(8,128)(2,1)S(1)}, u32[]{:S(2)}, u32[]{:S(2)}) %collective-permute-start.18) | collective-permute-done | bytes 393248 | tf_op jit(solution)/shard_map/ppermute | solution.py:654
  78.2 8.9 %shard_map.272 = (bf16[3,197,768]{2,1,0:T(8,128)(2,1)}, bf16[3,197,768]{2,1,0:T(8,128)(2,1)}, f32[9,768]{1,0:T(8,128)S(1)}, f32[9,768]{1,0:T(8,128)S(1)}) custom-call(s32[3]{0:T(128)S(1)} %copy-done.1, s32[3,98]{1,0:T(4,128)} %refs_1_.5, bf16[3,197,768]{2,1,0:T(8,128)(2,1)} %refs_2_.9, bf16[3,197,768]{2,1,0:T(8,128)(2,1)} %refs_3_.3, ...), custom_call_target="tpu_custom_call" | custom-call | flops 7699999744 | bytes 12951012 | tf_op jit(solution)/shard_map/pallas_call | solution.py:130
  88.4 3.9 %collective-permute-done.15.refs_1_ = bf16[384,512]{1,0:T(8,128)(2,1)S(1)} collective-permute-done((bf16[384,512]{1,0:T(8,128)(2,1)S(1)}, bf16[384,512]{1,0:T(8,128)(2,1)S(1)}, u32[]{:S(2)}, u32[]{:S(2)}) %collective-permute-start.15) | collective-permute-done | bytes 393248 | tf_op jit(solution)/shard_map/ppermute | solution.py:654
  92.8 1.7 %collective-permute-start.21 = (bf16[192,512]{1,0:T(8,128)(2,1)S(1)}, bf16[192,512]{1,0:T(8,128)(2,1)S(1)}, u32[]{:S(2)}, u32[]{:S(2)}) collective-permute-start(bf16[192,512]{1,0:T(8,128)(2,1)S(1)} %get-tuple-element.263), channel_id=1, source_target_pairs={{0,4},{2,6},{4,0},{6,2},{8,12},{10,14},{12,8},{14,10},{16,20},{18,... | collective-permute-start | bytes 589832 | tf_op jit(solution)/shard_map/ppermute | solution.py:654
  95.4 3.8 %collective-permute-done.26.refs_11_ = bf16[96,1024]{1,0:T(8,128)(2,1)S(1)} collective-permute-done((bf16[96,1024]{1,0:T(8,128)(2,1)S(1)}, bf16[96,1024]{1,0:T(8,128)(2,1)S(1)}, u32[]{:S(2)}, u32[]{:S(2)}) %collective-permute-start.26) | collective-permute-done | bytes 196640 | tf_op jit(solution)/shard_map/ppermute | solution.py:654
  99.3 2.0 %collective-permute-done.21.refs_2_ = bf16[192,512]{1,0:T(8,128)(2,1)S(1)} collective-permute-done((bf16[192,512]{1,0:T(8,128)(2,1)S(1)}, bf16[192,512]{1,0:T(8,128)(2,1)S(1)}, u32[]{:S(2)}, u32[]{:S(2)}) %collective-permute-start.21) | collective-permute-done | bytes 196640 | tf_op jit(solution)/shard_map/ppermute | solution.py:654
  103.5 2.6 %collective-permute-done.27.refs_3_ = bf16[96,512]{1,0:T(8,128)(2,1)S(1)} collective-permute-done((bf16[96,512]{1,0:T(8,128)(2,1)S(1)}, bf16[96,512]{1,0:T(8,128)(2,1)S(1)}, u32[]{:S(2)}, u32[]{:S(2)}) %collective-permute-start.27) | collective-permute-done | bytes 98336 | tf_op jit(solution)/shard_map/ppermute | solution.py:654
  109.1 2.6 %collective-permute-start.36 = (bf16[144,1024]{1,0:T(8,128)(2,1)S(1)}, bf16[144,1024]{1,0:T(8,128)(2,1)S(1)}, u32[]{:S(2)}, u32[]{:S(2)}) collective-permute-start(bf16[144,1024]{1,0:T(8,128)(2,1)S(1)} %shard_map.275), channel_id=1, source_target_pairs={{0,16},{2,18},{4,20},{6,22},{8,24},{10,26},{12,28},{14,30},{16,0},... | collective-permute-start | bytes 884744 | tf_op jit(solution)/shard_map/ppermute | solution.py:651
  112.5 3.7 %collective-permute-done.32 = f32[9,768]{1,0:T(8,128)S(1)} collective-permute-done((f32[9,768]{1,0:T(8,128)S(1)}, f32[9,768]{1,0:T(8,128)S(1)}, u32[]{:S(2)}, u32[]{:S(2)}) %collective-permute-start.32) | collective-permute-done | bytes 27680 | tf_op jit(solution)/shard_map/ppermute | solution.py:875
  117.1 2.3 %collective-permute-start.35 = (bf16[144,512]{1,0:T(8,128)(2,1)S(1)}, bf16[144,512]{1,0:T(8,128)(2,1)S(1)}, u32[]{:S(2)}, u32[]{:S(2)}) collective-permute-start(bf16[144,512]{1,0:T(8,128)(2,1)S(1)} %shard_map.277), channel_id=1, source_target_pairs={{0,16},{2,18},{4,20},{6,22},{8,24},{10,26},{12,28},{14,30},{16,0},... | collective-permute-start | bytes 442376 | tf_op jit(solution)/shard_map/ppermute | solution.py:651
  119.4 3.2 %collective-permute-done.33 = f32[9,768]{1,0:T(8,128)S(1)} collective-permute-done((f32[9,768]{1,0:T(8,128)S(1)}, f32[9,768]{1,0:T(8,128)S(1)}, u32[]{:S(2)}, u32[]{:S(2)}) %collective-permute-start.33) | collective-permute-done | bytes 27680 | tf_op jit(solution)/shard_map/ppermute | solution.py:875
  123.0 7.5 %collective-permute-done.34.refs_1_ = f32[9,768]{1,0:T(8,128)S(1)} collective-permute-done((f32[9,768]{1,0:T(8,128)S(1)}, f32[9,768]{1,0:T(8,128)S(1)}, u32[]{:S(2)}, u32[]{:S(2)}) %collective-permute-start.34) | collective-permute-done | bytes 27680 | tf_op jit(solution)/shard_map/ppermute | solution.py:879
  (76 shorter events, 26.6 us)
Async XLA Ops:
  0.6 11.6 %collective-permute-start = (bf16[3,768,384]{2,1,0:T(8,128)(2,1)}, bf16[3,768,384]{2,1,0:T(8,128)(2,1)S(1)}, u32[]{:S(2)}, u32[]{:S(2)}) collective-permute-start(bf16[3,768,384]{2,1,0:T(8,128)(2,1)} %refs_12_.1), channel_id=1, source_target_pairs={{0,1},{1,0},{2,3},{3,2},{4,5},{5,4},{6,7},{7,6},{8,9},{9,8},{10,11... | collective-permute-start | bytes 5308424 | tf_op jit(solution)/shard_map/ppermute | solution.py:630
  1.2 18.1 %collective-permute-start.2 = (bf16[768,1536]{1,0:T(8,128)(2,1)}, bf16[768,1536]{1,0:T(8,128)(2,1)S(1)}, u32[]{:S(2)}, u32[]{:S(2)}) collective-permute-start(bf16[768,1536]{1,0:T(8,128)(2,1)} %refs_1_.4), channel_id=1, source_target_pairs={{0,1},{1,0},{2,3},{3,2},{4,5},{5,4},{6,7},{7,6},{8,9},{9,8},{10,11... | collective-permute-start | bytes 7077896 | tf_op jit(solution)/shard_map/ppermute | solution.py:630
  1.2 18.0 %collective-permute-start.4 = (bf16[1536,768]{1,0:T(8,128)(2,1)}, bf16[1536,768]{1,0:T(8,128)(2,1)S(1)}, u32[]{:S(2)}, u32[]{:S(2)}) collective-permute-start(bf16[1536,768]{1,0:T(8,128)(2,1)} %refs_4_.5), channel_id=1, source_target_pairs={{0,1},{1,0},{2,3},{3,2},{4,5},{5,4},{6,7},{7,6},{8,9},{9,8},{10,11... | collective-permute-start | bytes 7077896 | tf_op jit(solution)/shard_map/ppermute | solution.py:630
  1.7 10.6 %collective-permute-start.1 = (bf16[384,768]{1,0:T(8,128)(2,1)}, bf16[384,768]{1,0:T(8,128)(2,1)S(1)}, u32[]{:S(2)}, u32[]{:S(2)}) collective-permute-start(bf16[384,768]{1,0:T(8,128)(2,1)} %refs_2_.8), channel_id=1, source_target_pairs={{0,1},{1,0},{2,3},{3,2},{4,5},{5,4},{6,7},{7,6},{8,9},{9,8},{10,11... | collective-permute-start | bytes 1769480 | tf_op jit(solution)/shard_map/ppermute | solution.py:630
  1.8 17.5 %collective-permute-start.3 = (f32[1536]{0:T(1024)}, f32[1536]{0:T(1024)S(1)}, u32[]{:S(2)}, u32[]{:S(2)}) collective-permute-start(f32[1536]{0:T(1024)} %refs_2_.7), channel_id=1, source_target_pairs={{0,1},{1,0},{2,3},{3,2},{4,5},{5,4},{6,7},{7,6},{8,9},{9,8},{10,11... | collective-permute-start | bytes 18440 | tf_op jit(solution)/shard_map/ppermute | solution.py:630
  35.8 20.8 %collective-permute-start.10 = (bf16[384,1024]{1,0:T(8,128)(2,1)S(1)}, bf16[384,1024]{1,0:T(8,128)(2,1)S(1)}, u32[]{:S(2)}, u32[]{:S(2)}) collective-permute-start(bf16[384,1024]{1,0:T(8,128)(2,1)S(1)} %get-tuple-element.196), channel_id=1, source_target_pairs={{0,2},{2,0},{4,6},{6,4},{8,10},{10,8},{12,14},{14,12},{16,18},{18,... | collective-permute-start | bytes 2359304 | tf_op jit(solution)/shard_map/ppermute | solution.py:654
  38.6 19.5 %collective-permute-start.11 = (bf16[384,1024]{1,0:T(8,128)(2,1)S(1)}, bf16[384,1024]{1,0:T(8,128)(2,1)S(1)}, u32[]{:S(2)}, u32[]{:S(2)}) collective-permute-start(bf16[384,1024]{1,0:T(8,128)(2,1)S(1)} %get-tuple-element.198), channel_id=1, source_target_pairs={{0,4},{2,6},{4,0},{6,2},{8,12},{10,14},{12,8},{14,10},{16,20},{18,... | collective-permute-start | bytes 2359304 | tf_op jit(solution)/shard_map/ppermute | solution.py:654
  40.1 24.4 %collective-permute-start.12 = (bf16[384,1024]{1,0:T(8,128)(2,1)S(1)}, bf16[384,1024]{1,0:T(8,128)(2,1)S(1)}, u32[]{:S(2)}, u32[]{:S(2)}) collective-permute-start(bf16[384,1024]{1,0:T(8,128)(2,1)S(1)} %get-tuple-element.200), channel_id=1, source_target_pairs={{0,8},{2,10},{4,12},{6,14},{8,0},{10,2},{12,4},{14,6},{16,24},{18,... | collective-permute-start | bytes 2359304 | tf_op jit(solution)/shard_map/ppermute | solution.py:654
  48.4 17.9 %collective-permute-start.13 = (bf16[336,1152]{1,0:T(8,128)(2,1)S(1)}, bf16[336,1152]{1,0:T(8,128)(2,1)S(1)}, u32[]{:S(2)}, u32[]{:S(2)}) collective-permute-start(bf16[336,1152]{1,0:T(8,128)(2,1)S(1)} %get-tuple-element.213.refs_11_), channel_id=1, source_target_pairs={{0,1},{1,0},{2,3},{3,2},{4,5},{5,4},{6,7},{7,6},{8,9},{9,8},{10,11... | collective-permute-start | bytes 2322440 | tf_op jit(solution)/shard_map/ppermute | solution.py:630
  48.5 17.8 %collective-permute-start.8 = (bf16[336,768]{1,0:T(8,128)(2,1)S(1)}, bf16[336,768]{1,0:T(8,128)(2,1)S(1)}, u32[]{:S(2)}, u32[]{:S(2)}) collective-permute-start(bf16[336,768]{1,0:T(8,128)(2,1)S(1)} %get-tuple-element.175.refs_1_.refs_0_), channel_id=1, source_target_pairs={{0,1},{1,0},{2,3},{3,2},{4,5},{5,4},{6,7},{7,6},{8,9},{9,8},{10,11... | collective-permute-start | bytes 1548296 | tf_op jit(solution)/shard_map/ppermute | solution.py:630
  56.6 9.6 %collective-permute-start.14 = (bf16[336,384]{1,0:T(8,128)(2,1)S(1)}, bf16[336,384]{1,0:T(8,128)(2,1)S(1)}, u32[]{:S(2)}, u32[]{:S(2)}) collective-permute-start(bf16[336,384]{1,0:T(8,128)(2,1)S(1)} %get-tuple-element.215), channel_id=1, source_target_pairs={{0,1},{1,0},{2,3},{3,2},{4,5},{5,4},{6,7},{7,6},{8,9},{9,8},{10,11... | collective-permute-start | bytes 774152 | tf_op jit(solution)/shard_map/ppermute | solution.py:630
  58.1 8.2 %collective-permute-start.9 = (bf16[336,768]{1,0:T(8,128)(2,1)S(1)}, bf16[336,768]{1,0:T(8,128)(2,1)S(1)}, u32[]{:S(2)}, u32[]{:S(2)}) collective-permute-start(bf16[336,768]{1,0:T(8,128)(2,1)S(1)} %get-tuple-element.194.refs_1_.refs_2_), channel_id=1, source_target_pairs={{0,1},{1,0},{2,3},{3,2},{4,5},{5,4},{6,7},{7,6},{8,9},{9,8},{10,11... | collective-permute-start | bytes 1548296 | tf_op jit(solution)/shard_map/ppermute | solution.py:630
  64.7 12.0 %collective-permute-start.18 = (bf16[192,1024]{1,0:T(8,128)(2,1)S(1)}, bf16[192,1024]{1,0:T(8,128)(2,1)S(1)}, u32[]{:S(2)}, u32[]{:S(2)}) collective-permute-start(bf16[192,1024]{1,0:T(8,128)(2,1)S(1)} %get-tuple-element.235), channel_id=1, source_target_pairs={{0,4},{2,6},{4,0},{6,2},{8,12},{10,14},{12,8},{14,10},{16,20},{18,... | collective-permute-start | bytes 1179656 | tf_op jit(solution)/shard_map/ppermute | solution.py:654
  70.2 17.0 %collective-permute-start.19 = (bf16[192,1024]{1,0:T(8,128)(2,1)S(1)}, bf16[192,1024]{1,0:T(8,128)(2,1)S(1)}, u32[]{:S(2)}, u32[]{:S(2)}) collective-permute-start(bf16[192,1024]{1,0:T(8,128)(2,1)S(1)} %get-tuple-element.236), channel_id=1, source_target_pairs={{0,8},{2,10},{4,12},{6,14},{8,0},{10,2},{12,4},{14,6},{16,24},{18,... | collective-permute-start | bytes 1179656 | tf_op jit(solution)/shard_map/ppermute | solution.py:654
  71.8 15.3 %collective-permute-start.20 = (bf16[192,1024]{1,0:T(8,128)(2,1)S(1)}, bf16[192,1024]{1,0:T(8,128)(2,1)S(1)}, u32[]{:S(2)}, u32[]{:S(2)}) collective-permute-start(bf16[192,1024]{1,0:T(8,128)(2,1)S(1)} %get-tuple-element.237), channel_id=1, source_target_pairs={{0,2},{2,0},{4,6},{6,4},{8,10},{10,8},{12,14},{14,12},{16,18},{18,... | collective-permute-start | bytes 1179656 | tf_op jit(solution)/shard_map/ppermute | solution.py:654
  72.6 19.6 %collective-permute-start.15 = (bf16[384,512]{1,0:T(8,128)(2,1)S(1)}, bf16[384,512]{1,0:T(8,128)(2,1)S(1)}, u32[]{:S(2)}, u32[]{:S(2)}) collective-permute-start(bf16[384,512]{1,0:T(8,128)(2,1)S(1)} %get-tuple-element.230), channel_id=1, source_target_pairs={{0,2},{2,0},{4,6},{6,4},{8,10},{10,8},{12,14},{14,12},{16,18},{18,... | collective-permute-start | bytes 1179656 | tf_op jit(solution)/shard_map/ppermute | solution.py:654
  73.9 18.8 %collective-permute-start.16 = (bf16[384,512]{1,0:T(8,128)(2,1)S(1)}, bf16[384,512]{1,0:T(8,128)(2,1)S(1)}, u32[]{:S(2)}, u32[]{:S(2)}) collective-permute-start(bf16[384,512]{1,0:T(8,128)(2,1)S(1)} %get-tuple-element.232), channel_id=1, source_target_pairs={{0,4},{2,6},{4,0},{6,2},{8,12},{10,14},{12,8},{14,10},{16,20},{18,... | collective-permute-start | bytes 1179656 | tf_op jit(solution)/shard_map/ppermute | solution.py:654
  76.6 16.0 %collective-permute-start.17 = (bf16[384,512]{1,0:T(8,128)(2,1)S(1)}, bf16[384,512]{1,0:T(8,128)(2,1)S(1)}, u32[]{:S(2)}, u32[]{:S(2)}) collective-permute-start(bf16[384,512]{1,0:T(8,128)(2,1)S(1)} %get-tuple-element.234), channel_id=1, source_target_pairs={{0,8},{2,10},{4,12},{6,14},{8,0},{10,2},{12,4},{14,6},{16,24},{18,... | collective-permute-start | bytes 1179656 | tf_op jit(solution)/shard_map/ppermute | solution.py:654
  87.4 7.2 %collective-permute-start.24 = (bf16[96,1024]{1,0:T(8,128)(2,1)S(1)}, bf16[96,1024]{1,0:T(8,128)(2,1)S(1)}, u32[]{:S(2)}, u32[]{:S(2)}) collective-permute-start(bf16[96,1024]{1,0:T(8,128)(2,1)S(1)} %get-tuple-element.266), channel_id=1, source_target_pairs={{0,8},{2,10},{4,12},{6,14},{8,0},{10,2},{12,4},{14,6},{16,24},{18,... | collective-permute-start | bytes 589832 | tf_op jit(solution)/shard_map/ppermute | solution.py:654
  87.9 7.5 %collective-permute-start.25 = (bf16[96,1024]{1,0:T(8,128)(2,1)S(1)}, bf16[96,1024]{1,0:T(8,128)(2,1)S(1)}, u32[]{:S(2)}, u32[]{:S(2)}) collective-permute-start(bf16[96,1024]{1,0:T(8,128)(2,1)S(1)} %get-tuple-element.267), channel_id=1, source_target_pairs={{0,2},{2,0},{4,6},{6,4},{8,10},{10,8},{12,14},{14,12},{16,18},{18,... | collective-permute-start | bytes 589832 | tf_op jit(solution)/shard_map/ppermute | solution.py:654
  92.8 8.5 %collective-permute-start.21 = (bf16[192,512]{1,0:T(8,128)(2,1)S(1)}, bf16[192,512]{1,0:T(8,128)(2,1)S(1)}, u32[]{:S(2)}, u32[]{:S(2)}) collective-permute-start(bf16[192,512]{1,0:T(8,128)(2,1)S(1)} %get-tuple-element.263), channel_id=1, source_target_pairs={{0,4},{2,6},{4,0},{6,2},{8,12},{10,14},{12,8},{14,10},{16,20},{18,... | collective-permute-start | bytes 589832 | tf_op jit(solution)/shard_map/ppermute | solution.py:654
  109.1 22.9 %collective-permute-start.36 = (bf16[144,1024]{1,0:T(8,128)(2,1)S(1)}, bf16[144,1024]{1,0:T(8,128)(2,1)S(1)}, u32[]{:S(2)}, u32[]{:S(2)}) collective-permute-start(bf16[144,1024]{1,0:T(8,128)(2,1)S(1)} %shard_map.275), channel_id=1, source_target_pairs={{0,16},{2,18},{4,20},{6,22},{8,24},{10,26},{12,28},{14,30},{16,0},... | collective-permute-start | bytes 884744 | tf_op jit(solution)/shard_map/ppermute | solution.py:651
  117.1 14.1 %collective-permute-start.35 = (bf16[144,512]{1,0:T(8,128)(2,1)S(1)}, bf16[144,512]{1,0:T(8,128)(2,1)S(1)}, u32[]{:S(2)}, u32[]{:S(2)}) collective-permute-start(bf16[144,512]{1,0:T(8,128)(2,1)S(1)} %shard_map.277), channel_id=1, source_target_pairs={{0,16},{2,18},{4,20},{6,22},{8,24},{10,26},{12,28},{14,30},{16,0},... | collective-permute-start | bytes 442376 | tf_op jit(solution)/shard_map/ppermute | solution.py:651
  122.7 7.8 %collective-permute-start.34 = (f32[9,768]{1,0:T(8,128)S(1)}, f32[9,768]{1,0:T(8,128)S(1)}, u32[]{:S(2)}, u32[]{:S(2)}) collective-permute-start(f32[9,768]{1,0:T(8,128)S(1)} %add.15.refs_0_), channel_id=1, source_target_pairs={{0,16},{2,18},{4,20},{6,22},{8,24},{10,26},{12,28},{14,30},{16,0},... | collective-permute-start | bytes 82952 | tf_op jit(solution)/shard_map/ppermute | solution.py:879
  (15 other events, 86.0 us)
where the time goes:
time: 133 us
  Pallas kernels  54.9 us (41%)
  waiting for transfers between devices  46.2 us (35%)
  starting transfers between devices  30.2 us (23%)
    pallas_call x18, Pallas kernels, call(): pl.pallas_call(body, out_shape=[(pltpu.HBM if i in far_out else pltpu.VME...  54.9 us
    ppermute x18, waiting for transfers between devices, send(): got = lax.ppermute(self.away[part], 'dp', self.swap(part))  25.3 us
    ppermute x18, starting transfers between devices, send(): got = lax.ppermute(self.away[part], 'dp', self.swap(part))  19.3 us
    ppermute x1, waiting for transfers between devices, on_device(): lax.ppermute(small, 'dp', partners(count, steps - 1))  7.47 us
    ppermute x3, waiting for transfers between devices, on_device(): small = small + lax.ppermute(small, 'dp', partners(count, bit))  7.27 us
    ppermute x13, waiting for transfers between devices, other_core(): return lax.ppermute(value, 'head', [(0, 1), (1, 0)])  6.17 us
    ppermute x2, starting transfers between devices, send(): self.last = lax.ppermute(self.away[0], 'dp', self.swap(0))  4.91 us
    ppermute x13, starting transfers between devices, other_core(): return lax.ppermute(value, 'head', [(0, 1), (1, 0)])  3.06 us
  transfers between devices with their start and end apart: 37, of which 14 were waited for; matrix products, arithmetic and copies ran while one was open for 0% of the time, Pallas kernels for 33%

commit v1 on v0

v1 whole, which is shorter than its diff:
```python
import functools

import jax
import jax.numpy as jnp
from jax import lax
from jax.experimental import pallas as pl
from jax.experimental.pallas import tpu as pltpu
from jax.sharding import PartitionSpec as P

HEAD_DIM = 64
norm_eps = 1e-06
root_half = 0.7071067811865476
inv_root_two_pi = 0.3989422804014327
f32, bf16 = jnp.float32, jnp.bfloat16


MIB = 1024 * 1024
SIDES = 2
FLOPS = 1
UNIT_BLOCK = 512


def rows_of(count):
    return -(-count // 16) * 16


def norm_stats(values):
    row_mean = jnp.mean(values, axis=-1, keepdims=True)
    centered = values - row_mean
    inv_std = lax.rsqrt(jnp.mean(centered * centered, axis=-1, keepdims=True) + norm_eps)
    return centered * inv_std, inv_std


def norm_back(grad_normed, gain, normed, inv_std):
    unit = grad_normed * gain
    return inv_std * (
        unit
        - jnp.mean(unit, axis=-1, keepdims=True)
        - normed * jnp.mean(unit * normed, axis=-1, keepdims=True)
    )


def dot(a, b, over=((1,), (0,))):
    return lax.dot_general(a, b, (over, ((), ())), preferred_element_type=f32)


def dot_turned(a, b):
    return dot(a, b, ((1,), (1,)))


def column_sum(values):
    return jnp.sum(values, axis=0, keepdims=True)


class Held:
    def __init__(self, ref, copy):
        self.ref, self.copy, self.shape = ref, copy, ref.shape

    def ready(self):
        if self.copy is not None:
            self.copy.wait()
            self.copy = None
        return self.ref

    def __getitem__(self, at):
        return self.ready()[at]


class Made:
    def __init__(self, ref, copy):
        self.ref, self.copy, self.shape, self.left = ref, copy, ref.shape, False

    def __getitem__(self, at):
        return self.ref[at]

    def __setitem__(self, at, value):
        self.ref[at] = value

    def leave(self):
        if not self.left:
            self.copy.start()
            self.left = True


class Far:
    def __init__(self, value):
        self.value = value


def call(kernel, out_shape, inputs, scratch=(), fetch=(), room=14):
    inputs = [*inputs, *[Far(x) for x in fetch]]
    values = [x.value if isinstance(x, Far) else x for x in inputs]
    shapes = [x.value if isinstance(x, Far) else x for x in out_shape]
    shapes += [shape(x.shape, x.dtype) for x in fetch]
    n_fetch, n_in, n_out = len(fetch), len(inputs), len(shapes)
    far_in = [i for i in range(n_in - n_fetch) if isinstance(inputs[i], Far)]
    far_out = [i for i, x in enumerate(out_shape) if isinstance(x, Far)]
    near, away = pl.BlockSpec(memory_space=pltpu.VMEM), pl.BlockSpec(memory_space=pltpu.HBM)
    in_hbm = [isinstance(x, Far) for x in inputs]

    def body(*refs):
        ins, outs, refs = list(refs[:n_in]), list(refs[n_in : n_in + n_out]), refs[n_in + n_out :]
        in_refs, refs = refs[: len(far_in)], refs[len(far_in) :]
        out_refs, refs = refs[: len(far_out)], refs[len(far_out) :]
        sems, extra = (refs[0], refs[1:]) if n_sems else (None, refs)
        for n, i in enumerate(far_in):
            copy = pltpu.make_async_copy(ins[i], in_refs[n], sems.at[n])
            copy.start()
            ins[i] = Held(in_refs[n], copy)
        for n, i in enumerate(far_out):
            copy = pltpu.make_async_copy(out_refs[n], outs[i], sems.at[len(far_in) + n])
            outs[i] = Made(out_refs[n], copy)
        fetched = []
        for n in range(n_fetch):
            copy = pltpu.make_async_copy(
                ins[n_in - n_fetch + n],
                outs[n_out - n_fetch + n],
                sems.at[len(far_in) + len(far_out) + n],
            )
            copy.start()
            fetched.append(copy)
        kernel(*ins[: n_in - n_fetch], *outs[: n_out - n_fetch], *extra)
        for i in far_in:
            ins[i].ready()
        for i in far_out:
            outs[i].leave()
        for copy in fetched:
            copy.wait()
        for i in far_out:
            outs[i].copy.wait()

    def landing(x):
        return (pltpu.SMEM if x.dtype == jnp.int32 and x.ndim == 1 else pltpu.VMEM)(x.shape, x.dtype)

    far_scratch = [landing(values[i]) for i in far_in]
    far_scratch += [pltpu.VMEM(shapes[i].shape, shapes[i].dtype) for i in far_out]
    n_sems = len(far_in) + len(far_out) + n_fetch
    if n_sems:
        far_scratch.append(pltpu.SemaphoreType.DMA((n_sems,)))
    values = [
        pltpu.with_memory_space_constraint(x, pltpu.HBM if far else pltpu.VMEM)
        for x, far in zip(values, in_hbm)
    ]
    return pl.pallas_call(
        body,
        out_shape=[
            (pltpu.HBM if i in far_out else pltpu.VMEM)(o.shape, o.dtype)
            for i, o in enumerate(shapes)
        ],
        in_specs=[away if far else near for far in in_hbm],
        out_specs=[away if i in far_out else near for i in range(n_out)],
        scratch_shapes=[*far_scratch, *scratch],
        compiler_params=pltpu.CompilerParams(vmem_limit_bytes=room * MIB),
        cost_estimate=pl.CostEstimate(flops=FLOPS, bytes_accessed=1, transcendentals=0),
    )(*values)


def line(ref):
    return ref[...].reshape(1, -1)


def shape(dims, kind):
    return jax.ShapeDtypeStruct(dims, kind)


def live_column(count_ref, images, padded):
    rows = lax.broadcasted_iota(jnp.int32, (padded, 1), 0)
    return jnp.concatenate(
        [jnp.where(rows < count_ref[b], 1.0, 0.0).astype(f32) for b in range(images)], axis=0
    )


def turned_hot(index_ref, padded_ref, image, slots, padded):
    wide = padded_ref[image : image + 1, :padded]
    place = lax.broadcasted_iota(jnp.int32, (slots, padded), 0)
    return jnp.where(place == wide, 1.0, 0.0).astype(bf16)


def fill_index(index_ref, padded_ref):
    padded_ref[...] = jnp.full(padded_ref.shape, -1, jnp.int32)
    padded_ref[: index_ref.shape[0], : index_ref.shape[1]] = index_ref[...]


def pick_rows(index_ref, source_ref, rows_ref, padded_ref):
    images, slots, _ = source_ref.shape
    padded = rows_ref.shape[0] // images
    fill_index(index_ref, padded_ref)
    for b in range(images):
        hot = turned_hot(index_ref, padded_ref, b, slots, padded)
        rows = slice(b * padded, (b + 1) * padded)
        rows_ref[rows, :] = dot(hot, source_ref[b], ((0,), (0,))).astype(bf16)


def front_kernel(
    index_ref,
    tokens_ref,
    router_w_ref,
    gain_ref,
    shift_ref,
    picked_ref,
    first_ref,
    router_ref,
    padded_ref,
):
    pick_rows(index_ref, tokens_ref, picked_ref, padded_ref)
    picked = picked_ref[...].astype(f32)
    router_ref[...] = jax.nn.sigmoid(jnp.sum(picked * line(router_w_ref), axis=-1, keepdims=True))
    normed, _ = norm_stats(picked)
    first_ref[...] = (normed * line(gain_ref) + line(shift_ref)).astype(bf16)


def grad_front_kernel(
    count_ref,
    index_ref,
    cotangent_ref,
    router_ref,
    grad_picked_ref,
    grad_mlp_ref,
    fc2_bias_grad_ref,
    padded_ref,
):
    images = cotangent_ref.shape[0]
    pick_rows(index_ref, cotangent_ref, grad_picked_ref, padded_ref)
    scale = live_column(count_ref, images, router_ref.shape[0] // images) * router_ref[...]
    grad_branch = scale * grad_picked_ref[...].astype(f32)
    grad_mlp_ref[...] = grad_branch.astype(bf16)
    fc2_bias_grad_ref[...] = column_sum(grad_branch)


def stacked_heads(pair):
    lane = lax.broadcasted_iota(jnp.int32, pair.shape, 1)
    zero = jnp.zeros_like(pair)
    return jnp.concatenate(
        [jnp.where(lane < HEAD_DIM, pair, zero), jnp.where(lane < HEAD_DIM, zero, pair)], axis=0
    )


def joined_heads(stacked):
    half = stacked.shape[0] // 2
    lane = lax.broadcasted_iota(jnp.int32, (half, stacked.shape[1]), 1)
    return jnp.where(lane < HEAD_DIM, stacked[:half], stacked[half:])


def pair_probs(queries, keys, count):
    scores = dot_turned(queries, keys) * HEAD_DIM ** (-0.5)
    lane = lax.broadcasted_iota(jnp.int32, scores.shape, 1)
    scores = jnp.where(lane < count, scores, -1e30)
    raised = jnp.exp(scores - jnp.max(scores, axis=-1, keepdims=True))
    return raised * (1.0 / jnp.sum(raised, axis=-1, keepdims=True))


def attention_kernel(
    count_ref,
    first_ref,
    qkv_own_ref,
    qkv_other_ref,
    proj_own_ref,
    proj_other_ref,
    picked_ref,
    proj_bias_ref,
    gain_ref,
    shift_ref,
    made_own_ref,
    made_other_ref,
    mixed_own_ref,
    mixed_other_ref,
    attention_ref,
    second_ref,
):
    images = count_ref.shape[0]
    padded = first_ref.shape[0] // images
    local = qkv_own_ref.shape[2]
    total = line(proj_bias_ref)
    for side in range(SIDES):
        w_ref = (qkv_own_ref, qkv_other_ref)[side]
        made_ref = (made_own_ref, made_other_ref)[side]
        mixed_ref = (mixed_own_ref, mixed_other_ref)[side]
        for t in range(3):
            made_ref[:, t * local : (t + 1) * local] = dot(first_ref[...], w_ref[t]).astype(
                bf16
            )
        for b in range(images):
            rows = slice(b * padded, (b + 1) * padded)
            for at in range(0, local, 2 * HEAD_DIM):
                q, k, v = (
                    made_ref[rows, t * local + at : t * local + at + 2 * HEAD_DIM]
                    for t in range(3)
                )
                probs = pair_probs(stacked_heads(q), k, count_ref[b]).astype(bf16)
                mixed_ref[rows, at : at + 2 * HEAD_DIM] = joined_heads(dot(probs, v)).astype(bf16)
        total = total + dot(mixed_ref[...], (proj_own_ref, proj_other_ref)[side][...])
    attention_ref[...] = total
    normed, _ = norm_stats(picked_ref[...].astype(f32) + total)
    second_ref[...] = (normed * line(gain_ref) + line(shift_ref)).astype(bf16)


def hidden_kernel(second_ref, w_fc1_ref, bias_ref, act_ref, slope_ref):
    for at in range(0, act_ref.shape[1], UNIT_BLOCK):
        block = slice(at, at + UNIT_BLOCK)
        pre = dot(second_ref[...], w_fc1_ref[:, block]) + bias_ref[block].reshape(1, -1)
        half = 0.5 * (1.0 + lax.erf(pre * root_half))
        act_ref[:, block] = (pre * half).astype(bf16)
        slope_ref[:, block] = half + pre * inv_root_two_pi * jnp.exp(-0.5 * pre * pre)


def hidden_back_kernel(grad_mlp_ref, w_fc2_ref, slope_ref, grad_pre_ref, unit_sum_ref):
    for at in range(0, slope_ref.shape[1], UNIT_BLOCK):
        block = slice(at, at + UNIT_BLOCK)
        grad_pre = dot_turned(grad_mlp_ref[...], w_fc2_ref[block, :]) * slope_ref[:, block]
        unit_sum_ref[block] = column_sum(grad_pre).reshape(UNIT_BLOCK)
        grad_pre_ref[:, block] = grad_pre.astype(bf16)


TOP_BITS = 4
UNITS = 1 << TOP_BITS


def my_bits():
    place = lax.axis_index("dp") >> (lax.axis_size("dp").bit_length() - 1 - TOP_BITS)
    return [(place >> bit) & 1 for bit in range(TOP_BITS)]


def order_of(part):
    return [(part + j) % 3 for j in range(3)] + [3]


def bits_left(part, step):
    return [bit for bit in range(TOP_BITS - 1, -1, -1) if bit not in order_of(part)[:step]]


def every_choice(bits):
    for j in range(1 << len(bits)):
        yield j, {bit: (j >> (len(bits) - 1 - i)) & 1 for i, bit in enumerate(bits)}


def unit_rows(ref, spread, chosen, unit, base=0):
    place = 0
    for bit in spread:
        place = place * 2 + chosen[bit]
    return ref[pl.ds(pl.multiple_of(base + place * unit, 16), unit), :]


def arrange_rows(turned_ref, mine, part, arranged_ref):
    unit = turned_ref.shape[0] // UNITS
    bit = order_of(part)[0]
    for side, value in enumerate((1 - mine[bit], mine[bit])):
        for j, chosen in every_choice(bits_left(part, 1)):
            chosen[bit] = value
            to = (side * UNITS // 2 + j) * unit
            arranged_ref[to : to + unit, :] = unit_rows(
                turned_ref, bits_left(part, 0), chosen, unit
            )


class Stream:
    def __init__(self, part, away, kept):
        self.part, self.step, self.away, self.terms = part, 0, away, [(kept, 0, 1)]
        self.unit = kept.shape[0] * 2 // UNITS

    def bit(self):
        return order_of(self.part)[self.step]

    def rows(self):
        return self.unit * UNITS >> (self.step + 1)

    def sent(self, got, base):
        self.step += 1
        self.away = None
        self.terms.append((got, base, self.step))


def listed(streams):
    arrays, plans = [], []
    for stream in streams:
        terms = [(stream.away, 0, 0)] if stream.away is not None else stream.terms
        plan = []
        for array, base, step in terms:
            found = [n for n, x in enumerate(arrays) if x is array]
            if not found:
                found = [len(arrays)]
                arrays.append(array)
            plan.append((found[0], base, step))
        plans.append(plan)
    return arrays, plans


def plan_sum(refs, plan, part, chosen, unit):
    total = 0.0
    for n, base, step in plan:
        total = total + unit_rows(refs[n], bits_left(part, step), chosen, unit, base).astype(f32)
    return total


def step_kernel(n_arrays, n_small, plans, *refs):
    mine = my_bits()
    small, outs = refs[n_arrays : n_arrays + n_small], refs[n_arrays + n_small :]
    if n_small:
        outs[-1][...] = sum(ref[...] for ref in small)
    for part, step, made, unit, plan, out, base in plans:
        order = order_of(part)
        if made:
            ref = refs[plan[0][0]]
            outs[out][base : base + ref.shape[0], :] = ref[...]
            continue
        for j, chosen in every_choice(bits_left(part, step + 1)):
            for bit in order[:step]:
                chosen[bit] = mine[bit]
            chosen[order[step]] = 1 - mine[order[step]]
            to = base + j * unit
            outs[out][to : to + unit, :] = plan_sum(refs, plan, part, chosen, unit).astype(bf16)


def finish_kernel(n_arrays, n_small, plans, *refs):
    mine = my_bits()
    chosen = {bit: mine[bit] for bit in range(TOP_BITS)}
    small, refs_out = refs[n_arrays : n_arrays + n_small], refs[n_arrays + n_small :]
    fc2_ref, fc1_ref, qkv_ref, proj_ref, *outs = refs_out
    local = qkv_ref.shape[2]
    third = local // 3
    for i, (part, unit, plan) in enumerate(plans):
        total = plan_sum(refs, plan, part, chosen, unit)
        if i < 6:
            (fc2_ref, fc1_ref)[i // 3][:, part * UNIT_BLOCK : (part + 1) * UNIT_BLOCK] = total
        else:
            qkv_ref[part] = total[:, :local]
            proj_ref[:, part * third : (part + 1) * third] = total[:, local:]
        if i == 5:
            fc2_ref.leave()
            fc1_ref.leave()
    total = sum(ref[...] for ref in small)
    width = total.shape[1]
    for i, out_ref in enumerate(outs[:-1]):
        out_ref[...] = total[i : i + 1, :].reshape(width)
    for i in range(total.shape[0] - 7):
        outs[-1][i * width : (i + 1) * width] = total[7 + i : 8 + i, :].reshape(width)


def both_rows(own, other):
    return jnp.concatenate([own, other], axis=0)


def weight_tile(arranged_ref, right, away_ref, kept_ref, columns):
    half = away_ref.shape[0]
    away_ref[:, columns] = dot(arranged_ref[:half, :], right).astype(bf16)
    kept_ref[:, columns] = dot(arranged_ref[half:, :], right)


def mlp_weights_kernel(left_own_ref, left_par_ref, right_own_ref, right_par_ref, *outs):
    away_refs, kept_refs, (turned_ref, arranged_ref) = outs[:3], outs[3:6], outs[6:]
    mine = my_bits()
    turned_ref[...] = both_rows(left_own_ref[...], left_par_ref[...]).T
    columns = slice(0, UNIT_BLOCK)
    for part in range(3):
        at = slice(part * UNIT_BLOCK, (part + 1) * UNIT_BLOCK)
        right = both_rows(right_own_ref[:, at], right_par_ref[:, at])
        arrange_rows(turned_ref, mine, part, arranged_ref)
        weight_tile(arranged_ref, right, away_refs[part], kept_refs[part], columns)


def attn_weights_kernel(
    first_own_ref,
    first_par_ref,
    grad_attn_own_ref,
    grad_attn_par_ref,
    qkv_own_ref,
    qkv_par_ref,
    mixed_own_ref,
    mixed_par_ref,
    *outs,
):
    away_refs, kept_refs, (turned_ref, arranged_ref) = outs[:3], outs[3:6], outs[6:]
    mine = my_bits()
    local = mixed_own_ref.shape[1]
    third = local // 3
    turned_ref[...] = both_rows(first_own_ref[...], first_par_ref[...]).T
    for part in range(3):
        at = slice(part * local, (part + 1) * local)
        right = both_rows(qkv_own_ref[:, at], qkv_par_ref[:, at])
        arrange_rows(turned_ref, mine, part, arranged_ref)
        weight_tile(arranged_ref, right, away_refs[part], kept_refs[part], slice(0, local))
    turned_ref[...] = both_rows(grad_attn_own_ref[...], grad_attn_par_ref[...]).T
    for part in range(3):
        at = slice(part * third, (part + 1) * third)
        right = both_rows(mixed_own_ref[:, at], mixed_par_ref[:, at])
        arrange_rows(turned_ref, mine, part, arranged_ref)
        weight_tile(
            arranged_ref, right, away_refs[part], kept_refs[part], slice(local, local + third)
        )


def weights(kernel, arrays, width, depth, columns):
    half = width // 2
    return call(
        kernel,
        [shape((half, columns), bf16)] * 3 + [shape((half, columns), f32)] * 3,
        arrays,
        scratch=[pltpu.VMEM((width, depth), bf16), pltpu.VMEM((width, depth), bf16)],
    )


def heads_back(count_ref, grad_attn_ref, proj_ref, made_ref, out_ref, mixed_scratch):
    images = count_ref.shape[0]
    padded = made_ref.shape[0] // images
    local = proj_ref.shape[0]
    factor = HEAD_DIM ** (-0.5)
    mixed_scratch[...] = dot_turned(grad_attn_ref[...], proj_ref[...]).astype(bf16)
    for b in range(images):
        rows = slice(b * padded, (b + 1) * padded)
        for at in range(0, local, 2 * HEAD_DIM):
            q, k, v = (
                made_ref[rows, t * local + at : t * local + at + 2 * HEAD_DIM] for t in range(3)
            )
            q = stacked_heads(q)
            grad_mixed = stacked_heads(mixed_scratch[rows, at : at + 2 * HEAD_DIM])
            probs = pair_probs(q, k, count_ref[b])
            grad_probs = dot_turned(grad_mixed, v)
            row_dot = jnp.sum(probs * grad_probs, axis=-1, keepdims=True)
            grad_scores = (probs * (grad_probs - row_dot)).astype(bf16)
            found = (
                joined_heads(dot(grad_scores, k)) * factor,
                dot(grad_scores, q, ((0,), (0,))) * factor,
                dot(probs.astype(bf16), grad_mixed, ((0,), (0,))),
            )
            for t in range(3):
                to = slice(t * local + at, t * local + at + 2 * HEAD_DIM)
                out_ref[rows, to] = found[t].astype(bf16)


def back_kernel(
    count_ref,
    grad_pre_other_ref,
    w_fc1_other_ref,
    grad_pre_ref,
    w_fc1_ref,
    picked_ref,
    attention_ref,
    grad_picked_ref,
    router_ref,
    gain_ref,
    made_ref,
    proj_ref,
    grad_attn_ref,
    grad_hidden_ref,
    out_ref,
    sums_ref,
    mixed_scratch,
):
    images = count_ref.shape[0]
    padded = picked_ref.shape[0] // images
    grad_second = dot_turned(grad_pre_other_ref[...], w_fc1_other_ref[...])
    grad_second = grad_second + dot_turned(grad_pre_ref[...], w_fc1_ref[...])
    normed, inv_std = norm_stats(picked_ref[...].astype(f32) + attention_ref[...])
    grad_hidden = norm_back(grad_second, line(gain_ref), normed, inv_std)
    grad_hidden_ref[...] = grad_hidden
    scale = live_column(count_ref, images, padded) * router_ref[...]
    grad_attention = scale * grad_picked_ref[...].astype(f32) + grad_hidden
    grad_attn_ref[...] = grad_attention.astype(bf16)
    sums_ref[0:1, :] = column_sum(grad_attention)
    sums_ref[1:2, :] = column_sum(grad_second * normed)
    sums_ref[2:3, :] = column_sum(grad_second)
    heads_back(count_ref, grad_attn_ref, proj_ref, made_ref, out_ref, mixed_scratch)


def branch_kernel(
    count_ref,
    picked_ref,
    grad_picked_ref,
    router_ref,
    attention_ref,
    act_own_ref,
    act_other_ref,
    w_fc2_ref,
    w_fc2_other_ref,
    fc2_bias_ref,
    update_ref,
    grad_logit_ref,
    router_grad_ref,
):
    images = count_ref.shape[0]
    padded = picked_ref.shape[0] // images
    router = router_ref[...]
    scale = live_column(count_ref, images, padded) * router
    mlp_out = dot(act_own_ref[...], w_fc2_ref[...]) + dot(act_other_ref[...], w_fc2_other_ref[...])
    branch = attention_ref[...] + (mlp_out + line(fc2_bias_ref))
    update_ref[...] = scale * branch
    grad_logit = (
        scale
        * (1.0 - router)
        * jnp.sum(grad_picked_ref[...].astype(f32) * branch, axis=-1, keepdims=True)
    )
    grad_logit_ref[...] = grad_logit
    router_grad_ref[...] = column_sum(grad_logit * picked_ref[...].astype(f32))


def first_back_kernel(
    qkv_own_ref,
    gain_ref,
    router_w_ref,
    picked_ref,
    grad_hidden_ref,
    grad_logit_ref,
    grad_qkv_own_ref,
    grad_qkv_other_ref,
    qkv_other_ref,
    fc2_bias_grad_ref,
    router_grad_ref,
    back_sums_ref,
    unit_own_ref,
    unit_other_ref,
    grad_kept_ref,
    keep_ref,
    send_ref,
):
    width = picked_ref.shape[1]
    local = qkv_other_ref.shape[2]
    grad_first = jnp.zeros(picked_ref.shape, f32)
    for side in range(SIDES):
        for t in range(3):
            grad_first = grad_first + dot_turned(
                (grad_qkv_own_ref, grad_qkv_other_ref)[side][:, t * local : (t + 1) * local],
                (qkv_own_ref, qkv_other_ref)[side][t],
            )
    normed, inv_std = norm_stats(picked_ref[...].astype(f32))
    grad_kept_ref[...] = (
        norm_back(grad_first, line(gain_ref), normed, inv_std)
        + grad_hidden_ref[...]
        + grad_logit_ref[...] * line(router_w_ref)
    )
    sums = (
        column_sum(grad_first * normed),
        column_sum(grad_first),
        back_sums_ref[0:1, :],
        back_sums_ref[1:2, :],
        back_sums_ref[2:3, :],
        fc2_bias_grad_ref[...],
        router_grad_ref[...],
    )
    for i, values in enumerate(sums):
        keep_ref[i : i + 1, :] = values
        send_ref[i : i + 1, :] = values
    for i in range(unit_own_ref.shape[0] // width):
        at = slice(i * width, (i + 1) * width)
        keep_ref[7 + i : 8 + i, :] = unit_own_ref[at].reshape(1, width)
        send_ref[7 + i : 8 + i, :] = unit_other_ref[at].reshape(1, width)


def put_back_kernel(n_small, index_ref, base_ref, change_ref, *refs):
    small_refs, outs, padded_ref = refs[:n_small], refs[n_small:-1], refs[-1]
    out_ref = outs[0]
    if n_small:
        outs[1][...] = sum(ref[...] for ref in small_refs)
    images, slots, _ = base_ref.shape
    padded = change_ref.shape[0] // images
    fill_index(index_ref, padded_ref)
    for b in range(images):
        hot = turned_hot(index_ref, padded_ref, b, slots, padded)
        change = change_ref[b * padded : (b + 1) * padded, :]
        high = change.astype(bf16)
        low = (change - high.astype(f32)).astype(bf16)
        updated = base_ref[b].astype(f32) + (dot(hot, high) + dot(hot, low))
        out_ref[b] = updated.astype(bf16)


def other_core(value):
    return lax.ppermute(value, "head", [(0, 1), (1, 0)])


def partners(count, bit):
    return [(i, i ^ (1 << bit)) for i in range(count)]


def swap(value, bit, count):
    return lax.ppermute(value, "dp", partners(count, bit + count.bit_length() - 1 - TOP_BITS))


def begin(halves, count):
    streams = [Stream(part, None, halves[3 + part]) for part in range(3)]
    for part, stream in enumerate(streams):
        stream.sent(swap(halves[part], stream.bit(), count), 0)
    return streams


def exchange(streams, count, after, small=()):
    arrays, plans = listed(streams)
    tied, after = lax.optimization_barrier((tuple(arrays), after))
    bits = []
    for stream in streams:
        if stream.bit() not in bits:
            bits.append(stream.bit())
    sizes, full, bases = [0] * len(bits), [], []
    for stream, plan in zip(streams, plans):
        out = bits.index(stream.bit())
        made = stream.away is not None
        full.append((stream.part, stream.step, made, stream.unit, plan, out, sizes[out]))
        bases.append(sizes[out])
        sizes[out] += stream.rows()
    columns = arrays[0].shape[1]
    outs = [shape((size, columns), bf16) for size in sizes]
    outs += [shape(array.shape, array.dtype) for array in small[:1]]
    made = call(
        functools.partial(step_kernel, len(arrays), len(small), full), outs, (*tied, *small)
    )
    made, after = lax.optimization_barrier((made, after))
    got = [swap(made[n], bit, count) for n, bit in enumerate(bits)]
    for stream, base in zip(streams, bases):
        stream.sent(got[bits.index(stream.bit())], base)
    return (after, made[-1]) if small else after


def fewer_rows(grad, count, axis):
    place = lax.axis_index("dp")
    for bit in range(count.bit_length() - 2 - TOP_BITS, -1, -1):
        half = grad.shape[axis] // 2
        mine = (place >> bit) & 1
        away = lax.dynamic_slice_in_dim(grad, (1 - mine) * half, half, axis).astype(bf16)
        kept = lax.dynamic_slice_in_dim(grad, mine * half, half, axis)
        grad = kept + lax.ppermute(away, "dp", partners(count, bit)).astype(f32)
    return grad


def on_device(
    tokens,
    kept_index,
    kept_count,
    ln1_gain,
    ln1_bias,
    w_qkv,
    w_proj,
    proj_bias,
    ln2_gain,
    ln2_bias,
    w_fc1,
    fc1_bias,
    w_fc2,
    fc2_bias,
    w_router,
    cotangent,
):
    images, slots, width = tokens.shape
    padded = rows_of(kept_index.shape[1])
    rows = images * padded
    local = w_qkv.shape[2]
    units = w_fc1.shape[1]
    count = lax.axis_size("dp")

    top = count.bit_length() - 1 - TOP_BITS
    w_qkv_other = other_core(w_qkv)
    w_proj_other = other_core(w_proj)
    index_scratch = pltpu.VMEM((8, 128), jnp.int32)
    heads_scratch = pltpu.VMEM((rows, local), bf16)
    tie = lax.optimization_barrier
    picked, first, router, *near = call(
        front_kernel,
        [shape((rows, width), bf16), shape((rows, width), bf16), shape((rows, 1), f32)],
        (Far(kept_index), Far(tokens), Far(w_router), Far(ln1_gain), Far(ln1_bias)),
        scratch=[index_scratch],
        fetch=(w_qkv, w_proj, proj_bias, ln2_gain, ln2_bias, fc1_bias, fc2_bias, ln1_gain, w_router),
    )
    w_qkv, w_proj, proj_bias, ln2_gain, ln2_bias, bias_own, fc2_bias, ln1_gain, w_router = near
    w_fc1_late, w_fc2_late, bias_late, first, w_qkv_other, w_proj_other = tie(
        (w_fc1, w_fc2, fc1_bias, first, w_qkv_other, w_proj_other)
    )
    w_fc1_other = other_core(w_fc1_late)
    bias_other = other_core(bias_late)
    w_fc2_other = other_core(w_fc2_late)
    first_par = other_core(first)

    made, made_other, mixed, mixed_other, attention, second, w_fc1, w_fc2 = call(
        attention_kernel,
        [
            shape((rows, 3 * local), bf16),
            shape((rows, 3 * local), bf16),
            shape((rows, local), bf16),
            shape((rows, local), bf16),
            shape((rows, width), f32),
            shape((rows, width), bf16),
        ],
        (
            Far(kept_count),
            first,
            w_qkv,
            w_qkv_other,
            w_proj,
            w_proj_other,
            picked,
            proj_bias,
            ln2_gain,
            ln2_bias,
        ),
        fetch=(w_fc1, w_fc2),
    )
    second, first_par = tie((second, first_par))
    mixed_par = other_core(mixed_other)
    second_par = other_core(second)

    def hidden(w, bias):
        return call(
            hidden_kernel,
            [shape((rows, units), bf16), shape((rows, units), f32)],
            (second, w, bias),
        )

    def hidden_back(w, slope):
        return call(
            hidden_back_kernel,
            [shape((rows, units), bf16), shape((units,), f32)],
            (grad_mlp, w, slope),
        )

    def mlp_weights(left, left_par, right, right_par):
        return weights(
            mlp_weights_kernel, (left, left_par, right, right_par), width, 2 * rows, UNIT_BLOCK
        )

    act_other, slope_other = hidden(w_fc1_other, bias_other)
    act_par = other_core(act_other)
    router, act_other = tie((router, act_other))
    grad_picked, grad_mlp, fc2_bias_sum, cotangent = call(
        grad_front_kernel,
        [shape((rows, width), bf16), shape((rows, width), bf16), shape((1, width), f32)],
        (Far(kept_count), Far(kept_index), Far(cotangent), router),
        scratch=[index_scratch],
        fetch=(cotangent,),
    )
    grad_mlp_par = other_core(grad_mlp)
    second, grad_mlp, mixed_par, second_par = tie((second, grad_mlp, mixed_par, second_par))
    act, slope = hidden(w_fc1, bias_own)
    halves = mlp_weights(grad_mlp, grad_mlp_par, act, act_par)
    halves, slope_other = tie((halves, slope_other))
    mlp_sums = begin(halves, count)
    grad_pre_other, unit_other = hidden_back(w_fc2_other, slope_other)
    grad_pre_par = other_core(grad_pre_other)
    grad_pre, unit_own = hidden_back(w_fc2, slope)
    halves = mlp_weights(second, second_par, grad_pre, grad_pre_par)
    halves, grad_pre = tie((halves, grad_pre))
    mlp_sums += begin(halves, count)

    grad_attn, grad_hidden, grad_qkv_other, back_sums = call(
        back_kernel,
        [
            shape((rows, width), bf16),
            shape((rows, width), f32),
            shape((rows, 3 * local), bf16),
            shape((8, width), f32),
        ],
        (
            Far(kept_count),
            grad_pre_other,
            w_fc1_other,
            grad_pre,
            w_fc1,
            picked,
            attention,
            grad_picked,
            router,
            ln2_gain,
            made_other,
            w_proj_other,
        ),
        scratch=[heads_scratch],
    )
    grad_attn_par = other_core(grad_attn)
    grad_qkv_par = other_core(grad_qkv_other)
    grad_attn = exchange(mlp_sums, count, grad_attn)
    grad_attn, grad_attn_par, grad_qkv_par = tie((grad_attn, grad_attn_par, grad_qkv_par))
    (grad_qkv,) = call(
        heads_back,
        [shape((rows, 3 * local), bf16)],
        (Far(kept_count), grad_attn, w_proj, made),
        scratch=[heads_scratch],
    )
    halves = weights(
        attn_weights_kernel,
        (first, first_par, grad_attn, grad_attn_par, grad_qkv, grad_qkv_par, mixed, mixed_par),
        width,
        2 * rows,
        local + local // 3,
    )
    attn_sums = [Stream(part, halves[part], halves[3 + part]) for part in range(3)]
    act = exchange((*mlp_sums, *attn_sums), count, act)
    update, grad_logit, router_sum = call(
        branch_kernel,
        [shape((rows, width), f32), shape((rows, 1), f32), shape((1, width), f32)],
        (
            Far(kept_count),
            picked,
            grad_picked,
            router,
            attention,
            act,
            act_other,
            w_fc2,
            w_fc2_other,
            fc2_bias,
        ),
    )

    sum_rows = 7 + units // width
    grad_kept, keep, send = call(
        first_back_kernel,
        [
            shape((rows, width), f32),
            shape((sum_rows, width), f32),
            shape((sum_rows, width), f32),
        ],
        (
            w_qkv,
            ln1_gain,
            w_router,
            picked,
            grad_hidden,
            grad_logit,
            grad_qkv,
            grad_qkv_other,
            w_qkv_other,
            fc2_bias_sum,
            router_sum,
            back_sums,
            unit_own,
            unit_other,
        ),
    )

    def put_back(base, change, *small):
        return call(
            functools.partial(put_back_kernel, len(small)),
            [Far(shape(base.shape, bf16)), *[shape(x.shape, x.dtype) for x in small[:1]]],
            (Far(kept_index), base, change, *small),
            scratch=[index_scratch],
        )

    got = other_core(send)
    update, keep = tie((update, keep))
    output, small = put_back(tokens, update, keep, got)
    got = swap(small, 0, count)
    grad_kept, output = tie((grad_kept, output))
    grad_kept, small = exchange((*mlp_sums, *attn_sums), count, grad_kept, (small, got))
    got = swap(small, 1, count)
    (input_grad,) = put_back(cotangent, grad_kept)
    input_grad, small = exchange(attn_sums, count, input_grad, (small, got))
    got = swap(small, 2, count)
    input_grad, small = exchange(attn_sums, count, input_grad, (small, got))
    for low in range(top):
        small = small + lax.ppermute(small, "dp", partners(count, low))
    got = swap(small, 3, count)
    sums = (*mlp_sums, *attn_sums)
    arrays, plans = listed(sums)
    plans = [(stream.part, stream.unit, plan) for stream, plan in zip(sums, plans)]
    unit = width // UNITS
    fc2_turned, fc1_grad, qkv_grad, proj_turned, *sums = call(
        functools.partial(finish_kernel, len(arrays), 2, plans),
        [
            Far(shape((unit, units), f32)),
            Far(shape((unit, units), f32)),
            Far(shape((3, unit, local), f32)),
            Far(shape((unit, local), f32)),
            *[Far(shape((width,), f32))] * 7,
            Far(shape((units,), f32)),
        ],
        (*arrays, small, got),
    )
    fc2_turned, fc1_grad, proj_turned = (
        fewer_rows(grad, count, 0) for grad in (fc2_turned, fc1_grad, proj_turned)
    )
    qkv_grad = fewer_rows(qkv_grad, count, 1)
    return (
        output,
        input_grad,
        sums[0],
        sums[1],
        qkv_grad,
        proj_turned.T,
        sums[2],
        sums[3],
        sums[4],
        fc1_grad,
        sums[7],
        fc2_turned.T,
        sums[5],
        sums[6],
    )


def solution(mesh):
    batch = ("dp", "head")
    return jax.shard_map(
        on_device,
        mesh=mesh,
        in_specs=(
            P(batch, None, None),
            P(batch, None),
            P(batch),
            P(),
            P(),
            P(None, None, "head"),
            P("head", None),
            P(),
            P(),
            P(),
            P(None, "head"),
            P("head"),
            P("head", None),
            P(),
            P(),
            P(batch, None, None),
        ),
        out_specs=(
            P(batch, None, None),
            P(batch, None, None),
            P(),
            P(),
            P(None, "dp", "head"),
            P("head", "dp"),
            P(),
            P(),
            P(),
            P("dp", "head"),
            P("head"),
            P("head", "dp"),
            P(),
            P(),
        ),
        check_vma=False,
    )
```

time: 133 us -> 107 us (0.80)
  waiting for transfers between devices: 46.2 us -> 25 us
  Pallas kernels: 54.9 us -> 48.5 us
  starting transfers between devices: 30.2 us -> 32.2 us
    ppermute x24, waiting for transfers between devices: 40 us -> 18 us  [swap(): lax.ppermute(value, 'dp', partners(count, bit + count.bit_length() - 1 -...]
    pallas_call x18 -> x22, Pallas kernels: 54.9 us -> 48.5 us  [call(): pl.pallas_call(body, out_shape=[(pltpu.HBM if i in far_out else pltpu.VME...]
    ppermute x13 -> x14, starting transfers between devices: 3.06 us -> 3.83 us  [other_core(): return lax.ppermute(value, 'head', [(0, 1), (1, 0)])]
    ppermute x13 -> x14, waiting for transfers between devices: 6.17 us -> 6.93 us  [other_core(): return lax.ppermute(value, 'head', [(0, 1), (1, 0)])]
  transfers between devices with their start and end apart: 37 -> 38, of which waited for: 14 -> 13; matrix products, arithmetic and copies ran while one was open for 0% -> 0% of each run, Pallas kernels for 33% -> 43%
where the time goes in v1:
time: 107 us
  Pallas kernels  48.5 us (45%)
  starting transfers between devices  32.2 us (30%)
  waiting for transfers between devices  25 us (23%)
  between operations  1.14 us (1%)
    pallas_call x22, Pallas kernels, call(): pl.pallas_call(body, out_shape=[(pltpu.HBM if i in far_out else pltpu.VME...  48.5 us
    ppermute x24, starting transfers between devices, swap(): lax.ppermute(value, 'dp', partners(count, bit + count.bit_length() - 1 -...  28.4 us
    ppermute x24, waiting for transfers between devices, swap(): lax.ppermute(value, 'dp', partners(count, bit + count.bit_length() - 1 -...  18 us
    ppermute x14, waiting for transfers between devices, other_core(): return lax.ppermute(value, 'head', [(0, 1), (1, 0)])  6.93 us
    ppermute x14, starting transfers between devices, other_core(): return lax.ppermute(value, 'head', [(0, 1), (1, 0)])  3.83 us
  transfers between devices with their start and end apart: 38, of which 13 were waited for; matrix products, arithmetic and copies ran while one was open for 0% of the time, Pallas kernels for 43%

profile of v1, /device:TPU:0, one launch (start us, length us, event | category | flops | bytes accessed | tf_op | source)
XLA Modules:
  0.0 106.8 jit_solution(4441104941688764373)
XLA Ops:
  1.3 2.3 %shard_map.263 = (bf16[336,768]{1,0:T(8,128)(2,1)S(1)}, bf16[336,768]{1,0:T(8,128)(2,1)S(1)}, f32[336,1]{1,0:T(8,128)S(1)}, bf16[3,768,384]{2,1,0:T(8,128)(2,1)S...) custom-call(s32[3,98]{1,0:T(4,128)} %refs_0_.15, ...), custom_call_target="tpu_custom_call" | custom-call | flops 1 | bytes 1 | tf_op jit(solution)/shard_map/pallas_call | solution.py:144
  3.6 2.0 %collective-permute-done.1.refs_5_.refs_11_ = bf16[384,768]{1,0:T(8,128)(2,1)S(1)} collective-permute-done((bf16[384,768]{1,0:T(8,128)(2,1)}, bf16[384,768]{1,0:T(8,128)(2,1)S(1)}, u32[]{:S(2)}, u32[]{:S(2)}) %collective-permute-start.1) | collective-permute-done | bytes 589856 | tf_op jit(solution)/shard_map/ppermute | solution.py:665
  6.6 5.1 %shard_map.264 = (bf16[336,1152]{1,0:T(8,128)(2,1)S(1)}, bf16[336,1152]{1,0:T(8,128)(2,1)S(1)}, bf16[336,384]{1,0:T(8,128)(2,1)S(1)}, bf16[336,384]{1,0:T(8,128)...) custom-call(s32[3]{0:T(128)} %refs_0_.13, ...), custom_call_target="tpu_custom_call" | custom-call | flops 1 | bytes 1 | tf_op jit(solution)/shard_map/pallas_call | solution.py:144
  11.7 1.9 %collective-permute-done.2.refs_1_ = bf16[336,768]{1,0:T(8,128)(2,1)S(1)} collective-permute-done((bf16[336,768]{1,0:T(8,128)(2,1)S(1)}, bf16[336,768]{1,0:T(8,128)(2,1)S(1)}, u32[]{:S(2)}, u32[]{:S(2)}) %collective-permute-start.2) | collective-permute-done | bytes 516128 | tf_op jit(solution)/shard_map/ppermute | solution.py:665
  15.7 1.8 %shard_map.266 = (bf16[336,768]{1,0:T(8,128)(2,1)S(1)}, bf16[336,768]{1,0:T(8,128)(2,1)S(1)}, f32[1,768]{1,0:T(1,128)S(1)}, bf16[3,197,768]{2,1,0:T(8,128)(2,1)S(1)}) custom-call(s32[3]{0:T(128)} %refs_0_.13, s32[3,98]{1,0:T(4,128)} %refs_0_.15, bf16[3,197,768]{2,1,0:T(8,128)(2,1)} %refs_4_.3, f32[336,1]{1,0:T(8,128)S(1)} %get-tuple-element.257.refs_3_.refs_8_, ...), custom_call_target="tpu_custom_call" | custom-call | flops 1 | bytes 1 | tf_op jit(solution)/shard_map/pallas_call | solution.py:144
  18.1 1.8 %collective-permute-done.5.refs_7_ = bf16[336,384]{1,0:T(8,128)(2,1)S(1)} collective-permute-done((bf16[336,384]{1,0:T(8,128)(2,1)S(1)}, bf16[336,384]{1,0:T(8,128)(2,1)S(1)}, u32[]{:S(2)}, u32[]{:S(2)}) %collective-permute-start.5) | collective-permute-done | bytes 258080 | tf_op jit(solution)/shard_map/ppermute | solution.py:665
  21.4 2.5 %shard_map.268 = (bf16[384,512]{1,0:T(8,128)(2,1)S(1)}, bf16[384,512]{1,0:T(8,128)(2,1)S(1)}, bf16[384,512]{1,0:T(8,128)(2,1)S(1)}, f32[384,512]{1,0:T(8,128)S(1...) custom-call(bf16[336,768]{1,0:T(8,128)(2,1)S(1)} %get-tuple-element.260.refs_0_, ...), custom_call_target="tpu_custom_call" | custom-call | flops 1 | bytes 1 | tf_op jit(solution)/shard_map/pallas_call | solution.py:144
  25.4 2.6 %collective-permute-start.11 = (bf16[384,512]{1,0:T(8,128)(2,1)S(1)}, bf16[384,512]{1,0:T(8,128)(2,1)S(1)}, u32[]{:S(2)}, u32[]{:S(2)}) collective-permute-start(bf16[384,512]{1,0:T(8,128)(2,1)S(1)} %get-tuple-element.291), channel_id=1, source_target_pairs={{0,2},{2,0},{4,6},{6,4},{8,10},{10,8},{12,14},{14,12},{16,18},{18,... | collective-permute-start | bytes 1179656 | tf_op jit(solution)/shard_map/ppermute | solution.py:673
  32.3 2.5 %shard_map.271 = (bf16[384,512]{1,0:T(8,128)(2,1)S(1)}, bf16[384,512]{1,0:T(8,128)(2,1)S(1)}, bf16[384,512]{1,0:T(8,128)(2,1)S(1)}, f32[384,512]{1,0:T(8,128)S(1...) custom-call(bf16[336,768]{1,0:T(8,128)(2,1)S(1)} %get-tuple-element.262.refs_0_, ...), custom_call_target="tpu_custom_call" | custom-call | flops 1 | bytes 1 | tf_op jit(solution)/shard_map/pallas_call | solution.py:144
  35.9 2.1 %collective-permute-done.11.refs_1_ = bf16[384,512]{1,0:T(8,128)(2,1)S(1)} collective-permute-done((bf16[384,512]{1,0:T(8,128)(2,1)S(1)}, bf16[384,512]{1,0:T(8,128)(2,1)S(1)}, u32[]{:S(2)}, u32[]{:S(2)}) %collective-permute-start.11) | collective-permute-done | bytes 393248 | tf_op jit(solution)/shard_map/ppermute | solution.py:673
  38.0 2.1 %collective-permute-start.16 = (bf16[384,512]{1,0:T(8,128)(2,1)S(1)}, bf16[384,512]{1,0:T(8,128)(2,1)S(1)}, u32[]{:S(2)}, u32[]{:S(2)}) collective-permute-start(bf16[384,512]{1,0:T(8,128)(2,1)S(1)} %get-tuple-element.301), channel_id=1, source_target_pairs={{0,8},{2,10},{4,12},{6,14},{8,0},{10,2},{12,4},{14,6},{16,24},{18,... | collective-permute-start | bytes 1179656 | tf_op jit(solution)/shard_map/ppermute | solution.py:673
  40.0 8.4 %shard_map.272 = (bf16[336,768]{1,0:T(8,128)(2,1)S(1)}, f32[336,768]{1,0:T(8,128)S(1)}, bf16[336,1152]{1,0:T(8,128)(2,1)S(1)}, f32[8,768]{1,0:T(8,128)S(1)}) custom-call(s32[3]{0:T(128)} %refs_0_.13, bf16[336,1536]{1,0:T(8,128)(2,1)S(1)} %get-tuple-element.274.refs_1_, bf16[768,1536]{1,0:T(8,128)(2,1)S(1)} %collective-permute-done.3.refs_1_.refs_2_, ...), custom_call_target="tpu_custom_call" | custom-call | flops 1 | bytes 1 | tf_op jit(solution)/shard_map/pallas_call | solution.py:144
  53.3 5.1 %shard_map.274.refs_4_.refs_6_ = bf16[336,1152]{1,0:T(8,128)(2,1)S(1)} custom-call(s32[3]{0:T(128)} %refs_0_.13, bf16[336,768]{1,0:T(8,128)(2,1)S(1)} %get-tuple-element.325.refs_1_.refs_2_, bf16[384,768]{1,0:T(8,128)(2,1)S(1)} %get-tuple-element.246.refs_4_.refs_2_, bf16[336,1152]{1,0:T(8,128)(2,1)S(1)} %get-tuple-element.327.refs_3_), custom_call_target="tpu_custom_call" | custom-call | flops 1 | bytes 1 | tf_op jit(solution)/shard_map/pallas_call | solution.py:144
  58.4 3.9 %shard_map.275 = (bf16[384,512]{1,0:T(8,128)(2,1)S(1)}, bf16[384,512]{1,0:T(8,128)(2,1)S(1)}, bf16[384,512]{1,0:T(8,128)(2,1)S(1)}, f32[384,512]{1,0:T(8,128)S(1...) custom-call(bf16[336,768]{1,0:T(8,128)(2,1)S(1)} %get-tuple-element.244.refs_1_.refs_0_, ...), custom_call_target="tpu_custom_call" | custom-call | flops 1 | bytes 1 | tf_op jit(solution)/shard_map/pallas_call | solution.py:144
  65.8 2.7 %shard_map.277 = (f32[336,768]{1,0:T(8,128)S(1)}, f32[336,1]{1,0:T(8,128)S(1)}, f32[1,768]{1,0:T(1,128)S(1)}) custom-call(s32[3]{0:T(128)} %refs_0_.13, bf16[336,768]{1,0:T(8,128)(2,1)S(1)} %get-tuple-element.242.refs_6_.refs_5_.refs_1_.refs_3_, bf16[336,768]{1,0:T(8,128)(2,1)S(1)} %get-tuple-element.287.refs_7_.refs_2_, ...), custom_call_target="tpu_custom_call" | custom-call | flops 1 | bytes 1 | tf_op jit(solution)/shard_map/pallas_call | solution.py:144
  68.5 2.4 %shard_map.278 = (f32[336,768]{1,0:T(8,128)S(1)}, f32[9,768]{1,0:T(8,128)S(1)}, f32[9,768]{1,0:T(8,128)S(1)}) custom-call(bf16[3,768,384]{2,1,0:T(8,128)(2,1)S(1)} %get-tuple-element.239.refs_2_.refs_0_, f32[768]{0:T(1024)S(1)} %get-tuple-element.240.refs_1_, f32[768]{0:T(1024)S(1)} %get-tuple-element.241.refs_2_, ...), custom_call_target="tpu_custom_call" | custom-call | flops 1 | bytes 1 | tf_op jit(solution)/shard_map/pallas_call | solution.py:144
  72.2 2.3 %shard_map.279 = (bf16[3,197,768]{2,1,0:T(8,128)(2,1)}, f32[9,768]{1,0:T(8,128)S(1)}) custom-call(s32[3,98]{1,0:T(4,128)} %refs_0_.15, bf16[3,197,768]{2,1,0:T(8,128)(2,1)S(1)} %copy-done, f32[336,768]{1,0:T(8,128)S(1)} %get-tuple-element.368.refs_2_, f32[9,768]{1,0:T(8,128)S(1)} %get-tuple-element.369.refs_3_, f32[9,768]{1,0:T(8,128)S(1)} %collective-permute-done.22.refs_4_), custom_call_target="tpu_custom_call" | custom-call | flops 1 | bytes 1 | tf_op jit(solution)/shard_map/pallas_call | solution.py:144
  82.0 2.5 %collective-permute-start.35 = (bf16[288,512]{1,0:T(8,128)(2,1)S(1)}, bf16[288,512]{1,0:T(8,128)(2,1)S(1)}, u32[]{:S(2)}, u32[]{:S(2)}) collective-permute-start(bf16[288,512]{1,0:T(8,128)(2,1)S(1)} %get-tuple-element.449), channel_id=1, source_target_pairs={{0,16},{2,18},{4,20},{6,22},{8,24},{10,26},{12,28},{14,30},{16,0},... | collective-permute-start | bytes 884744 | tf_op jit(solution)/shard_map/ppermute | solution.py:673
  85.1 2.3 %shard_map.281 = bf16[3,197,768]{2,1,0:T(8,128)(2,1)} custom-call(s32[3,98]{1,0:T(4,128)} %refs_0_.15, bf16[3,197,768]{2,1,0:T(8,128)(2,1)S(1)} %get-tuple-element.411.refs_1_, f32[336,768]{1,0:T(8,128)S(1)} %get-tuple-element.412.refs_2_), custom_call_target="tpu_custom_call" | custom-call | flops 1 | bytes 1 | tf_op jit(solution)/shard_map/pallas_call | solution.py:144
  87.4 3.6 %collective-permute-done.28.refs_5_.refs_6_.refs_24_ = bf16[192,512]{1,0:T(8,128)(2,1)S(1)} collective-permute-done((bf16[192,512]{1,0:T(8,128)(2,1)S(1)}, bf16[192,512]{1,0:T(8,128)(2,1)S(1)}, u32[]{:S(2)}, u32[]{:S(2)}) %collective-permute-start.28) | collective-permute-done | bytes 196640 | tf_op jit(solution)/shard_map/ppermute | solution.py:673
  91.9 1.8 %collective-permute-start.34 = (f32[9,768]{1,0:T(8,128)S(1)}, f32[9,768]{1,0:T(8,128)S(1)}, u32[]{:S(2)}, u32[]{:S(2)}) collective-permute-start(f32[9,768]{1,0:T(8,128)S(1)} %get-tuple-element.444.refs_12_), channel_id=1, source_target_pairs={{0,8},{2,10},{4,12},{6,14},{8,0},{10,2},{12,4},{14,6},{16,24},{18,... | collective-permute-start | bytes 82952 | tf_op jit(solution)/shard_map/ppermute | solution.py:673
  93.6 2.6 %collective-permute-done.31.refs_3_.refs_21_ = bf16[96,512]{1,0:T(8,128)(2,1)S(1)} collective-permute-done((bf16[96,512]{1,0:T(8,128)(2,1)S(1)}, bf16[96,512]{1,0:T(8,128)(2,1)S(1)}, u32[]{:S(2)}, u32[]{:S(2)}) %collective-permute-start.31) | collective-permute-done | bytes 98336 | tf_op jit(solution)/shard_map/ppermute | solution.py:673
  97.3 2.3 %collective-permute-start.36 = (bf16[144,512]{1,0:T(8,128)(2,1)S(1)}, bf16[144,512]{1,0:T(8,128)(2,1)S(1)}, u32[]{:S(2)}, u32[]{:S(2)}) collective-permute-start(bf16[144,512]{1,0:T(8,128)(2,1)S(1)} %get-tuple-element.450), channel_id=1, source_target_pairs={{0,16},{2,18},{4,20},{6,22},{8,24},{10,26},{12,28},{14,30},{16,0},... | collective-permute-start | bytes 442376 | tf_op jit(solution)/shard_map/ppermute | solution.py:673
  100.3 5.2 %collective-permute-done.37.refs_30_ = f32[9,768]{1,0:T(8,128)S(1)} collective-permute-done((f32[9,768]{1,0:T(8,128)S(1)}, f32[9,768]{1,0:T(8,128)S(1)}, u32[]{:S(2)}, u32[]{:S(2)}) %collective-permute-start.37) | collective-permute-done | bytes 27680 | tf_op jit(solution)/shard_map/ppermute | solution.py:673
  (80 shorter events, 34.1 us)
Async XLA Ops:
  5.6 8.0 %collective-permute-start.3 = (bf16[768,1536]{1,0:T(8,128)(2,1)S(1)}, bf16[768,1536]{1,0:T(8,128)(2,1)S(1)}, u32[]{:S(2)}, u32[]{:S(2)}) collective-permute-start(bf16[768,1536]{1,0:T(8,128)(2,1)S(1)} %copy-done.1), channel_id=1, source_target_pairs={{0,1},{1,0},{2,3},{3,2},{4,5},{5,4},{6,7},{7,6},{8,9},{9,8},{10,11... | collective-permute-start | bytes 7077896 | tf_op jit(solution)/shard_map/ppermute | solution.py:665
  5.9 18.0 %collective-permute-start.7 = (bf16[1536,768]{1,0:T(8,128)(2,1)}, bf16[1536,768]{1,0:T(8,128)(2,1)S(1)}, u32[]{:S(2)}, u32[]{:S(2)}) collective-permute-start(bf16[1536,768]{1,0:T(8,128)(2,1)} %refs_11_.3), channel_id=1, source_target_pairs={{0,1},{1,0},{2,3},{3,2},{4,5},{5,4},{6,7},{7,6},{8,9},{9,8},{10,11... | collective-permute-start | bytes 7077896 | tf_op jit(solution)/shard_map/ppermute | solution.py:665
  6.1 7.5 %collective-permute-start.2 = (bf16[336,768]{1,0:T(8,128)(2,1)S(1)}, bf16[336,768]{1,0:T(8,128)(2,1)S(1)}, u32[]{:S(2)}, u32[]{:S(2)}) collective-permute-start(bf16[336,768]{1,0:T(8,128)(2,1)S(1)} %get-tuple-element.244.refs_1_.refs_0_), channel_id=1, source_target_pairs={{0,1},{1,0},{2,3},{3,2},{4,5},{5,4},{6,7},{7,6},{8,9},{9,8},{10,11... | collective-permute-start | bytes 1548296 | tf_op jit(solution)/shard_map/ppermute | solution.py:665
  6.5 7.2 %collective-permute-start.4 = (f32[1536]{0:T(1024)S(1)}, f32[1536]{0:T(1024)S(1)}, u32[]{:S(2)}, u32[]{:S(2)}) collective-permute-start(f32[1536]{0:T(1024)S(1)} %copy-done.2), channel_id=1, source_target_pairs={{0,1},{1,0},{2,3},{3,2},{4,5},{5,4},{6,7},{7,6},{8,9},{9,8},{10,11... | collective-permute-start | bytes 18440 | tf_op jit(solution)/shard_map/ppermute | solution.py:665
  15.2 6.3 %collective-permute-start.9 = (bf16[336,1536]{1,0:T(8,128)(2,1)S(1)}, bf16[336,1536]{1,0:T(8,128)(2,1)S(1)}, u32[]{:S(2)}, u32[]{:S(2)}) collective-permute-start(bf16[336,1536]{1,0:T(8,128)(2,1)S(1)} %get-tuple-element.357.refs_6_), channel_id=1, source_target_pairs={{0,1},{1,0},{2,3},{3,2},{4,5},{5,4},{6,7},{7,6},{8,9},{9,8},{10,11... | collective-permute-start | bytes 3096584 | tf_op jit(solution)/shard_map/ppermute | solution.py:665
  25.0 7.4 %collective-permute-start.10 = (bf16[336,1536]{1,0:T(8,128)(2,1)S(1)}, bf16[336,1536]{1,0:T(8,128)(2,1)S(1)}, u32[]{:S(2)}, u32[]{:S(2)}) collective-permute-start(bf16[336,1536]{1,0:T(8,128)(2,1)S(1)} %get-tuple-element.274.refs_1_), channel_id=1, source_target_pairs={{0,1},{1,0},{2,3},{3,2},{4,5},{5,4},{6,7},{7,6},{8,9},{9,8},{10,11... | collective-permute-start | bytes 3096584 | tf_op jit(solution)/shard_map/ppermute | solution.py:665
  25.4 12.6 %collective-permute-start.11 = (bf16[384,512]{1,0:T(8,128)(2,1)S(1)}, bf16[384,512]{1,0:T(8,128)(2,1)S(1)}, u32[]{:S(2)}, u32[]{:S(2)}) collective-permute-start(bf16[384,512]{1,0:T(8,128)(2,1)S(1)} %get-tuple-element.291), channel_id=1, source_target_pairs={{0,2},{2,0},{4,6},{6,4},{8,10},{10,8},{12,14},{14,12},{16,18},{18,... | collective-permute-start | bytes 1179656 | tf_op jit(solution)/shard_map/ppermute | solution.py:673
  28.0 20.5 %collective-permute-start.12 = (bf16[384,512]{1,0:T(8,128)(2,1)S(1)}, bf16[384,512]{1,0:T(8,128)(2,1)S(1)}, u32[]{:S(2)}, u32[]{:S(2)}) collective-permute-start(bf16[384,512]{1,0:T(8,128)(2,1)S(1)} %get-tuple-element.293), channel_id=1, source_target_pairs={{0,4},{2,6},{4,0},{6,2},{8,12},{10,14},{12,8},{14,10},{16,20},{18,... | collective-permute-start | bytes 1179656 | tf_op jit(solution)/shard_map/ppermute | solution.py:673
  29.5 19.0 %collective-permute-start.13 = (bf16[384,512]{1,0:T(8,128)(2,1)S(1)}, bf16[384,512]{1,0:T(8,128)(2,1)S(1)}, u32[]{:S(2)}, u32[]{:S(2)}) collective-permute-start(bf16[384,512]{1,0:T(8,128)(2,1)S(1)} %get-tuple-element.295), channel_id=1, source_target_pairs={{0,8},{2,10},{4,12},{6,14},{8,0},{10,2},{12,4},{14,6},{16,24},{18,... | collective-permute-start | bytes 1179656 | tf_op jit(solution)/shard_map/ppermute | solution.py:673
  34.8 14.3 %collective-permute-start.14 = (bf16[384,512]{1,0:T(8,128)(2,1)S(1)}, bf16[384,512]{1,0:T(8,128)(2,1)S(1)}, u32[]{:S(2)}, u32[]{:S(2)}) collective-permute-start(bf16[384,512]{1,0:T(8,128)(2,1)S(1)} %get-tuple-element.297), channel_id=1, source_target_pairs={{0,2},{2,0},{4,6},{6,4},{8,10},{10,8},{12,14},{14,12},{16,18},{18,... | collective-permute-start | bytes 1179656 | tf_op jit(solution)/shard_map/ppermute | solution.py:673
  35.4 13.7 %collective-permute-start.15 = (bf16[384,512]{1,0:T(8,128)(2,1)S(1)}, bf16[384,512]{1,0:T(8,128)(2,1)S(1)}, u32[]{:S(2)}, u32[]{:S(2)}) collective-permute-start(bf16[384,512]{1,0:T(8,128)(2,1)S(1)} %get-tuple-element.299), channel_id=1, source_target_pairs={{0,4},{2,6},{4,0},{6,2},{8,12},{10,14},{12,8},{14,10},{16,20},{18,... | collective-permute-start | bytes 1179656 | tf_op jit(solution)/shard_map/ppermute | solution.py:673
  38.0 11.1 %collective-permute-start.16 = (bf16[384,512]{1,0:T(8,128)(2,1)S(1)}, bf16[384,512]{1,0:T(8,128)(2,1)S(1)}, u32[]{:S(2)}, u32[]{:S(2)}) collective-permute-start(bf16[384,512]{1,0:T(8,128)(2,1)S(1)} %get-tuple-element.301), channel_id=1, source_target_pairs={{0,8},{2,10},{4,12},{6,14},{8,0},{10,2},{12,4},{14,6},{16,24},{18,... | collective-permute-start | bytes 1179656 | tf_op jit(solution)/shard_map/ppermute | solution.py:673
  49.3 13.1 %collective-permute-start.17 = (bf16[384,512]{1,0:T(8,128)(2,1)S(1)}, bf16[384,512]{1,0:T(8,128)(2,1)S(1)}, u32[]{:S(2)}, u32[]{:S(2)}) collective-permute-start(bf16[384,512]{1,0:T(8,128)(2,1)S(1)} %get-tuple-element.319), channel_id=1, source_target_pairs={{0,4},{2,6},{4,0},{6,2},{8,12},{10,14},{12,8},{14,10},{16,20},{18,... | collective-permute-start | bytes 1179656 | tf_op jit(solution)/shard_map/ppermute | solution.py:673
  50.9 11.5 %collective-permute-start.18 = (bf16[384,512]{1,0:T(8,128)(2,1)S(1)}, bf16[384,512]{1,0:T(8,128)(2,1)S(1)}, u32[]{:S(2)}, u32[]{:S(2)}) collective-permute-start(bf16[384,512]{1,0:T(8,128)(2,1)S(1)} %get-tuple-element.320), channel_id=1, source_target_pairs={{0,8},{2,10},{4,12},{6,14},{8,0},{10,2},{12,4},{14,6},{16,24},{18,... | collective-permute-start | bytes 1179656 | tf_op jit(solution)/shard_map/ppermute | solution.py:673
  51.8 10.6 %collective-permute-start.19 = (bf16[384,512]{1,0:T(8,128)(2,1)S(1)}, bf16[384,512]{1,0:T(8,128)(2,1)S(1)}, u32[]{:S(2)}, u32[]{:S(2)}) collective-permute-start(bf16[384,512]{1,0:T(8,128)(2,1)S(1)} %get-tuple-element.321), channel_id=1, source_target_pairs={{0,2},{2,0},{4,6},{6,4},{8,10},{10,8},{12,14},{14,12},{16,18},{18,... | collective-permute-start | bytes 1179656 | tf_op jit(solution)/shard_map/ppermute | solution.py:673
  62.7 14.0 %collective-permute-start.23 = (bf16[576,512]{1,0:T(8,128)(2,1)S(1)}, bf16[576,512]{1,0:T(8,128)(2,1)S(1)}, u32[]{:S(2)}, u32[]{:S(2)}) collective-permute-start(bf16[576,512]{1,0:T(8,128)(2,1)S(1)} %get-tuple-element.374), channel_id=1, source_target_pairs={{0,2},{2,0},{4,6},{6,4},{8,10},{10,8},{12,14},{14,12},{16,18},{18,... | collective-permute-start | bytes 1769480 | tf_op jit(solution)/shard_map/ppermute | solution.py:673
  63.7 13.9 %collective-permute-start.24 = (bf16[576,512]{1,0:T(8,128)(2,1)S(1)}, bf16[576,512]{1,0:T(8,128)(2,1)S(1)}, u32[]{:S(2)}, u32[]{:S(2)}) collective-permute-start(bf16[576,512]{1,0:T(8,128)(2,1)S(1)} %get-tuple-element.375), channel_id=1, source_target_pairs={{0,8},{2,10},{4,12},{6,14},{8,0},{10,2},{12,4},{14,6},{16,24},{18,... | collective-permute-start | bytes 1769480 | tf_op jit(solution)/shard_map/ppermute | solution.py:673
  65.2 13.3 %collective-permute-start.25 = (bf16[576,512]{1,0:T(8,128)(2,1)S(1)}, bf16[576,512]{1,0:T(8,128)(2,1)S(1)}, u32[]{:S(2)}, u32[]{:S(2)}) collective-permute-start(bf16[576,512]{1,0:T(8,128)(2,1)S(1)} %get-tuple-element.376), channel_id=1, source_target_pairs={{0,4},{2,6},{4,0},{6,2},{8,12},{10,14},{12,8},{14,10},{16,20},{18,... | collective-permute-start | bytes 1769480 | tf_op jit(solution)/shard_map/ppermute | solution.py:673
  78.9 8.5 %collective-permute-start.27 = (bf16[192,512]{1,0:T(8,128)(2,1)S(1)}, bf16[192,512]{1,0:T(8,128)(2,1)S(1)}, u32[]{:S(2)}, u32[]{:S(2)}) collective-permute-start(bf16[192,512]{1,0:T(8,128)(2,1)S(1)} %get-tuple-element.408), channel_id=1, source_target_pairs={{0,4},{2,6},{4,0},{6,2},{8,12},{10,14},{12,8},{14,10},{16,20},{18,... | collective-permute-start | bytes 589832 | tf_op jit(solution)/shard_map/ppermute | solution.py:673
  80.4 10.5 %collective-permute-start.28 = (bf16[192,512]{1,0:T(8,128)(2,1)S(1)}, bf16[192,512]{1,0:T(8,128)(2,1)S(1)}, u32[]{:S(2)}, u32[]{:S(2)}) collective-permute-start(bf16[192,512]{1,0:T(8,128)(2,1)S(1)} %get-tuple-element.409), channel_id=1, source_target_pairs={{0,8},{2,10},{4,12},{6,14},{8,0},{10,2},{12,4},{14,6},{16,24},{18,... | collective-permute-start | bytes 589832 | tf_op jit(solution)/shard_map/ppermute | solution.py:673
  81.1 9.9 %collective-permute-start.29 = (bf16[192,512]{1,0:T(8,128)(2,1)S(1)}, bf16[192,512]{1,0:T(8,128)(2,1)S(1)}, u32[]{:S(2)}, u32[]{:S(2)}) collective-permute-start(bf16[192,512]{1,0:T(8,128)(2,1)S(1)} %get-tuple-element.410), channel_id=1, source_target_pairs={{0,2},{2,0},{4,6},{6,4},{8,10},{10,8},{12,14},{14,12},{16,18},{18,... | collective-permute-start | bytes 589832 | tf_op jit(solution)/shard_map/ppermute | solution.py:673
  82.0 18.3 %collective-permute-start.35 = (bf16[288,512]{1,0:T(8,128)(2,1)S(1)}, bf16[288,512]{1,0:T(8,128)(2,1)S(1)}, u32[]{:S(2)}, u32[]{:S(2)}) collective-permute-start(bf16[288,512]{1,0:T(8,128)(2,1)S(1)} %get-tuple-element.449), channel_id=1, source_target_pairs={{0,16},{2,18},{4,20},{6,22},{8,24},{10,26},{12,28},{14,30},{16,0},... | collective-permute-start | bytes 884744 | tf_op jit(solution)/shard_map/ppermute | solution.py:673
  84.5 6.4 %collective-permute-start.30 = (f32[9,768]{1,0:T(8,128)S(1)}, f32[9,768]{1,0:T(8,128)S(1)}, u32[]{:S(2)}, u32[]{:S(2)}) collective-permute-start(f32[9,768]{1,0:T(8,128)S(1)} %get-tuple-element.422.refs_9_), channel_id=1, source_target_pairs={{0,4},{2,6},{4,0},{6,2},{8,12},{10,14},{12,8},{14,10},{16,20},{18,... | collective-permute-start | bytes 82952 | tf_op jit(solution)/shard_map/ppermute | solution.py:673
  97.3 8.2 %collective-permute-start.36 = (bf16[144,512]{1,0:T(8,128)(2,1)S(1)}, bf16[144,512]{1,0:T(8,128)(2,1)S(1)}, u32[]{:S(2)}, u32[]{:S(2)}) collective-permute-start(bf16[144,512]{1,0:T(8,128)(2,1)S(1)} %get-tuple-element.450), channel_id=1, source_target_pairs={{0,16},{2,18},{4,20},{6,22},{8,24},{10,26},{12,28},{14,30},{16,0},... | collective-permute-start | bytes 442376 | tf_op jit(solution)/shard_map/ppermute | solution.py:673
  (17 other events, 74.9 us)

commit v2 on v1

--- a/solution.py
+++ b/solution.py
@@ -163,66 +163,52 @@
     return jax.ShapeDtypeStruct(dims, kind)
 
 
-def live_column(count_ref, images, padded):
-    rows = lax.broadcasted_iota(jnp.int32, (padded, 1), 0)
-    return jnp.concatenate(
-        [jnp.where(rows < count_ref[b], 1.0, 0.0).astype(f32) for b in range(images)], axis=0
-    )
-
-
-def turned_hot(index_ref, padded_ref, image, slots, padded):
-    wide = padded_ref[image : image + 1, :padded]
+def turned_hot(index_ref, image, slots, padded):
     place = lax.broadcasted_iota(jnp.int32, (slots, padded), 0)
-    return jnp.where(place == wide, 1.0, 0.0).astype(bf16)
-
-
-def fill_index(index_ref, padded_ref):
-    padded_ref[...] = jnp.full(padded_ref.shape, -1, jnp.int32)
-    padded_ref[: index_ref.shape[0], : index_ref.shape[1]] = index_ref[...]
-
-
-def pick_rows(index_ref, source_ref, rows_ref, padded_ref):
-    images, slots, _ = source_ref.shape
-    padded = rows_ref.shape[0] // images
-    fill_index(index_ref, padded_ref)
-    for b in range(images):
-        hot = turned_hot(index_ref, padded_ref, b, slots, padded)
-        rows = slice(b * padded, (b + 1) * padded)
-        rows_ref[rows, :] = dot(hot, source_ref[b], ((0,), (0,))).astype(bf16)
+    return jnp.where(place == index_ref[image : image + 1, :padded], 1.0, 0.0).astype(bf16)
 
 
 def front_kernel(
-    index_ref,
+    index_in_ref,
     tokens_ref,
+    count_in_ref,
     router_w_ref,
     gain_ref,
     shift_ref,
+    cotangent_ref,
+    index_ref,
+    count_ref,
     picked_ref,
+    grad_picked_ref,
     first_ref,
+    grad_mlp_ref,
     router_ref,
-    padded_ref,
+    scale_ref,
+    fc2_bias_grad_ref,
 ):
-    pick_rows(index_ref, tokens_ref, picked_ref, padded_ref)
+    images, slots, _ = tokens_ref.shape
+    padded = picked_ref.shape[0] // images
+    index_ref[...] = jnp.full(index_ref.shape, -1, jnp.int32)
+    index_ref[:images, : index_in_ref.shape[1]] = index_in_ref[...]
+    for b in range(images):
+        hot = turned_hot(index_ref, b, slots, padded)
+        picked_ref[b * padded : (b + 1) * padded, :] = dot(hot, tokens_ref[b], ((0,), (0,))).astype(
+            bf16
+        )
     picked = picked_ref[...].astype(f32)
-    router_ref[...] = jax.nn.sigmoid(jnp.sum(picked * line(router_w_ref), axis=-1, keepdims=True))
+    router = jax.nn.sigmoid(jnp.sum(picked * line(router_w_ref), axis=-1, keepdims=True))
+    router_ref[...] = router
     normed, _ = norm_stats(picked)
     first_ref[...] = (normed * line(gain_ref) + line(shift_ref)).astype(bf16)
-
-
-def grad_front_kernel(
-    count_ref,
-    index_ref,
-    cotangent_ref,
-    router_ref,
-    grad_picked_ref,
-    grad_mlp_ref,
-    fc2_bias_grad_ref,
-    padded_ref,
-):
-    images = cotangent_ref.shape[0]
-    pick_rows(index_ref, cotangent_ref, grad_picked_ref, padded_ref)
-    scale = live_column(count_ref, images, router_ref.shape[0] // images) * router_ref[...]
-    grad_branch = scale * grad_picked_ref[...].astype(f32)
+    rows = lax.broadcasted_iota(jnp.int32, (padded, 1), 0)
+    for b in range(images):
+        count_ref[b : b + 1, :] = jnp.full((1, count_ref.shape[1]), count_in_ref[b], jnp.int32)
+        at = slice(b * padded, (b + 1) * padded)
+        live = jnp.where(rows < count_in_ref[b], 1.0, 0.0).astype(f32)
+        scale_ref[at, :] = live * router_ref[at, :]
+        hot = turned_hot(index_ref, b, slots, padded)
+        grad_picked_ref[at, :] = dot(hot, cotangent_ref[b], ((0,), (0,))).astype(bf16)
+    grad_branch = scale_ref[...] * grad_picked_ref[...].astype(f32)
     grad_mlp_ref[...] = grad_branch.astype(bf16)
     fc2_bias_grad_ref[...] = column_sum(grad_branch)
 
@@ -241,19 +227,52 @@
     return jnp.where(lane < HEAD_DIM, stacked[:half], stacked[half:])
 
 
-def pair_probs(queries, keys, count):
-    scores = dot_turned(queries, keys) * HEAD_DIM ** (-0.5)
-    lane = lax.broadcasted_iota(jnp.int32, scores.shape, 1)
-    scores = jnp.where(lane < count, scores, -1e30)
-    raised = jnp.exp(scores - jnp.max(scores, axis=-1, keepdims=True))
-    return raised * (1.0 / jnp.sum(raised, axis=-1, keepdims=True))
+def pairs_of_heads(images, padded, local):
+    return [
+        (b, slice(b * padded, (b + 1) * padded), at)
+        for b in range(images)
+        for at in range(0, local, 2 * HEAD_DIM)
+    ]
+
+
+def saved_qkv(made_ref, rows, at):
+    local = made_ref.shape[1] // 3
+    return [made_ref[rows, t * local + at : t * local + at + 2 * HEAD_DIM] for t in range(3)]
+
+
+def probabilities(scores, count, axis):
+    key = lax.broadcasted_iota(jnp.int32, scores.shape, axis)
+    scores = jnp.where(key < count, scores, -1e30)
+    raised = jnp.exp(scores - jnp.max(scores, axis=axis, keepdims=True))
+    return raised * (1.0 / jnp.sum(raised, axis=axis, keepdims=True))
+
+
+def project(first_ref, w_ref, made_ref):
+    local = w_ref.shape[2]
+    for t in range(3):
+        made_ref[:, t * local : (t + 1) * local] = dot(first_ref[...], w_ref[t]).astype(bf16)
+
+
+def attend(images, count_ref, made_ref, mixed_ref):
+    padded, local = made_ref.shape[0] // images, mixed_ref.shape[1]
+    units = pairs_of_heads(images, padded, local)
+    qkv = [saved_qkv(made_ref, rows, at) for _, rows, at in units]
+    scores = [dot_turned(stacked_heads(q), k) * HEAD_DIM ** (-0.5) for q, k, _ in qkv]
+    probs = [
+        probabilities(x, count_ref[b : b + 1, 0:1], 1).astype(bf16)
+        for x, (b, _, _) in zip(scores, units)
+    ]
+    mixed = [joined_heads(dot(x, v)) for x, (_, _, v) in zip(probs, qkv)]
+    for x, (_, rows, at) in zip(mixed, units):
+        mixed_ref[rows, at : at + 2 * HEAD_DIM] = x.astype(bf16)
 
 
 def attention_kernel(
+    images,
     count_ref,
     first_ref,
-    qkv_own_ref,
-    qkv_other_ref,
+    w_own_ref,
+    w_other_ref,
     proj_own_ref,
     proj_other_ref,
     picked_ref,
@@ -266,32 +285,22 @@
     mixed_other_ref,
     attention_ref,
     second_ref,
+    pack_ref,
 ):
-    images = count_ref.shape[0]
-    padded = first_ref.shape[0] // images
-    local = qkv_own_ref.shape[2]
-    total = line(proj_bias_ref)
-    for side in range(SIDES):
-        w_ref = (qkv_own_ref, qkv_other_ref)[side]
-        made_ref = (made_own_ref, made_other_ref)[side]
-        mixed_ref = (mixed_own_ref, mixed_other_ref)[side]
-        for t in range(3):
-            made_ref[:, t * local : (t + 1) * local] = dot(first_ref[...], w_ref[t]).astype(
-                bf16
-            )
-        for b in range(images):
-            rows = slice(b * padded, (b + 1) * padded)
-            for at in range(0, local, 2 * HEAD_DIM):
-                q, k, v = (
-                    made_ref[rows, t * local + at : t * local + at + 2 * HEAD_DIM]
-                    for t in range(3)
-                )
-                probs = pair_probs(stacked_heads(q), k, count_ref[b]).astype(bf16)
-                mixed_ref[rows, at : at + 2 * HEAD_DIM] = joined_heads(dot(probs, v)).astype(bf16)
-        total = total + dot(mixed_ref[...], (proj_own_ref, proj_other_ref)[side][...])
+    width = first_ref.shape[1]
+    pack_ref[:, :width] = first_ref[...]
+    project(first_ref, w_own_ref, made_own_ref)
+    project(first_ref, w_other_ref, made_other_ref)
+    attend(images, count_ref, made_own_ref, mixed_own_ref)
+    attend(images, count_ref, made_other_ref, mixed_other_ref)
+    total = line(proj_bias_ref) + dot(mixed_own_ref[...], proj_own_ref[...])
+    total = total + dot(mixed_other_ref[...], proj_other_ref[...])
     attention_ref[...] = total
     normed, _ = norm_stats(picked_ref[...].astype(f32) + total)
-    second_ref[...] = (normed * line(gain_ref) + line(shift_ref)).astype(bf16)
+    second = (normed * line(gain_ref) + line(shift_ref)).astype(bf16)
+    second_ref[...] = second
+    pack_ref[:, width : 2 * width] = second
+    pack_ref[:, 2 * width :] = mixed_other_ref[...]
 
 
 def hidden_kernel(second_ref, w_fc1_ref, bias_ref, act_ref, slope_ref):
@@ -312,6 +321,7 @@
 
 
 TOP_BITS = 4
+FC2_EARLY, FC1_EARLY, ATTN_EARLY = 1, 0, 0
 UNITS = 1 << TOP_BITS
 
 
@@ -320,12 +330,13 @@
     return [(place >> bit) & 1 for bit in range(TOP_BITS)]
 
 
-def order_of(part):
-    return [(part + j) % 3 for j in range(3)] + [3]
-
-
-def bits_left(part, step):
-    return [bit for bit in range(TOP_BITS - 1, -1, -1) if bit not in order_of(part)[:step]]
+def order_of(part, early=0):
+    order = [(part + j) % 3 for j in range(3)] + [3]
+    return order[:2] + [3, order[2]] if part < early else order
+
+
+def bits_left(order, step):
+    return [bit for bit in range(TOP_BITS - 1, -1, -1) if bit not in order[:step]]
 
 
 def every_choice(bits):
@@ -342,23 +353,25 @@
 
 def arrange_rows(turned_ref, mine, part, arranged_ref):
     unit = turned_ref.shape[0] // UNITS
-    bit = order_of(part)[0]
+    order = order_of(part)
+    bit = order[0]
     for side, value in enumerate((1 - mine[bit], mine[bit])):
-        for j, chosen in every_choice(bits_left(part, 1)):
+        for j, chosen in every_choice(bits_left(order, 1)):
             chosen[bit] = value
             to = (side * UNITS // 2 + j) * unit
             arranged_ref[to : to + unit, :] = unit_rows(
-                turned_ref, bits_left(part, 0), chosen, unit
+                turned_ref, bits_left(order, 0), chosen, unit
             )
 
 
 class Stream:
-    def __init__(self, part, away, kept):
+    def __init__(self, part, away, kept, early):
         self.part, self.step, self.away, self.terms = part, 0, away, [(kept, 0, 1)]
+        self.order = order_of(part, early)
         self.unit = kept.shape[0] * 2 // UNITS
 
     def bit(self):
-        return order_of(self.part)[self.step]
+        return self.order[self.step]
 
     def rows(self):
         return self.unit * UNITS >> (self.step + 1)
@@ -384,10 +397,10 @@
     return arrays, plans
 
 
-def plan_sum(refs, plan, part, chosen, unit):
+def plan_sum(refs, plan, order, chosen, unit):
     total = 0.0
     for n, base, step in plan:
-        total = total + unit_rows(refs[n], bits_left(part, step), chosen, unit, base).astype(f32)
+        total = total + unit_rows(refs[n], bits_left(order, step), chosen, unit, base).astype(f32)
     return total
 
 
@@ -396,18 +409,17 @@
     small, outs = refs[n_arrays : n_arrays + n_small], refs[n_arrays + n_small :]
     if n_small:
         outs[-1][...] = sum(ref[...] for ref in small)
-    for part, step, made, unit, plan, out, base in plans:
-        order = order_of(part)
+    for order, step, made, unit, plan, out, base in plans:
         if made:
             ref = refs[plan[0][0]]
             outs[out][base : base + ref.shape[0], :] = ref[...]
             continue
-        for j, chosen in every_choice(bits_left(part, step + 1)):
+        for j, chosen in every_choice(bits_left(order, step + 1)):
             for bit in order[:step]:
                 chosen[bit] = mine[bit]
             chosen[order[step]] = 1 - mine[order[step]]
             to = base + j * unit
-            outs[out][to : to + unit, :] = plan_sum(refs, plan, part, chosen, unit).astype(bf16)
+            outs[out][to : to + unit, :] = plan_sum(refs, plan, order, chosen, unit).astype(bf16)
 
 
 def finish_kernel(n_arrays, n_small, plans, *refs):
@@ -417,8 +429,8 @@
     fc2_ref, fc1_ref, qkv_ref, proj_ref, *outs = refs_out
     local = qkv_ref.shape[2]
     third = local // 3
-    for i, (part, unit, plan) in enumerate(plans):
-        total = plan_sum(refs, plan, part, chosen, unit)
+    for i, (part, order, unit, plan) in enumerate(plans):
+        total = plan_sum(refs, plan, order, chosen, unit)
         if i < 6:
             (fc2_ref, fc1_ref)[i // 3][:, part * UNIT_BLOCK : (part + 1) * UNIT_BLOCK] = total
         else:
@@ -445,10 +457,11 @@
     kept_ref[:, columns] = dot(arranged_ref[half:, :], right)
 
 
-def mlp_weights_kernel(left_own_ref, left_par_ref, right_own_ref, right_par_ref, *outs):
+def mlp_weights_kernel(at_left, left_own_ref, left_par_ref, right_own_ref, right_par_ref, *outs):
     away_refs, kept_refs, (turned_ref, arranged_ref) = outs[:3], outs[3:6], outs[6:]
     mine = my_bits()
-    turned_ref[...] = both_rows(left_own_ref[...], left_par_ref[...]).T
+    left_par = left_par_ref[:, at_left : at_left + left_own_ref.shape[1]]
+    turned_ref[...] = both_rows(left_own_ref[...], left_par).T
     columns = slice(0, UNIT_BLOCK)
     for part in range(3):
         at = slice(part * UNIT_BLOCK, (part + 1) * UNIT_BLOCK)
@@ -459,20 +472,19 @@
 
 def attn_weights_kernel(
     first_own_ref,
-    first_par_ref,
+    pack_par_ref,
     grad_attn_own_ref,
     grad_attn_par_ref,
     qkv_own_ref,
     qkv_par_ref,
     mixed_own_ref,
-    mixed_par_ref,
     *outs,
 ):
     away_refs, kept_refs, (turned_ref, arranged_ref) = outs[:3], outs[3:6], outs[6:]
     mine = my_bits()
-    local = mixed_own_ref.shape[1]
+    width, local = first_own_ref.shape[1], mixed_own_ref.shape[1]
     third = local // 3
-    turned_ref[...] = both_rows(first_own_ref[...], first_par_ref[...]).T
+    turned_ref[...] = both_rows(first_own_ref[...], pack_par_ref[:, :width]).T
     for part in range(3):
         at = slice(part * local, (part + 1) * local)
         right = both_rows(qkv_own_ref[:, at], qkv_par_ref[:, at])
@@ -481,7 +493,7 @@
     turned_ref[...] = both_rows(grad_attn_own_ref[...], grad_attn_par_ref[...]).T
     for part in range(3):
         at = slice(part * third, (part + 1) * third)
-        right = both_rows(mixed_own_ref[:, at], mixed_par_ref[:, at])
+        right = both_rows(mixed_own_ref[:, at], pack_par_ref[:, 2 * width + at.start : 2 * width + at.stop])
         arrange_rows(turned_ref, mine, part, arranged_ref)
         weight_tile(
             arranged_ref, right, away_refs[part], kept_refs[part], slice(local, local + third)
@@ -498,36 +510,37 @@
     )
 
 
-def heads_back(count_ref, grad_attn_ref, proj_ref, made_ref, out_ref, mixed_scratch):
-    images = count_ref.shape[0]
-    padded = made_ref.shape[0] // images
-    local = proj_ref.shape[0]
+def heads_back(images, count_ref, grad_attn_ref, proj_ref, made_ref, out_ref, mixed_scratch):
+    padded, local = made_ref.shape[0] // images, proj_ref.shape[0]
     factor = HEAD_DIM ** (-0.5)
     mixed_scratch[...] = dot_turned(grad_attn_ref[...], proj_ref[...]).astype(bf16)
-    for b in range(images):
-        rows = slice(b * padded, (b + 1) * padded)
-        for at in range(0, local, 2 * HEAD_DIM):
-            q, k, v = (
-                made_ref[rows, t * local + at : t * local + at + 2 * HEAD_DIM] for t in range(3)
-            )
-            q = stacked_heads(q)
-            grad_mixed = stacked_heads(mixed_scratch[rows, at : at + 2 * HEAD_DIM])
-            probs = pair_probs(q, k, count_ref[b])
-            grad_probs = dot_turned(grad_mixed, v)
-            row_dot = jnp.sum(probs * grad_probs, axis=-1, keepdims=True)
-            grad_scores = (probs * (grad_probs - row_dot)).astype(bf16)
-            found = (
-                joined_heads(dot(grad_scores, k)) * factor,
-                dot(grad_scores, q, ((0,), (0,))) * factor,
-                dot(probs.astype(bf16), grad_mixed, ((0,), (0,))),
-            )
+    units = pairs_of_heads(images, padded, local)
+    for first in range(0, len(units), 3):
+        some = units[first : first + 3]
+        q, k, v = zip(*[saved_qkv(made_ref, rows, at) for _, rows, at in some])
+        q = [stacked_heads(x) for x in q]
+        grad_mixed = [
+            stacked_heads(mixed_scratch[rows, at : at + 2 * HEAD_DIM]) for _, rows, at in some
+        ]
+        scores = [dot_turned(x, y) * factor for x, y in zip(k, q)]
+        grad_probs = [dot_turned(x, y) for x, y in zip(v, grad_mixed)]
+        probs = [
+            probabilities(x, count_ref[b : b + 1, 0:1], 0) for x, (b, _, _) in zip(scores, some)
+        ]
+        grad_scores = [
+            (p * (g - jnp.sum(p * g, axis=0, keepdims=True))).astype(bf16)
+            for p, g in zip(probs, grad_probs)
+        ]
+        grad_k = [dot(x, y) * factor for x, y in zip(grad_scores, q)]
+        grad_v = [dot(x.astype(bf16), y) for x, y in zip(probs, grad_mixed)]
+        grad_q = [joined_heads(dot(x, y, ((0,), (0,)))) * factor for x, y in zip(grad_scores, k)]
+        for (_, rows, at), *found in zip(some, grad_q, grad_k, grad_v):
             for t in range(3):
                 to = slice(t * local + at, t * local + at + 2 * HEAD_DIM)
                 out_ref[rows, to] = found[t].astype(bf16)
 
 
 def back_kernel(
-    count_ref,
     grad_pre_other_ref,
     w_fc1_other_ref,
     grad_pre_ref,
@@ -535,37 +548,29 @@
     picked_ref,
     attention_ref,
     grad_picked_ref,
-    router_ref,
+    scale_ref,
     gain_ref,
-    made_ref,
-    proj_ref,
     grad_attn_ref,
     grad_hidden_ref,
-    out_ref,
     sums_ref,
-    mixed_scratch,
 ):
-    images = count_ref.shape[0]
-    padded = picked_ref.shape[0] // images
     grad_second = dot_turned(grad_pre_other_ref[...], w_fc1_other_ref[...])
     grad_second = grad_second + dot_turned(grad_pre_ref[...], w_fc1_ref[...])
     normed, inv_std = norm_stats(picked_ref[...].astype(f32) + attention_ref[...])
     grad_hidden = norm_back(grad_second, line(gain_ref), normed, inv_std)
     grad_hidden_ref[...] = grad_hidden
-    scale = live_column(count_ref, images, padded) * router_ref[...]
-    grad_attention = scale * grad_picked_ref[...].astype(f32) + grad_hidden
+    grad_attention = scale_ref[...] * grad_picked_ref[...].astype(f32) + grad_hidden
     grad_attn_ref[...] = grad_attention.astype(bf16)
     sums_ref[0:1, :] = column_sum(grad_attention)
     sums_ref[1:2, :] = column_sum(grad_second * normed)
     sums_ref[2:3, :] = column_sum(grad_second)
-    heads_back(count_ref, grad_attn_ref, proj_ref, made_ref, out_ref, mixed_scratch)
 
 
 def branch_kernel(
-    count_ref,
     picked_ref,
     grad_picked_ref,
     router_ref,
+    scale_ref,
     attention_ref,
     act_own_ref,
     act_other_ref,
@@ -576,16 +581,13 @@
     grad_logit_ref,
     router_grad_ref,
 ):
-    images = count_ref.shape[0]
-    padded = picked_ref.shape[0] // images
-    router = router_ref[...]
-    scale = live_column(count_ref, images, padded) * router
+    scale = scale_ref[...]
     mlp_out = dot(act_own_ref[...], w_fc2_ref[...]) + dot(act_other_ref[...], w_fc2_other_ref[...])
     branch = attention_ref[...] + (mlp_out + line(fc2_bias_ref))
     update_ref[...] = scale * branch
     grad_logit = (
         scale
-        * (1.0 - router)
+        * (1.0 - router_ref[...])
         * jnp.sum(grad_picked_ref[...].astype(f32) * branch, axis=-1, keepdims=True)
     )
     grad_logit_ref[...] = grad_logit
@@ -645,20 +647,18 @@
 
 
 def put_back_kernel(n_small, index_ref, base_ref, change_ref, *refs):
-    small_refs, outs, padded_ref = refs[:n_small], refs[n_small:-1], refs[-1]
-    out_ref = outs[0]
+    small_refs, outs = refs[:n_small], refs[n_small:]
     if n_small:
         outs[1][...] = sum(ref[...] for ref in small_refs)
     images, slots, _ = base_ref.shape
     padded = change_ref.shape[0] // images
-    fill_index(index_ref, padded_ref)
     for b in range(images):
-        hot = turned_hot(index_ref, padded_ref, b, slots, padded)
+        hot = turned_hot(index_ref, b, slots, padded)
         change = change_ref[b * padded : (b + 1) * padded, :]
         high = change.astype(bf16)
         low = (change - high.astype(f32)).astype(bf16)
         updated = base_ref[b].astype(f32) + (dot(hot, high) + dot(hot, low))
-        out_ref[b] = updated.astype(bf16)
+        outs[0][b] = updated.astype(bf16)
 
 
 def other_core(value):
@@ -673,10 +673,14 @@
     return lax.ppermute(value, "dp", partners(count, bit + count.bit_length() - 1 - TOP_BITS))
 
 
-def begin(halves, count):
-    streams = [Stream(part, None, halves[3 + part]) for part in range(3)]
-    for part, stream in enumerate(streams):
-        stream.sent(swap(halves[part], stream.bit(), count), 0)
+def waiting(halves, early=0):
+    return [Stream(part, halves[part], halves[3 + part], early) for part in range(3)]
+
+
+def begin(halves, count, early=0):
+    streams = waiting(halves, early)
+    for stream in streams:
+        stream.sent(swap(stream.away, stream.bit(), count), 0)
     return streams
 
 
@@ -691,7 +695,7 @@
     for stream, plan in zip(streams, plans):
         out = bits.index(stream.bit())
         made = stream.away is not None
-        full.append((stream.part, stream.step, made, stream.unit, plan, out, sizes[out]))
+        full.append((stream.order, stream.step, made, stream.unit, plan, out, sizes[out]))
         bases.append(sizes[out])
         sizes[out] += stream.rows()
     columns = arrays[0].shape[1]
@@ -705,6 +709,19 @@
     for stream, base in zip(streams, bases):
         stream.sent(got[bits.index(stream.bit())], base)
     return (after, made[-1]) if small else after
+
+
+def arrived(streams, after):
+    arrays = []
+    for stream in streams:
+        if all(stream.terms[-1][0] is not x for x in arrays):
+            arrays.append(stream.terms[-1][0])
+    tied, after = lax.optimization_barrier((arrays, after))
+    for stream in streams:
+        array, base, step = stream.terms[-1]
+        place = [x is array for x in arrays].index(True)
+        stream.terms[-1] = (tied[place], base, step)
+    return after
 
 
 def fewer_rows(grad, count, axis):
@@ -746,27 +763,62 @@
     top = count.bit_length() - 1 - TOP_BITS
     w_qkv_other = other_core(w_qkv)
     w_proj_other = other_core(w_proj)
-    index_scratch = pltpu.VMEM((8, 128), jnp.int32)
-    heads_scratch = pltpu.VMEM((rows, local), bf16)
+    bias_other = other_core(fc1_bias)
     tie = lax.optimization_barrier
-    picked, first, router, *near = call(
+    table = shape((8, 128), jnp.int32)
+    (
+        index,
+        counts,
+        picked,
+        grad_picked,
+        first,
+        grad_mlp,
+        router,
+        scale,
+        fc2_bias_sum,
+        w_qkv,
+        w_proj,
+        proj_bias,
+        ln2_gain,
+        ln2_bias,
+        bias_own,
+        fc2_bias,
+        ln1_gain,
+        w_router,
+    ) = call(
         front_kernel,
-        [shape((rows, width), bf16), shape((rows, width), bf16), shape((rows, 1), f32)],
-        (Far(kept_index), Far(tokens), Far(w_router), Far(ln1_gain), Far(ln1_bias)),
-        scratch=[index_scratch],
-        fetch=(w_qkv, w_proj, proj_bias, ln2_gain, ln2_bias, fc1_bias, fc2_bias, ln1_gain, w_router),
-    )
-    w_qkv, w_proj, proj_bias, ln2_gain, ln2_bias, bias_own, fc2_bias, ln1_gain, w_router = near
-    w_fc1_late, w_fc2_late, bias_late, first, w_qkv_other, w_proj_other = tie(
-        (w_fc1, w_fc2, fc1_bias, first, w_qkv_other, w_proj_other)
+        [table, table]
+        + [shape((rows, width), bf16)] * 4
+        + [shape((rows, 1), f32)] * 2
+        + [shape((1, width), f32)],
+        (
+            Far(kept_index),
+            Far(tokens),
+            Far(kept_count),
+            Far(w_router),
+            Far(ln1_gain),
+            Far(ln1_bias),
+            Far(cotangent),
+        ),
+        fetch=(
+            w_qkv,
+            w_proj,
+            proj_bias,
+            ln2_gain,
+            ln2_bias,
+            fc1_bias,
+            fc2_bias,
+            ln1_gain,
+            w_router,
+        ),
+    )
+    w_fc1_late, bias_other, first, w_qkv_other, w_proj_other = tie(
+        (w_fc1, bias_other, first, w_qkv_other, w_proj_other)
     )
     w_fc1_other = other_core(w_fc1_late)
-    bias_other = other_core(bias_late)
-    w_fc2_other = other_core(w_fc2_late)
-    first_par = other_core(first)
-
-    made, made_other, mixed, mixed_other, attention, second, w_fc1, w_fc2 = call(
-        attention_kernel,
+
+    made, made_other, mixed, mixed_other, attention, second, pack = call(
+        functools.partial(attention_kernel, images),
         [
             shape((rows, 3 * local), bf16),
             shape((rows, 3 * local), bf16),
@@ -774,9 +826,10 @@
             shape((rows, local), bf16),
             shape((rows, width), f32),
             shape((rows, width), bf16),
+            shape((rows, 2 * width + local), bf16),
         ],
         (
-            Far(kept_count),
+            counts,
             first,
             w_qkv,
             w_qkv_other,
@@ -787,11 +840,9 @@
             ln2_gain,
             ln2_bias,
         ),
-        fetch=(w_fc1, w_fc2),
-    )
-    second, first_par = tie((second, first_par))
-    mixed_par = other_core(mixed_other)
-    second_par = other_core(second)
+    )
+    second, grad_mlp = tie((second, grad_mlp))
+    grad_mlp_par = other_core(grad_mlp)
 
     def hidden(w, bias):
         return call(
@@ -807,44 +858,35 @@
             (grad_mlp, w, slope),
         )
 
-    def mlp_weights(left, left_par, right, right_par):
+    def mlp_weights(left, left_par, at_left, right, right_par):
         return weights(
-            mlp_weights_kernel, (left, left_par, right, right_par), width, 2 * rows, UNIT_BLOCK
+            functools.partial(mlp_weights_kernel, at_left),
+            (left, left_par, right, right_par),
+            width,
+            2 * rows,
+            UNIT_BLOCK,
         )
 
     act_other, slope_other = hidden(w_fc1_other, bias_other)
     act_par = other_core(act_other)
-    router, act_other = tie((router, act_other))
-    grad_picked, grad_mlp, fc2_bias_sum, cotangent = call(
-        grad_front_kernel,
-        [shape((rows, width), bf16), shape((rows, width), bf16), shape((1, width), f32)],
-        (Far(kept_count), Far(kept_index), Far(cotangent), router),
-        scratch=[index_scratch],
-        fetch=(cotangent,),
-    )
-    grad_mlp_par = other_core(grad_mlp)
-    second, grad_mlp, mixed_par, second_par = tie((second, grad_mlp, mixed_par, second_par))
+    bias_own, act_other = tie((bias_own, act_other))
     act, slope = hidden(w_fc1, bias_own)
-    halves = mlp_weights(grad_mlp, grad_mlp_par, act, act_par)
+    w_fc2_late, act_par, grad_mlp_par, pack, slope = tie(
+        (w_fc2, act_par, grad_mlp_par, pack, slope)
+    )
+    w_fc2_other = other_core(w_fc2_late)
+    pack_par = other_core(pack)
+    grad_pre, unit_own = hidden_back(w_fc2, slope)
+    act, grad_pre = tie((act, grad_pre))
+    halves = mlp_weights(grad_mlp, grad_mlp_par, 0, act, act_par)
     halves, slope_other = tie((halves, slope_other))
-    mlp_sums = begin(halves, count)
+    fc2_sums = begin(halves, count, FC2_EARLY)
     grad_pre_other, unit_other = hidden_back(w_fc2_other, slope_other)
     grad_pre_par = other_core(grad_pre_other)
-    grad_pre, unit_own = hidden_back(w_fc2, slope)
-    halves = mlp_weights(second, second_par, grad_pre, grad_pre_par)
-    halves, grad_pre = tie((halves, grad_pre))
-    mlp_sums += begin(halves, count)
-
-    grad_attn, grad_hidden, grad_qkv_other, back_sums = call(
+    grad_attn, grad_hidden, back_sums = call(
         back_kernel,
-        [
-            shape((rows, width), bf16),
-            shape((rows, width), f32),
-            shape((rows, 3 * local), bf16),
-            shape((8, width), f32),
-        ],
+        [shape((rows, width), bf16), shape((rows, width), f32), shape((8, width), f32)],
         (
-            Far(kept_count),
             grad_pre_other,
             w_fc1_other,
             grad_pre,
@@ -852,40 +894,47 @@
             picked,
             attention,
             grad_picked,
-            router,
+            scale,
             ln2_gain,
-            made_other,
-            w_proj_other,
         ),
-        scratch=[heads_scratch],
+    )
+    grad_pre, grad_attn = tie((grad_pre, grad_attn))
+    halves = mlp_weights(second, pack_par, width, grad_pre, grad_pre_par)
+
+    def attention_back(w, saved, grad):
+        return call(
+            functools.partial(heads_back, images),
+            [shape((rows, 3 * local), bf16)],
+            (counts, grad, w, saved),
+            scratch=[pltpu.VMEM((rows, local), bf16)],
+        )[0]
+
+    halves, grad_attn = tie((halves, grad_attn))
+    grad_qkv_other = attention_back(w_proj_other, made_other, grad_attn)
+    fc1_sums = waiting(halves, FC1_EARLY)
+    grad_attn, grad_qkv_other = exchange(
+        (*fc2_sums, *fc1_sums), count, (grad_attn, grad_qkv_other)
     )
     grad_attn_par = other_core(grad_attn)
     grad_qkv_par = other_core(grad_qkv_other)
-    grad_attn = exchange(mlp_sums, count, grad_attn)
-    grad_attn, grad_attn_par, grad_qkv_par = tie((grad_attn, grad_attn_par, grad_qkv_par))
-    (grad_qkv,) = call(
-        heads_back,
-        [shape((rows, 3 * local), bf16)],
-        (Far(kept_count), grad_attn, w_proj, made),
-        scratch=[heads_scratch],
-    )
+    grad_qkv = attention_back(w_proj, made, grad_attn)
     halves = weights(
         attn_weights_kernel,
-        (first, first_par, grad_attn, grad_attn_par, grad_qkv, grad_qkv_par, mixed, mixed_par),
+        (first, pack_par, grad_attn, grad_attn_par, grad_qkv, grad_qkv_par, mixed),
         width,
         2 * rows,
         local + local // 3,
     )
-    attn_sums = [Stream(part, halves[part], halves[3 + part]) for part in range(3)]
-    act = exchange((*mlp_sums, *attn_sums), count, act)
+    attn_sums = waiting(halves, ATTN_EARLY)
+    act = exchange((*fc2_sums, *fc1_sums, *attn_sums), count, act)
     update, grad_logit, router_sum = call(
         branch_kernel,
         [shape((rows, width), f32), shape((rows, 1), f32), shape((1, width), f32)],
         (
-            Far(kept_count),
             picked,
             grad_picked,
             router,
+            scale,
             attention,
             act,
             act_other,
@@ -925,8 +974,7 @@
         return call(
             functools.partial(put_back_kernel, len(small)),
             [Far(shape(base.shape, bf16)), *[shape(x.shape, x.dtype) for x in small[:1]]],
-            (Far(kept_index), base, change, *small),
-            scratch=[index_scratch],
+            (index, base, change, *small),
         )
 
     got = other_core(send)
@@ -934,18 +982,22 @@
     output, small = put_back(tokens, update, keep, got)
     got = swap(small, 0, count)
     grad_kept, output = tie((grad_kept, output))
-    grad_kept, small = exchange((*mlp_sums, *attn_sums), count, grad_kept, (small, got))
+    (input_grad,) = put_back(cotangent, grad_kept)
+    input_grad, small = exchange(
+        (*fc2_sums, *fc1_sums, *attn_sums), count, input_grad, (small, got)
+    )
     got = swap(small, 1, count)
-    (input_grad,) = put_back(cotangent, grad_kept)
-    input_grad, small = exchange(attn_sums, count, input_grad, (small, got))
+    input_grad = arrived(fc2_sums, input_grad)
+    input_grad, small = exchange((*fc1_sums, *attn_sums), count, input_grad, (small, got))
     got = swap(small, 2, count)
+    input_grad = arrived(fc1_sums, input_grad)
     input_grad, small = exchange(attn_sums, count, input_grad, (small, got))
     for low in range(top):
         small = small + lax.ppermute(small, "dp", partners(count, low))
     got = swap(small, 3, count)
-    sums = (*mlp_sums, *attn_sums)
+    sums = (*fc2_sums, *fc1_sums, *attn_sums)
     arrays, plans = listed(sums)
-    plans = [(stream.part, stream.unit, plan) for stream, plan in zip(sums, plans)]
+    plans = [(stream.part, stream.order, stream.unit, plan) for stream, plan in zip(sums, plans)]
     unit = width // UNITS
     fc2_turned, fc1_grad, qkv_grad, proj_turned, *sums = call(
         functools.partial(finish_kernel, len(arrays), 2, plans),

time: 107 us -> 103 us (0.963)
  Pallas kernels: 48.5 us -> 36.5 us
  waiting for transfers between devices: 25 us -> 31.4 us
  starting transfers between devices: 32.2 us -> 34.2 us
    pallas_call x22, Pallas kernels: 48.5 us -> 36.5 us  [call(): pl.pallas_call(body, out_shape=[(pltpu.HBM if i in far_out else pltpu.VME...]
    ppermute x24 -> x23, waiting for transfers between devices: 18 us -> 26.8 us  [swap(): lax.ppermute(value, 'dp', partners(count, bit + count.bit_length() - 1 -...]
    ppermute x24 -> x23, starting transfers between devices: 28.4 us -> 31.1 us  [swap(): lax.ppermute(value, 'dp', partners(count, bit + count.bit_length() - 1 -...]
    ppermute x14 -> x12, waiting for transfers between devices: 6.93 us -> 4.57 us  [other_core(): return lax.ppermute(value, 'head', [(0, 1), (1, 0)])]
    ppermute x14 -> x12, starting transfers between devices: 3.83 us -> 3.13 us  [other_core(): return lax.ppermute(value, 'head', [(0, 1), (1, 0)])]
  transfers between devices with their start and end apart: 38 -> 35, of which waited for: 13 -> 17; matrix products, arithmetic and copies ran while one was open for 0% -> 0% of each run, Pallas kernels for 43% -> 32%
where the time goes in v2:
time: 103 us
  Pallas kernels  36.5 us (35%)
  starting transfers between devices  34.2 us (33%)
  waiting for transfers between devices  31.4 us (30%)
  between operations  1.1 us (1%)
    pallas_call x22, Pallas kernels, call(): pl.pallas_call(body, out_shape=[(pltpu.HBM if i in far_out else pltpu.VME...  36.5 us
    ppermute x23, starting transfers between devices, swap(): lax.ppermute(value, 'dp', partners(count, bit + count.bit_length() - 1 -...  31.1 us
    ppermute x23, waiting for transfers between devices, swap(): lax.ppermute(value, 'dp', partners(count, bit + count.bit_length() - 1 -...  26.8 us
    ppermute x12, waiting for transfers between devices, other_core(): return lax.ppermute(value, 'head', [(0, 1), (1, 0)])  4.57 us
    ppermute x12, starting transfers between devices, other_core(): return lax.ppermute(value, 'head', [(0, 1), (1, 0)])  3.13 us
  transfers between devices with their start and end apart: 35, of which 17 were waited for; matrix products, arithmetic and copies ran while one was open for 0% of the time, Pallas kernels for 32%

profile of v2, /device:TPU:0, one launch (start us, length us, event | category | flops | bytes accessed | tf_op | source)
XLA Modules:
  0.0 103.2 jit_solution(17125989397449258744)
XLA Ops:
  1.7 2.6 %shard_map.263 = (s32[8,128]{1,0:T(8,128)S(1)}, s32[8,128]{1,0:T(8,128)S(1)}, bf16[336,768]{1,0:T(8,128)(2,1)S(1)}, bf16[336,768]{1,0:T(8,128)(2,1)S(1)}, bf16[3...) custom-call(s32[3,98]{1,0:T(4,128)} %refs_0_.1, ...), custom_call_target="tpu_custom_call" | custom-call | flops 1 | bytes 1 | tf_op jit(solution)/shard_map/pallas_call | solution.py:144
  6.0 3.9 %shard_map.264 = (bf16[336,1152]{1,0:T(8,128)(2,1)S(1)}, bf16[336,1152]{1,0:T(8,128)(2,1)S(1)}, bf16[336,384]{1,0:T(8,128)(2,1)S(1)}, bf16[336,384]{1,0:T(8,128)...) custom-call(s32[8,128]{1,0:T(8,128)S(1)} %get-tuple-element.252.refs_0_, ...), custom_call_target="tpu_custom_call" | custom-call | flops 1 | bytes 1 | tf_op jit(solution)/shard_map/pallas_call | solution.py:144
  16.7 2.5 %shard_map.268 = (bf16[384,512]{1,0:T(8,128)(2,1)S(1)}, bf16[384,512]{1,0:T(8,128)(2,1)S(1)}, bf16[384,512]{1,0:T(8,128)(2,1)S(1)}, f32[384,512]{1,0:T(8,128)S(1...) custom-call(bf16[336,768]{1,0:T(8,128)(2,1)S(1)} %get-tuple-element.263.refs_0_, ...), custom_call_target="tpu_custom_call" | custom-call | flops 1 | bytes 1 | tf_op jit(solution)/shard_map/pallas_call | solution.py:144
  21.2 2.6 %collective-permute-start.7 = (bf16[384,512]{1,0:T(8,128)(2,1)S(1)}, bf16[384,512]{1,0:T(8,128)(2,1)S(1)}, u32[]{:S(2)}, u32[]{:S(2)}) collective-permute-start(bf16[384,512]{1,0:T(8,128)(2,1)S(1)} %get-tuple-element.295), channel_id=1, source_target_pairs={{0,2},{2,0},{4,6},{6,4},{8,10},{10,8},{12,14},{14,12},{16,18},{18,... | collective-permute-start | bytes 1179656 | tf_op jit(solution)/shard_map/ppermute | solution.py:673
  25.4 1.6 %collective-permute-start.9 = (bf16[384,512]{1,0:T(8,128)(2,1)S(1)}, bf16[384,512]{1,0:T(8,128)(2,1)S(1)}, u32[]{:S(2)}, u32[]{:S(2)}) collective-permute-start(bf16[384,512]{1,0:T(8,128)(2,1)S(1)} %get-tuple-element.299), channel_id=1, source_target_pairs={{0,8},{2,10},{4,12},{6,14},{8,0},{10,2},{12,4},{14,6},{16,24},{18,... | collective-permute-start | bytes 1179656 | tf_op jit(solution)/shard_map/ppermute | solution.py:673
  26.9 2.5 %shard_map.270 = (bf16[336,768]{1,0:T(8,128)(2,1)S(1)}, f32[336,768]{1,0:T(8,128)S(1)}, f32[8,768]{1,0:T(8,128)S(1)}) custom-call(bf16[336,1536]{1,0:T(8,128)(2,1)S(1)} %get-tuple-element.287.refs_0_, bf16[768,1536]{1,0:T(8,128)(2,1)S(1)} %collective-permute-done.3.refs_1_, bf16[336,1536]{1,0:T(8,128)(2,1)S(1)} %get-tuple-element.302.refs_2_, ...), custom_call_target="tpu_custom_call" | custom-call | flops 1 | bytes 1 | tf_op jit(solution)/shard_map/pallas_call | solution.py:144
  29.5 2.5 %shard_map.271 = (bf16[384,512]{1,0:T(8,128)(2,1)S(1)}, bf16[384,512]{1,0:T(8,128)(2,1)S(1)}, bf16[384,512]{1,0:T(8,128)(2,1)S(1)}, f32[384,512]{1,0:T(8,128)S(1...) custom-call(bf16[336,768]{1,0:T(8,128)(2,1)S(1)} %get-tuple-element.264.refs_0_, ...), custom_call_target="tpu_custom_call" | custom-call | flops 1 | bytes 1 | tf_op jit(solution)/shard_map/pallas_call | solution.py:144
  31.9 1.8 %shard_map.272.refs_7_ = bf16[336,1152]{1,0:T(8,128)(2,1)S(1)} custom-call(s32[8,128]{1,0:T(8,128)S(1)} %get-tuple-element.252.refs_0_, bf16[336,768]{1,0:T(8,128)(2,1)S(1)} %get-tuple-element.335.refs_1_.refs_2_, bf16[384,768]{1,0:T(8,128)(2,1)S(1)} %collective-permute-done.2.refs_5_.refs_2_, bf16[336,1152]{1,0:T(8,128)(2,1)S(1)} %get-tuple-element.314.refs_3_), custom_call_target="tpu_custom_call" | custom-call | flops 1 | bytes 1 | tf_op jit(solution)/shard_map/pallas_call | solution.py:144
  37.0 1.6 %collective-permute-start.13 = (bf16[576,512]{1,0:T(8,128)(2,1)S(1)}, bf16[576,512]{1,0:T(8,128)(2,1)S(1)}, u32[]{:S(2)}, u32[]{:S(2)}) collective-permute-start(bf16[576,512]{1,0:T(8,128)(2,1)S(1)} %get-tuple-element.330), channel_id=1, source_target_pairs={{0,8},{2,10},{4,12},{6,14},{8,0},{10,2},{12,4},{14,6},{16,24},{18,... | collective-permute-start | bytes 1769480 | tf_op jit(solution)/shard_map/ppermute | solution.py:673
  39.1 1.8 %shard_map.274.refs_4_.refs_6_ = bf16[336,1152]{1,0:T(8,128)(2,1)S(1)} custom-call(s32[8,128]{1,0:T(8,128)S(1)} %get-tuple-element.252.refs_0_, bf16[336,768]{1,0:T(8,128)(2,1)S(1)} %get-tuple-element.335.refs_1_.refs_2_, bf16[384,768]{1,0:T(8,128)(2,1)S(1)} %get-tuple-element.256.refs_4_.refs_2_, bf16[336,1152]{1,0:T(8,128)(2,1)S(1)} %get-tuple-element.336.refs_3_), custom_call_target="tpu_custom_call" | custom-call | flops 1 | bytes 1 | tf_op jit(solution)/shard_map/pallas_call | solution.py:144
  41.0 3.7 %shard_map.275 = (bf16[384,512]{1,0:T(8,128)(2,1)S(1)}, bf16[384,512]{1,0:T(8,128)(2,1)S(1)}, bf16[384,512]{1,0:T(8,128)(2,1)S(1)}, f32[384,512]{1,0:T(8,128)S(1...) custom-call(bf16[336,768]{1,0:T(8,128)(2,1)S(1)} %get-tuple-element.254.refs_1_.refs_0_, ...), custom_call_target="tpu_custom_call" | custom-call | flops 1 | bytes 1 | tf_op jit(solution)/shard_map/pallas_call | solution.py:144
  44.7 7.5 %collective-permute-done.12.refs_2_.refs_5_ = bf16[576,512]{1,0:T(8,128)(2,1)S(1)} collective-permute-done((bf16[576,512]{1,0:T(8,128)(2,1)S(1)}, bf16[576,512]{1,0:T(8,128)(2,1)S(1)}, u32[]{:S(2)}, u32[]{:S(2)}) %collective-permute-start.12) | collective-permute-done | bytes 589856 | tf_op jit(solution)/shard_map/ppermute | solution.py:673
  56.6 2.6 %collective-permute-start.19 = (bf16[96,512]{1,0:T(8,128)(2,1)S(1)}, bf16[96,512]{1,0:T(8,128)(2,1)S(1)}, u32[]{:S(2)}, u32[]{:S(2)}) collective-permute-start(bf16[96,512]{1,0:T(8,128)(2,1)S(1)} %get-tuple-element.382), channel_id=1, source_target_pairs={{0,16},{2,18},{4,20},{6,22},{8,24},{10,26},{12,28},{14,30},{16,0},... | collective-permute-start | bytes 294920 | tf_op jit(solution)/shard_map/ppermute | solution.py:673
  59.1 2.0 %shard_map.277 = (f32[336,768]{1,0:T(8,128)S(1)}, f32[336,1]{1,0:T(8,128)S(1)}, f32[1,768]{1,0:T(1,128)S(1)}) custom-call(bf16[336,768]{1,0:T(8,128)(2,1)S(1)} %get-tuple-element.251.refs_6_.refs_4_.refs_0_.refs_3_, bf16[336,768]{1,0:T(8,128)(2,1)S(1)} %get-tuple-element.290.refs_6_.refs_1_, f32[336,1]{1,0:T(8,128)S(1)} %get-tuple-element.293.refs_2_, ...), custom_call_target="tpu_custom_call" | custom-call | flops 1 | bytes 1 | tf_op jit(solution)/shard_map/pallas_call | solution.py:144
  61.2 2.6 %shard_map.278 = (f32[336,768]{1,0:T(8,128)S(1)}, f32[9,768]{1,0:T(8,128)S(1)}, f32[9,768]{1,0:T(8,128)S(1)}) custom-call(bf16[3,768,384]{2,1,0:T(8,128)(2,1)S(1)} %get-tuple-element.248.refs_2_.refs_0_, f32[768]{0:T(1024)S(1)} %get-tuple-element.249.refs_1_, f32[768]{0:T(1024)S(1)} %get-tuple-element.250.refs_2_, ...), custom_call_target="tpu_custom_call" | custom-call | flops 1 | bytes 1 | tf_op jit(solution)/shard_map/pallas_call | solution.py:144
  65.1 1.6 %shard_map.279 = (bf16[3,197,768]{2,1,0:T(8,128)(2,1)}, f32[9,768]{1,0:T(8,128)S(1)}) custom-call(s32[8,128]{1,0:T(8,128)S(1)} %get-tuple-element.372.refs_0_, bf16[3,197,768]{2,1,0:T(8,128)(2,1)S(1)} %copy-done.2, f32[336,768]{1,0:T(8,128)S(1)} %get-tuple-element.375.refs_2_, f32[9,768]{1,0:T(8,128)S(1)} %get-tuple-element.376.refs_3_, ...), custom_call_target="tpu_custom_call" | custom-call | flops 1 | bytes 1 | tf_op jit(solution)/shard_map/pallas_call | solution.py:144
  68.3 1.6 %shard_map.280 = bf16[3,197,768]{2,1,0:T(8,128)(2,1)} custom-call(s32[8,128]{1,0:T(8,128)S(1)} %get-tuple-element.372.refs_0_, bf16[3,197,768]{2,1,0:T(8,128)(2,1)S(1)} %copy-done.3, f32[336,768]{1,0:T(8,128)S(1)} %get-tuple-element.387.refs_2_), custom_call_target="tpu_custom_call" | custom-call | flops 1 | bytes 1 | tf_op jit(solution)/shard_map/pallas_call | solution.py:144
  70.0 1.9 %collective-permute-done.21.refs_14_.refs_6_.refs_9_.refs_18_ = bf16[576,512]{1,0:T(8,128)(2,1)S(1)} collective-permute-done((bf16[576,512]{1,0:T(8,128)(2,1)S(1)}, bf16[576,512]{1,0:T(8,128)(2,1)S(1)}, u32[]{:S(2)}, u32[]{:S(2)}) %collective-permute-start.21) | collective-permute-done | bytes 589856 | tf_op jit(solution)/shard_map/ppermute | solution.py:673
  72.2 2.7 %collective-permute-start.24 = (bf16[336,512]{1,0:T(8,128)(2,1)S(1)}, bf16[336,512]{1,0:T(8,128)(2,1)S(1)}, u32[]{:S(2)}, u32[]{:S(2)}) collective-permute-start(bf16[336,512]{1,0:T(8,128)(2,1)S(1)} %get-tuple-element.415), channel_id=1, source_target_pairs={{0,8},{2,10},{4,12},{6,14},{8,0},{10,2},{12,4},{14,6},{16,24},{18,... | collective-permute-start | bytes 1032200 | tf_op jit(solution)/shard_map/ppermute | solution.py:673
  79.0 3.5 %collective-permute-done.26.refs_9_ = bf16[96,512]{1,0:T(8,128)(2,1)S(1)} collective-permute-done((bf16[96,512]{1,0:T(8,128)(2,1)S(1)}, bf16[96,512]{1,0:T(8,128)(2,1)S(1)}, u32[]{:S(2)}, u32[]{:S(2)}) %collective-permute-start.26) | collective-permute-done | bytes 98336 | tf_op jit(solution)/shard_map/ppermute | solution.py:673
  83.4 2.2 %collective-permute-start.31 = (bf16[144,512]{1,0:T(8,128)(2,1)S(1)}, bf16[144,512]{1,0:T(8,128)(2,1)S(1)}, u32[]{:S(2)}, u32[]{:S(2)}) collective-permute-start(bf16[144,512]{1,0:T(8,128)(2,1)S(1)} %get-tuple-element.445), channel_id=1, source_target_pairs={{0,16},{2,18},{4,20},{6,22},{8,24},{10,26},{12,28},{14,30},{16,0},... | collective-permute-start | bytes 442376 | tf_op jit(solution)/shard_map/ppermute | solution.py:673
  85.8 1.9 %collective-permute-start.29 = (bf16[96,512]{1,0:T(8,128)(2,1)S(1)}, bf16[96,512]{1,0:T(8,128)(2,1)S(1)}, u32[]{:S(2)}, u32[]{:S(2)}) collective-permute-start(bf16[96,512]{1,0:T(8,128)(2,1)S(1)} %get-tuple-element.443), channel_id=1, source_target_pairs={{0,2},{2,0},{4,6},{6,4},{8,10},{10,8},{12,14},{14,12},{16,18},{18,... | collective-permute-start | bytes 294920 | tf_op jit(solution)/shard_map/ppermute | solution.py:673
  89.6 3.4 %collective-permute-done.31.refs_16_ = bf16[144,512]{1,0:T(8,128)(2,1)S(1)} collective-permute-done((bf16[144,512]{1,0:T(8,128)(2,1)S(1)}, bf16[144,512]{1,0:T(8,128)(2,1)S(1)}, u32[]{:S(2)}, u32[]{:S(2)}) %collective-permute-start.31) | collective-permute-done | bytes 147488 | tf_op jit(solution)/shard_map/ppermute | solution.py:673
  96.2 5.8 %collective-permute-done.34.refs_30_ = f32[9,768]{1,0:T(8,128)S(1)} collective-permute-done((f32[9,768]{1,0:T(8,128)S(1)}, f32[9,768]{1,0:T(8,128)S(1)}, u32[]{:S(2)}, u32[]{:S(2)}) %collective-permute-start.34) | collective-permute-done | bytes 27680 | tf_op jit(solution)/shard_map/ppermute | solution.py:673
  (76 shorter events, 35.7 us)
Async XLA Ops:
  15.6 13.9 %collective-permute-start.10 = (bf16[336,1920]{1,0:T(8,128)(2,1)S(1)}, bf16[336,1920]{1,0:T(8,128)(2,1)S(1)}, u32[]{:S(2)}, u32[]{:S(2)}) collective-permute-start(bf16[336,1920]{1,0:T(8,128)(2,1)S(1)} %get-tuple-element.300), channel_id=1, source_target_pairs={{0,1},{1,0},{2,3},{3,2},{4,5},{5,4},{6,7},{7,6},{8,9},{9,8},{10,11... | collective-permute-start | bytes 3870728 | tf_op jit(solution)/shard_map/ppermute | solution.py:665
  20.8 8.7 %collective-permute-start.11 = (bf16[336,1536]{1,0:T(8,128)(2,1)S(1)}, bf16[336,1536]{1,0:T(8,128)(2,1)S(1)}, u32[]{:S(2)}, u32[]{:S(2)}) collective-permute-start(bf16[336,1536]{1,0:T(8,128)(2,1)S(1)} %get-tuple-element.287.refs_0_), channel_id=1, source_target_pairs={{0,1},{1,0},{2,3},{3,2},{4,5},{5,4},{6,7},{7,6},{8,9},{9,8},{10,11... | collective-permute-start | bytes 3096584 | tf_op jit(solution)/shard_map/ppermute | solution.py:665
  21.2 12.6 %collective-permute-start.7 = (bf16[384,512]{1,0:T(8,128)(2,1)S(1)}, bf16[384,512]{1,0:T(8,128)(2,1)S(1)}, u32[]{:S(2)}, u32[]{:S(2)}) collective-permute-start(bf16[384,512]{1,0:T(8,128)(2,1)S(1)} %get-tuple-element.295), channel_id=1, source_target_pairs={{0,2},{2,0},{4,6},{6,4},{8,10},{10,8},{12,14},{14,12},{16,18},{18,... | collective-permute-start | bytes 1179656 | tf_op jit(solution)/shard_map/ppermute | solution.py:673
  23.8 11.1 %collective-permute-start.8 = (bf16[384,512]{1,0:T(8,128)(2,1)S(1)}, bf16[384,512]{1,0:T(8,128)(2,1)S(1)}, u32[]{:S(2)}, u32[]{:S(2)}) collective-permute-start(bf16[384,512]{1,0:T(8,128)(2,1)S(1)} %get-tuple-element.297), channel_id=1, source_target_pairs={{0,4},{2,6},{4,0},{6,2},{8,12},{10,14},{12,8},{14,10},{16,20},{18,... | collective-permute-start | bytes 1179656 | tf_op jit(solution)/shard_map/ppermute | solution.py:673
  25.4 10.8 %collective-permute-start.9 = (bf16[384,512]{1,0:T(8,128)(2,1)S(1)}, bf16[384,512]{1,0:T(8,128)(2,1)S(1)}, u32[]{:S(2)}, u32[]{:S(2)}) collective-permute-start(bf16[384,512]{1,0:T(8,128)(2,1)S(1)} %get-tuple-element.299), channel_id=1, source_target_pairs={{0,8},{2,10},{4,12},{6,14},{8,0},{10,2},{12,4},{14,6},{16,24},{18,... | collective-permute-start | bytes 1179656 | tf_op jit(solution)/shard_map/ppermute | solution.py:673
  36.4 15.7 %collective-permute-start.12 = (bf16[576,512]{1,0:T(8,128)(2,1)S(1)}, bf16[576,512]{1,0:T(8,128)(2,1)S(1)}, u32[]{:S(2)}, u32[]{:S(2)}) collective-permute-start(bf16[576,512]{1,0:T(8,128)(2,1)S(1)} %get-tuple-element.329), channel_id=1, source_target_pairs={{0,4},{2,6},{4,0},{6,2},{8,12},{10,14},{12,8},{14,10},{16,20},{18,... | collective-permute-start | bytes 1769480 | tf_op jit(solution)/shard_map/ppermute | solution.py:673
  37.0 15.4 %collective-permute-start.13 = (bf16[576,512]{1,0:T(8,128)(2,1)S(1)}, bf16[576,512]{1,0:T(8,128)(2,1)S(1)}, u32[]{:S(2)}, u32[]{:S(2)}) collective-permute-start(bf16[576,512]{1,0:T(8,128)(2,1)S(1)} %get-tuple-element.330), channel_id=1, source_target_pairs={{0,8},{2,10},{4,12},{6,14},{8,0},{10,2},{12,4},{14,6},{16,24},{18,... | collective-permute-start | bytes 1769480 | tf_op jit(solution)/shard_map/ppermute | solution.py:673
  38.6 15.1 %collective-permute-start.14 = (bf16[576,512]{1,0:T(8,128)(2,1)S(1)}, bf16[576,512]{1,0:T(8,128)(2,1)S(1)}, u32[]{:S(2)}, u32[]{:S(2)}) collective-permute-start(bf16[576,512]{1,0:T(8,128)(2,1)S(1)} %get-tuple-element.331), channel_id=1, source_target_pairs={{0,2},{2,0},{4,6},{6,4},{8,10},{10,8},{12,14},{14,12},{16,18},{18,... | collective-permute-start | bytes 1769480 | tf_op jit(solution)/shard_map/ppermute | solution.py:673
  54.0 17.9 %collective-permute-start.18 = (bf16[672,512]{1,0:T(8,128)(2,1)S(1)}, bf16[672,512]{1,0:T(8,128)(2,1)S(1)}, u32[]{:S(2)}, u32[]{:S(2)}) collective-permute-start(bf16[672,512]{1,0:T(8,128)(2,1)S(1)} %get-tuple-element.381), channel_id=1, source_target_pairs={{0,2},{2,0},{4,6},{6,4},{8,10},{10,8},{12,14},{14,12},{16,18},{18,... | collective-permute-start | bytes 2064392 | tf_op jit(solution)/shard_map/ppermute | solution.py:673
  54.6 17.3 %collective-permute-start.20 = (bf16[672,512]{1,0:T(8,128)(2,1)S(1)}, bf16[672,512]{1,0:T(8,128)(2,1)S(1)}, u32[]{:S(2)}, u32[]{:S(2)}) collective-permute-start(bf16[672,512]{1,0:T(8,128)(2,1)S(1)} %get-tuple-element.383), channel_id=1, source_target_pairs={{0,4},{2,6},{4,0},{6,2},{8,12},{10,14},{12,8},{14,10},{16,20},{18,... | collective-permute-start | bytes 2064392 | tf_op jit(solution)/shard_map/ppermute | solution.py:673
  56.1 15.8 %collective-permute-start.21 = (bf16[576,512]{1,0:T(8,128)(2,1)S(1)}, bf16[576,512]{1,0:T(8,128)(2,1)S(1)}, u32[]{:S(2)}, u32[]{:S(2)}) collective-permute-start(bf16[576,512]{1,0:T(8,128)(2,1)S(1)} %get-tuple-element.384), channel_id=1, source_target_pairs={{0,8},{2,10},{4,12},{6,14},{8,0},{10,2},{12,4},{14,6},{16,24},{18,... | collective-permute-start | bytes 1769480 | tf_op jit(solution)/shard_map/ppermute | solution.py:673
  56.6 13.5 %collective-permute-start.19 = (bf16[96,512]{1,0:T(8,128)(2,1)S(1)}, bf16[96,512]{1,0:T(8,128)(2,1)S(1)}, u32[]{:S(2)}, u32[]{:S(2)}) collective-permute-start(bf16[96,512]{1,0:T(8,128)(2,1)S(1)} %get-tuple-element.382), channel_id=1, source_target_pairs={{0,16},{2,18},{4,20},{6,22},{8,24},{10,26},{12,28},{14,30},{16,0},... | collective-permute-start | bytes 294920 | tf_op jit(solution)/shard_map/ppermute | solution.py:673
  66.8 5.2 %collective-permute-start.22 = (f32[9,768]{1,0:T(8,128)S(1)}, f32[9,768]{1,0:T(8,128)S(1)}, u32[]{:S(2)}, u32[]{:S(2)}) collective-permute-start(f32[9,768]{1,0:T(8,128)S(1)} %get-tuple-element.407.refs_19_), channel_id=1, source_target_pairs={{0,2},{2,0},{4,6},{6,4},{8,10},{10,8},{12,14},{14,12},{16,18},{18,... | collective-permute-start | bytes 82952 | tf_op jit(solution)/shard_map/ppermute | solution.py:673
  72.2 11.0 %collective-permute-start.24 = (bf16[336,512]{1,0:T(8,128)(2,1)S(1)}, bf16[336,512]{1,0:T(8,128)(2,1)S(1)}, u32[]{:S(2)}, u32[]{:S(2)}) collective-permute-start(bf16[336,512]{1,0:T(8,128)(2,1)S(1)} %get-tuple-element.415), channel_id=1, source_target_pairs={{0,8},{2,10},{4,12},{6,14},{8,0},{10,2},{12,4},{14,6},{16,24},{18,... | collective-permute-start | bytes 1032200 | tf_op jit(solution)/shard_map/ppermute | solution.py:673
  74.9 8.3 %collective-permute-start.23 = (bf16[288,512]{1,0:T(8,128)(2,1)S(1)}, bf16[288,512]{1,0:T(8,128)(2,1)S(1)}, u32[]{:S(2)}, u32[]{:S(2)}) collective-permute-start(bf16[288,512]{1,0:T(8,128)(2,1)S(1)} %get-tuple-element.414), channel_id=1, source_target_pairs={{0,4},{2,6},{4,0},{6,2},{8,12},{10,14},{12,8},{14,10},{16,20},{18,... | collective-permute-start | bytes 884744 | tf_op jit(solution)/shard_map/ppermute | solution.py:673
  75.4 7.8 %collective-permute-start.25 = (bf16[288,512]{1,0:T(8,128)(2,1)S(1)}, bf16[288,512]{1,0:T(8,128)(2,1)S(1)}, u32[]{:S(2)}, u32[]{:S(2)}) collective-permute-start(bf16[288,512]{1,0:T(8,128)(2,1)S(1)} %get-tuple-element.416), channel_id=1, source_target_pairs={{0,2},{2,0},{4,6},{6,4},{8,10},{10,8},{12,14},{14,12},{16,18},{18,... | collective-permute-start | bytes 884744 | tf_op jit(solution)/shard_map/ppermute | solution.py:673
  76.9 5.6 %collective-permute-start.26 = (bf16[96,512]{1,0:T(8,128)(2,1)S(1)}, bf16[96,512]{1,0:T(8,128)(2,1)S(1)}, u32[]{:S(2)}, u32[]{:S(2)}) collective-permute-start(bf16[96,512]{1,0:T(8,128)(2,1)S(1)} %get-tuple-element.417), channel_id=1, source_target_pairs={{0,16},{2,18},{4,20},{6,22},{8,24},{10,26},{12,28},{14,30},{16,0},... | collective-permute-start | bytes 294920 | tf_op jit(solution)/shard_map/ppermute | solution.py:673
  77.6 5.7 %collective-permute-start.27 = (f32[9,768]{1,0:T(8,128)S(1)}, f32[9,768]{1,0:T(8,128)S(1)}, u32[]{:S(2)}, u32[]{:S(2)}) collective-permute-start(f32[9,768]{1,0:T(8,128)S(1)} %get-tuple-element.435.refs_15_), channel_id=1, source_target_pairs={{0,4},{2,6},{4,0},{6,2},{8,12},{10,14},{12,8},{14,10},{16,20},{18,... | collective-permute-start | bytes 82952 | tf_op jit(solution)/shard_map/ppermute | solution.py:673
  83.4 9.6 %collective-permute-start.31 = (bf16[144,512]{1,0:T(8,128)(2,1)S(1)}, bf16[144,512]{1,0:T(8,128)(2,1)S(1)}, u32[]{:S(2)}, u32[]{:S(2)}) collective-permute-start(bf16[144,512]{1,0:T(8,128)(2,1)S(1)} %get-tuple-element.445), channel_id=1, source_target_pairs={{0,16},{2,18},{4,20},{6,22},{8,24},{10,26},{12,28},{14,30},{16,0},... | collective-permute-start | bytes 442376 | tf_op jit(solution)/shard_map/ppermute | solution.py:673
  85.6 7.4 %collective-permute-start.28 = (bf16[96,512]{1,0:T(8,128)(2,1)S(1)}, bf16[96,512]{1,0:T(8,128)(2,1)S(1)}, u32[]{:S(2)}, u32[]{:S(2)}) collective-permute-start(bf16[96,512]{1,0:T(8,128)(2,1)S(1)} %get-tuple-element.442), channel_id=1, source_target_pairs={{0,8},{2,10},{4,12},{6,14},{8,0},{10,2},{12,4},{14,6},{16,24},{18,... | collective-permute-start | bytes 294920 | tf_op jit(solution)/shard_map/ppermute | solution.py:673
  85.8 7.3 %collective-permute-start.29 = (bf16[96,512]{1,0:T(8,128)(2,1)S(1)}, bf16[96,512]{1,0:T(8,128)(2,1)S(1)}, u32[]{:S(2)}, u32[]{:S(2)}) collective-permute-start(bf16[96,512]{1,0:T(8,128)(2,1)S(1)} %get-tuple-element.443), channel_id=1, source_target_pairs={{0,2},{2,0},{4,6},{6,4},{8,10},{10,8},{12,14},{14,12},{16,18},{18,... | collective-permute-start | bytes 294920 | tf_op jit(solution)/shard_map/ppermute | solution.py:673
  87.7 5.4 %collective-permute-start.30 = (bf16[96,512]{1,0:T(8,128)(2,1)S(1)}, bf16[96,512]{1,0:T(8,128)(2,1)S(1)}, u32[]{:S(2)}, u32[]{:S(2)}) collective-permute-start(bf16[96,512]{1,0:T(8,128)(2,1)S(1)} %get-tuple-element.444), channel_id=1, source_target_pairs={{0,4},{2,6},{4,0},{6,2},{8,12},{10,14},{12,8},{14,10},{16,20},{18,... | collective-permute-start | bytes 294920 | tf_op jit(solution)/shard_map/ppermute | solution.py:673
  93.2 8.7 %collective-permute-start.33 = (bf16[144,512]{1,0:T(8,128)(2,1)S(1)}, bf16[144,512]{1,0:T(8,128)(2,1)S(1)}, u32[]{:S(2)}, u32[]{:S(2)}) collective-permute-start(bf16[144,512]{1,0:T(8,128)(2,1)S(1)} %get-tuple-element.468), channel_id=1, source_target_pairs={{0,16},{2,18},{4,20},{6,22},{8,24},{10,26},{12,28},{14,30},{16,0},... | collective-permute-start | bytes 442376 | tf_op jit(solution)/shard_map/ppermute | solution.py:673
  94.7 7.2 %collective-permute-start.34 = (f32[9,768]{1,0:T(8,128)S(1)}, f32[9,768]{1,0:T(8,128)S(1)}, u32[]{:S(2)}, u32[]{:S(2)}) collective-permute-start(f32[9,768]{1,0:T(8,128)S(1)} %get-tuple-element.469.refs_29_), channel_id=1, source_target_pairs={{0,16},{2,18},{4,20},{6,22},{8,24},{10,26},{12,28},{14,30},{16,0},... | collective-permute-start | bytes 82952 | tf_op jit(solution)/shard_map/ppermute | solution.py:673
  (15 other events, 58.8 us)

commit v3 on v2

--- a/solution.py
+++ b/solution.py
@@ -422,23 +422,28 @@
             outs[out][to : to + unit, :] = plan_sum(refs, plan, order, chosen, unit).astype(bf16)
 
 
-def finish_kernel(n_arrays, n_small, plans, *refs):
+def mlp_finish_kernel(n_arrays, plans, *refs):
     mine = my_bits()
     chosen = {bit: mine[bit] for bit in range(TOP_BITS)}
-    small, refs_out = refs[n_arrays : n_arrays + n_small], refs[n_arrays + n_small :]
-    fc2_ref, fc1_ref, qkv_ref, proj_ref, *outs = refs_out
+    outs = refs[n_arrays:]
+    for i, (part, order, unit, plan) in enumerate(plans):
+        total = plan_sum(refs, plan, order, chosen, unit)
+        outs[i // 3][:, part * UNIT_BLOCK : (part + 1) * UNIT_BLOCK] = total
+
+
+def attn_finish_kernel(n_arrays, n_small, plans, *refs):
+    mine = my_bits()
+    chosen = {bit: mine[bit] for bit in range(TOP_BITS)}
+    small, (qkv_ref, proj_ref, *outs) = (
+        refs[n_arrays : n_arrays + n_small],
+        refs[n_arrays + n_small :],
+    )
     local = qkv_ref.shape[2]
     third = local // 3
-    for i, (part, order, unit, plan) in enumerate(plans):
+    for part, order, unit, plan in plans:
         total = plan_sum(refs, plan, order, chosen, unit)
-        if i < 6:
-            (fc2_ref, fc1_ref)[i // 3][:, part * UNIT_BLOCK : (part + 1) * UNIT_BLOCK] = total
-        else:
-            qkv_ref[part] = total[:, :local]
-            proj_ref[:, part * third : (part + 1) * third] = total[:, local:]
-        if i == 5:
-            fc2_ref.leave()
-            fc1_ref.leave()
+        qkv_ref[part] = total[:, :local]
+        proj_ref[:, part * third : (part + 1) * third] = total[:, local:]
     total = sum(ref[...] for ref in small)
     width = total.shape[1]
     for i, out_ref in enumerate(outs[:-1]):
@@ -812,6 +817,7 @@
             w_router,
         ),
     )
+    grad_mlp_par = other_core(grad_mlp)
     w_fc1_late, bias_other, first, w_qkv_other, w_proj_other = tie(
         (w_fc1, bias_other, first, w_qkv_other, w_proj_other)
     )
@@ -841,8 +847,8 @@
             ln2_bias,
         ),
     )
-    second, grad_mlp = tie((second, grad_mlp))
-    grad_mlp_par = other_core(grad_mlp)
+    second, grad_mlp_par, w_fc2_late = tie((second, grad_mlp_par, w_fc2))
+    w_fc2_other = other_core(w_fc2_late)
 
     def hidden(w, bias):
         return call(
@@ -871,18 +877,15 @@
     act_par = other_core(act_other)
     bias_own, act_other = tie((bias_own, act_other))
     act, slope = hidden(w_fc1, bias_own)
-    w_fc2_late, act_par, grad_mlp_par, pack, slope = tie(
-        (w_fc2, act_par, grad_mlp_par, pack, slope)
-    )
-    w_fc2_other = other_core(w_fc2_late)
+    grad_pre, unit_own = hidden_back(w_fc2, slope)
+    slope_other, grad_pre = tie((slope_other, grad_pre))
+    grad_pre_other, unit_other = hidden_back(w_fc2_other, slope_other)
+    act, grad_pre, grad_pre_other, pack = tie((act, grad_pre, grad_pre_other, pack))
+    halves = mlp_weights(grad_mlp, grad_mlp_par, 0, act, act_par)
+    grad_pre_par = other_core(grad_pre_other)
     pack_par = other_core(pack)
-    grad_pre, unit_own = hidden_back(w_fc2, slope)
-    act, grad_pre = tie((act, grad_pre))
-    halves = mlp_weights(grad_mlp, grad_mlp_par, 0, act, act_par)
-    halves, slope_other = tie((halves, slope_other))
+    halves, grad_pre_other = tie((halves, grad_pre_other))
     fc2_sums = begin(halves, count, FC2_EARLY)
-    grad_pre_other, unit_other = hidden_back(w_fc2_other, slope_other)
-    grad_pre_par = other_core(grad_pre_other)
     grad_attn, grad_hidden, back_sums = call(
         back_kernel,
         [shape((rows, width), bf16), shape((rows, width), f32), shape((8, width), f32)],
@@ -987,23 +990,32 @@
         (*fc2_sums, *fc1_sums, *attn_sums), count, input_grad, (small, got)
     )
     got = swap(small, 1, count)
-    input_grad = arrived(fc2_sums, input_grad)
     input_grad, small = exchange((*fc1_sums, *attn_sums), count, input_grad, (small, got))
+    small = arrived(fc2_sums, small)
     got = swap(small, 2, count)
-    input_grad = arrived(fc1_sums, input_grad)
     input_grad, small = exchange(attn_sums, count, input_grad, (small, got))
     for low in range(top):
         small = small + lax.ppermute(small, "dp", partners(count, low))
     got = swap(small, 3, count)
-    sums = (*fc2_sums, *fc1_sums, *attn_sums)
-    arrays, plans = listed(sums)
-    plans = [(stream.part, stream.order, stream.unit, plan) for stream, plan in zip(sums, plans)]
     unit = width // UNITS
-    fc2_turned, fc1_grad, qkv_grad, proj_turned, *sums = call(
-        functools.partial(finish_kernel, len(arrays), 2, plans),
+
+    def final(streams):
+        arrays, plans = listed(streams)
+        return arrays, [
+            (stream.part, stream.order, stream.unit, plan) for stream, plan in zip(streams, plans)
+        ]
+
+    arrays, plans = final((*fc2_sums, *fc1_sums))
+    fc2_turned, fc1_grad = call(
+        functools.partial(mlp_finish_kernel, len(arrays), plans),
+        [Far(shape((unit, units), f32)), Far(shape((unit, units), f32))],
+        tuple(arrays),
+    )
+    small, fc2_turned, fc1_grad = tie((small, fc2_turned, fc1_grad))
+    arrays, plans = final(attn_sums)
+    qkv_grad, proj_turned, *sums = call(
+        functools.partial(attn_finish_kernel, len(arrays), 2, plans),
         [
-            Far(shape((unit, units), f32)),
-            Far(shape((unit, units), f32)),
             Far(shape((3, unit, local), f32)),
             Far(shape((unit, local), f32)),
             *[Far(shape((width,), f32))] * 7,

time: 103 us -> 100 us (0.971)
  waiting for transfers between devices: 31.4 us -> 27.5 us
    ppermute x23, waiting for transfers between devices: 26.8 us -> 24.7 us  [swap(): lax.ppermute(value, 'dp', partners(count, bit + count.bit_length() - 1 -...]
    ppermute x12, waiting for transfers between devices: 4.57 us -> 2.76 us  [other_core(): return lax.ppermute(value, 'head', [(0, 1), (1, 0)])]
    pallas_call x22 -> x23, Pallas kernels: 36.5 us -> 37.3 us  [call(): pl.pallas_call(body, out_shape=[(pltpu.HBM if i in far_out else pltpu.VME...]
  transfers between devices with their start and end apart: 35 -> 35, of which waited for: 17 -> 16; matrix products, arithmetic and copies ran while one was open for 0% -> 0% of each run, Pallas kernels for 32% -> 36%
where the time goes in v3:
time: 100 us
  Pallas kernels  37.3 us (37%)
  starting transfers between devices  34.2 us (34%)
  waiting for transfers between devices  27.5 us (28%)
  between operations  1.12 us (1%)
    pallas_call x23, Pallas kernels, call(): pl.pallas_call(body, out_shape=[(pltpu.HBM if i in far_out else pltpu.VME...  37.3 us
    ppermute x23, starting transfers between devices, swap(): lax.ppermute(value, 'dp', partners(count, bit + count.bit_length() - 1 -...  31.2 us
    ppermute x23, waiting for transfers between devices, swap(): lax.ppermute(value, 'dp', partners(count, bit + count.bit_length() - 1 -...  24.7 us
    ppermute x12, starting transfers between devices, other_core(): return lax.ppermute(value, 'head', [(0, 1), (1, 0)])  3 us
    ppermute x12, waiting for transfers between devices, other_core(): return lax.ppermute(value, 'head', [(0, 1), (1, 0)])  2.76 us
  transfers between devices with their start and end apart: 35, of which 16 were waited for; matrix products, arithmetic and copies ran while one was open for 0% of the time, Pallas kernels for 36%

profile of v3, /device:TPU:0, one launch (start us, length us, event | category | flops | bytes accessed | tf_op | source)
XLA Modules:
  0.0 100.1 jit_solution(3278831107455314947)
XLA Ops:
  1.3 2.7 %shard_map.263 = (s32[8,128]{1,0:T(8,128)S(1)}, s32[8,128]{1,0:T(8,128)S(1)}, bf16[336,768]{1,0:T(8,128)(2,1)S(1)}, bf16[336,768]{1,0:T(8,128)(2,1)S(1)}, bf16[3...) custom-call(s32[3,98]{1,0:T(4,128)} %refs_0_.1, ...), custom_call_target="tpu_custom_call" | custom-call | flops 1 | bytes 1 | tf_op jit(solution)/shard_map/pallas_call | solution.py:144
  6.6 4.0 %shard_map.264 = (bf16[336,1152]{1,0:T(8,128)(2,1)S(1)}, bf16[336,1152]{1,0:T(8,128)(2,1)S(1)}, bf16[336,384]{1,0:T(8,128)(2,1)S(1)}, bf16[336,384]{1,0:T(8,128)...) custom-call(s32[8,128]{1,0:T(8,128)S(1)} %get-tuple-element.254.refs_0_, ...), custom_call_target="tpu_custom_call" | custom-call | flops 1 | bytes 1 | tf_op jit(solution)/shard_map/pallas_call | solution.py:144
  17.0 2.5 %shard_map.269 = (bf16[384,512]{1,0:T(8,128)(2,1)S(1)}, bf16[384,512]{1,0:T(8,128)(2,1)S(1)}, bf16[384,512]{1,0:T(8,128)(2,1)S(1)}, f32[384,512]{1,0:T(8,128)S(1...) custom-call(bf16[336,768]{1,0:T(8,128)(2,1)S(1)} %get-tuple-element.253.refs_0_, ...), custom_call_target="tpu_custom_call" | custom-call | flops 1 | bytes 1 | tf_op jit(solution)/shard_map/pallas_call | solution.py:144
  19.4 2.7 %collective-permute-start.7 = (bf16[384,512]{1,0:T(8,128)(2,1)S(1)}, bf16[384,512]{1,0:T(8,128)(2,1)S(1)}, u32[]{:S(2)}, u32[]{:S(2)}) collective-permute-start(bf16[384,512]{1,0:T(8,128)(2,1)S(1)} %get-tuple-element.296), channel_id=1, source_target_pairs={{0,2},{2,0},{4,6},{6,4},{8,10},{10,8},{12,14},{14,12},{16,18},{18,... | collective-permute-start | bytes 1179656 | tf_op jit(solution)/shard_map/ppermute | solution.py:678
  25.2 2.5 %shard_map.270 = (bf16[336,768]{1,0:T(8,128)(2,1)S(1)}, f32[336,768]{1,0:T(8,128)S(1)}, f32[8,768]{1,0:T(8,128)S(1)}) custom-call(bf16[336,1536]{1,0:T(8,128)(2,1)S(1)} %get-tuple-element.288.refs_0_, bf16[768,1536]{1,0:T(8,128)(2,1)S(1)} %collective-permute-done.4.refs_1_, bf16[336,1536]{1,0:T(8,128)(2,1)S(1)} %get-tuple-element.303.refs_2_, ...), custom_call_target="tpu_custom_call" | custom-call | flops 1 | bytes 1 | tf_op jit(solution)/shard_map/pallas_call | solution.py:144
  27.8 2.5 %shard_map.271 = (bf16[384,512]{1,0:T(8,128)(2,1)S(1)}, bf16[384,512]{1,0:T(8,128)(2,1)S(1)}, bf16[384,512]{1,0:T(8,128)(2,1)S(1)}, f32[384,512]{1,0:T(8,128)S(1...) custom-call(bf16[336,768]{1,0:T(8,128)(2,1)S(1)} %get-tuple-element.265.refs_0_, ...), custom_call_target="tpu_custom_call" | custom-call | flops 1 | bytes 1 | tf_op jit(solution)/shard_map/pallas_call | solution.py:144
  30.3 1.8 %shard_map.272.refs_7_ = bf16[336,1152]{1,0:T(8,128)(2,1)S(1)} custom-call(s32[8,128]{1,0:T(8,128)S(1)} %get-tuple-element.254.refs_0_, bf16[336,768]{1,0:T(8,128)(2,1)S(1)} %get-tuple-element.336.refs_1_.refs_2_, bf16[384,768]{1,0:T(8,128)(2,1)S(1)} %collective-permute-done.2.refs_5_.refs_2_, bf16[336,1152]{1,0:T(8,128)(2,1)S(1)} %get-tuple-element.315.refs_3_), custom_call_target="tpu_custom_call" | custom-call | flops 1 | bytes 1 | tf_op jit(solution)/shard_map/pallas_call | solution.py:144
  37.4 1.8 %shard_map.274.refs_4_.refs_6_ = bf16[336,1152]{1,0:T(8,128)(2,1)S(1)} custom-call(s32[8,128]{1,0:T(8,128)S(1)} %get-tuple-element.254.refs_0_, bf16[336,768]{1,0:T(8,128)(2,1)S(1)} %get-tuple-element.336.refs_1_.refs_2_, bf16[384,768]{1,0:T(8,128)(2,1)S(1)} %get-tuple-element.258.refs_4_.refs_2_, bf16[336,1152]{1,0:T(8,128)(2,1)S(1)} %get-tuple-element.337.refs_3_), custom_call_target="tpu_custom_call" | custom-call | flops 1 | bytes 1 | tf_op jit(solution)/shard_map/pallas_call | solution.py:144
  39.3 3.7 %shard_map.275 = (bf16[384,512]{1,0:T(8,128)(2,1)S(1)}, bf16[384,512]{1,0:T(8,128)(2,1)S(1)}, bf16[384,512]{1,0:T(8,128)(2,1)S(1)}, f32[384,512]{1,0:T(8,128)S(1...) custom-call(bf16[336,768]{1,0:T(8,128)(2,1)S(1)} %get-tuple-element.256.refs_1_.refs_0_, ...), custom_call_target="tpu_custom_call" | custom-call | flops 1 | bytes 1 | tf_op jit(solution)/shard_map/pallas_call | solution.py:144
  43.0 7.5 %collective-permute-done.12.refs_2_.refs_5_ = bf16[576,512]{1,0:T(8,128)(2,1)S(1)} collective-permute-done((bf16[576,512]{1,0:T(8,128)(2,1)S(1)}, bf16[576,512]{1,0:T(8,128)(2,1)S(1)}, u32[]{:S(2)}, u32[]{:S(2)}) %collective-permute-start.12) | collective-permute-done | bytes 589856 | tf_op jit(solution)/shard_map/ppermute | solution.py:678
  54.9 2.6 %collective-permute-start.19 = (bf16[96,512]{1,0:T(8,128)(2,1)S(1)}, bf16[96,512]{1,0:T(8,128)(2,1)S(1)}, u32[]{:S(2)}, u32[]{:S(2)}) collective-permute-start(bf16[96,512]{1,0:T(8,128)(2,1)S(1)} %get-tuple-element.383), channel_id=1, source_target_pairs={{0,16},{2,18},{4,20},{6,22},{8,24},{10,26},{12,28},{14,30},{16,0},... | collective-permute-start | bytes 294920 | tf_op jit(solution)/shard_map/ppermute | solution.py:678
  57.4 2.1 %shard_map.277 = (f32[336,768]{1,0:T(8,128)S(1)}, f32[336,1]{1,0:T(8,128)S(1)}, f32[1,768]{1,0:T(1,128)S(1)}) custom-call(bf16[336,768]{1,0:T(8,128)(2,1)S(1)} %get-tuple-element.252.refs_6_.refs_4_.refs_0_.refs_3_, bf16[336,768]{1,0:T(8,128)(2,1)S(1)} %get-tuple-element.291.refs_6_.refs_1_, f32[336,1]{1,0:T(8,128)S(1)} %get-tuple-element.294.refs_2_, ...), custom_call_target="tpu_custom_call" | custom-call | flops 1 | bytes 1 | tf_op jit(solution)/shard_map/pallas_call | solution.py:144
  59.5 2.6 %shard_map.278 = (f32[336,768]{1,0:T(8,128)S(1)}, f32[9,768]{1,0:T(8,128)S(1)}, f32[9,768]{1,0:T(8,128)S(1)}) custom-call(bf16[3,768,384]{2,1,0:T(8,128)(2,1)S(1)} %get-tuple-element.249.refs_2_.refs_0_, f32[768]{0:T(1024)S(1)} %get-tuple-element.250.refs_1_, f32[768]{0:T(1024)S(1)} %get-tuple-element.251.refs_2_, ...), custom_call_target="tpu_custom_call" | custom-call | flops 1 | bytes 1 | tf_op jit(solution)/shard_map/pallas_call | solution.py:144
  63.5 1.6 %shard_map.279 = (bf16[3,197,768]{2,1,0:T(8,128)(2,1)}, f32[9,768]{1,0:T(8,128)S(1)}) custom-call(s32[8,128]{1,0:T(8,128)S(1)} %get-tuple-element.373.refs_0_, bf16[3,197,768]{2,1,0:T(8,128)(2,1)S(1)} %copy-done.2, f32[336,768]{1,0:T(8,128)S(1)} %get-tuple-element.376.refs_2_, f32[9,768]{1,0:T(8,128)S(1)} %get-tuple-element.377.refs_3_, ...), custom_call_target="tpu_custom_call" | custom-call | flops 1 | bytes 1 | tf_op jit(solution)/shard_map/pallas_call | solution.py:144
  68.3 1.9 %collective-permute-done.21.refs_14_.refs_6_.refs_9_.refs_18_.refs_10_ = bf16[576,512]{1,0:T(8,128)(2,1)S(1)} collective-permute-done((bf16[576,512]{1,0:T(8,128)(2,1)S(1)}, bf16[576,512]{1,0:T(8,128)(2,1)S(1)}, u32[]{:S(2)}, u32[]{:S(2)}) %collective-permute-start.21) | collective-permute-done | bytes 589856 | tf_op jit(solution)/shard_map/ppermute | solution.py:678
  70.5 2.7 %collective-permute-start.24 = (bf16[336,512]{1,0:T(8,128)(2,1)S(1)}, bf16[336,512]{1,0:T(8,128)(2,1)S(1)}, u32[]{:S(2)}, u32[]{:S(2)}) collective-permute-start(bf16[336,512]{1,0:T(8,128)(2,1)S(1)} %get-tuple-element.416), channel_id=1, source_target_pairs={{0,8},{2,10},{4,12},{6,14},{8,0},{10,2},{12,4},{14,6},{16,24},{18,... | collective-permute-start | bytes 1032200 | tf_op jit(solution)/shard_map/ppermute | solution.py:678
  75.2 1.7 %collective-permute-start.26 = (f32[9,768]{1,0:T(8,128)S(1)}, f32[9,768]{1,0:T(8,128)S(1)}, u32[]{:S(2)}, u32[]{:S(2)}) collective-permute-start(f32[9,768]{1,0:T(8,128)S(1)} %get-tuple-element.434.refs_15_), channel_id=1, source_target_pairs={{0,4},{2,6},{4,0},{6,2},{8,12},{10,14},{12,8},{14,10},{16,20},{18,... | collective-permute-start | bytes 82952 | tf_op jit(solution)/shard_map/ppermute | solution.py:678
  77.3 2.6 %collective-permute-done.23.refs_11_.refs_2_.refs_21_ = bf16[288,512]{1,0:T(8,128)(2,1)S(1)} collective-permute-done((bf16[288,512]{1,0:T(8,128)(2,1)S(1)}, bf16[288,512]{1,0:T(8,128)(2,1)S(1)}, u32[]{:S(2)}, u32[]{:S(2)}) %collective-permute-start.23) | collective-permute-done | bytes 294944 | tf_op jit(solution)/shard_map/ppermute | solution.py:678
  82.0 2.2 %collective-permute-start.28 = (bf16[96,512]{1,0:T(8,128)(2,1)S(1)}, bf16[96,512]{1,0:T(8,128)(2,1)S(1)}, u32[]{:S(2)}, u32[]{:S(2)}) collective-permute-start(bf16[96,512]{1,0:T(8,128)(2,1)S(1)} %get-tuple-element.442), channel_id=1, source_target_pairs={{0,2},{2,0},{4,6},{6,4},{8,10},{10,8},{12,14},{14,12},{16,18},{18,... | collective-permute-start | bytes 294920 | tf_op jit(solution)/shard_map/ppermute | solution.py:678
  84.7 1.9 %collective-permute-start.31 = (f32[9,768]{1,0:T(8,128)S(1)}, f32[9,768]{1,0:T(8,128)S(1)}, u32[]{:S(2)}, u32[]{:S(2)}) collective-permute-start(f32[9,768]{1,0:T(8,128)S(1)} %get-tuple-element.459.refs_12_), channel_id=1, source_target_pairs={{0,8},{2,10},{4,12},{6,14},{8,0},{10,2},{12,4},{14,6},{16,24},{18,... | collective-permute-start | bytes 82952 | tf_op jit(solution)/shard_map/ppermute | solution.py:678
  86.9 1.9 %collective-permute-done.29.refs_11_.refs_12_ = bf16[96,512]{1,0:T(8,128)(2,1)S(1)} collective-permute-done((bf16[96,512]{1,0:T(8,128)(2,1)S(1)}, bf16[96,512]{1,0:T(8,128)(2,1)S(1)}, u32[]{:S(2)}, u32[]{:S(2)}) %collective-permute-start.29) | collective-permute-done | bytes 98336 | tf_op jit(solution)/shard_map/ppermute | solution.py:678
  88.9 2.2 %collective-permute-start.32 = (bf16[144,512]{1,0:T(8,128)(2,1)S(1)}, bf16[144,512]{1,0:T(8,128)(2,1)S(1)}, u32[]{:S(2)}, u32[]{:S(2)}) collective-permute-start(bf16[144,512]{1,0:T(8,128)(2,1)S(1)} %get-tuple-element.464), channel_id=1, source_target_pairs={{0,16},{2,18},{4,20},{6,22},{8,24},{10,26},{12,28},{14,30},{16,0},... | collective-permute-start | bytes 442376 | tf_op jit(solution)/shard_map/ppermute | solution.py:678
  91.9 2.9 %collective-permute-done.33.refs_16_ = bf16[144,512]{1,0:T(8,128)(2,1)S(1)} collective-permute-done((bf16[144,512]{1,0:T(8,128)(2,1)S(1)}, bf16[144,512]{1,0:T(8,128)(2,1)S(1)}, u32[]{:S(2)}, u32[]{:S(2)}) %collective-permute-start.33) | collective-permute-done | bytes 147488 | tf_op jit(solution)/shard_map/ppermute | solution.py:678
  95.8 3.3 %collective-permute-done.34.refs_14_ = f32[9,768]{1,0:T(8,128)S(1)} collective-permute-done((f32[9,768]{1,0:T(8,128)S(1)}, f32[9,768]{1,0:T(8,128)S(1)}, u32[]{:S(2)}, u32[]{:S(2)}) %collective-permute-start.34) | collective-permute-done | bytes 27680 | tf_op jit(solution)/shard_map/ppermute | solution.py:678
  (79 shorter events, 35.1 us)
Async XLA Ops:
  0.7 5.4 %collective-permute-start.1 = (bf16[3,768,384]{2,1,0:T(8,128)(2,1)}, bf16[3,768,384]{2,1,0:T(8,128)(2,1)S(1)}, u32[]{:S(2)}, u32[]{:S(2)}) collective-permute-start(bf16[3,768,384]{2,1,0:T(8,128)(2,1)} %refs_7_.2), channel_id=1, source_target_pairs={{0,1},{1,0},{2,3},{3,2},{4,5},{5,4},{6,7},{7,6},{8,9},{9,8},{10,11... | collective-permute-start | bytes 5308424 | tf_op jit(solution)/shard_map/ppermute | solution.py:670
  4.0 6.5 %collective-permute-start.3 = (bf16[336,768]{1,0:T(8,128)(2,1)S(1)}, bf16[336,768]{1,0:T(8,128)(2,1)S(1)}, u32[]{:S(2)}, u32[]{:S(2)}) collective-permute-start(bf16[336,768]{1,0:T(8,128)(2,1)S(1)} %get-tuple-element.253.refs_0_), channel_id=1, source_target_pairs={{0,1},{1,0},{2,3},{3,2},{4,5},{5,4},{6,7},{7,6},{8,9},{9,8},{10,11... | collective-permute-start | bytes 1548296 | tf_op jit(solution)/shard_map/ppermute | solution.py:670
  16.4 11.4 %collective-permute-start.10 = (bf16[336,1920]{1,0:T(8,128)(2,1)S(1)}, bf16[336,1920]{1,0:T(8,128)(2,1)S(1)}, u32[]{:S(2)}, u32[]{:S(2)}) collective-permute-start(bf16[336,1920]{1,0:T(8,128)(2,1)S(1)} %get-tuple-element.301), channel_id=1, source_target_pairs={{0,1},{1,0},{2,3},{3,2},{4,5},{5,4},{6,7},{7,6},{8,9},{9,8},{10,11... | collective-permute-start | bytes 3870728 | tf_op jit(solution)/shard_map/ppermute | solution.py:670
  16.6 11.1 %collective-permute-start.11 = (bf16[336,1536]{1,0:T(8,128)(2,1)S(1)}, bf16[336,1536]{1,0:T(8,128)(2,1)S(1)}, u32[]{:S(2)}, u32[]{:S(2)}) collective-permute-start(bf16[336,1536]{1,0:T(8,128)(2,1)S(1)} %get-tuple-element.288.refs_0_), channel_id=1, source_target_pairs={{0,1},{1,0},{2,3},{3,2},{4,5},{5,4},{6,7},{7,6},{8,9},{9,8},{10,11... | collective-permute-start | bytes 3096584 | tf_op jit(solution)/shard_map/ppermute | solution.py:670
  19.4 12.7 %collective-permute-start.7 = (bf16[384,512]{1,0:T(8,128)(2,1)S(1)}, bf16[384,512]{1,0:T(8,128)(2,1)S(1)}, u32[]{:S(2)}, u32[]{:S(2)}) collective-permute-start(bf16[384,512]{1,0:T(8,128)(2,1)S(1)} %get-tuple-element.296), channel_id=1, source_target_pairs={{0,2},{2,0},{4,6},{6,4},{8,10},{10,8},{12,14},{14,12},{16,18},{18,... | collective-permute-start | bytes 1179656 | tf_op jit(solution)/shard_map/ppermute | solution.py:678
  22.1 11.1 %collective-permute-start.8 = (bf16[384,512]{1,0:T(8,128)(2,1)S(1)}, bf16[384,512]{1,0:T(8,128)(2,1)S(1)}, u32[]{:S(2)}, u32[]{:S(2)}) collective-permute-start(bf16[384,512]{1,0:T(8,128)(2,1)S(1)} %get-tuple-element.298), channel_id=1, source_target_pairs={{0,4},{2,6},{4,0},{6,2},{8,12},{10,14},{12,8},{14,10},{16,20},{18,... | collective-permute-start | bytes 1179656 | tf_op jit(solution)/shard_map/ppermute | solution.py:678
  23.6 10.8 %collective-permute-start.9 = (bf16[384,512]{1,0:T(8,128)(2,1)S(1)}, bf16[384,512]{1,0:T(8,128)(2,1)S(1)}, u32[]{:S(2)}, u32[]{:S(2)}) collective-permute-start(bf16[384,512]{1,0:T(8,128)(2,1)S(1)} %get-tuple-element.300), channel_id=1, source_target_pairs={{0,8},{2,10},{4,12},{6,14},{8,0},{10,2},{12,4},{14,6},{16,24},{18,... | collective-permute-start | bytes 1179656 | tf_op jit(solution)/shard_map/ppermute | solution.py:678
  34.7 15.7 %collective-permute-start.12 = (bf16[576,512]{1,0:T(8,128)(2,1)S(1)}, bf16[576,512]{1,0:T(8,128)(2,1)S(1)}, u32[]{:S(2)}, u32[]{:S(2)}) collective-permute-start(bf16[576,512]{1,0:T(8,128)(2,1)S(1)} %get-tuple-element.330), channel_id=1, source_target_pairs={{0,4},{2,6},{4,0},{6,2},{8,12},{10,14},{12,8},{14,10},{16,20},{18,... | collective-permute-start | bytes 1769480 | tf_op jit(solution)/shard_map/ppermute | solution.py:678
  35.3 15.4 %collective-permute-start.13 = (bf16[576,512]{1,0:T(8,128)(2,1)S(1)}, bf16[576,512]{1,0:T(8,128)(2,1)S(1)}, u32[]{:S(2)}, u32[]{:S(2)}) collective-permute-start(bf16[576,512]{1,0:T(8,128)(2,1)S(1)} %get-tuple-element.331), channel_id=1, source_target_pairs={{0,8},{2,10},{4,12},{6,14},{8,0},{10,2},{12,4},{14,6},{16,24},{18,... | collective-permute-start | bytes 1769480 | tf_op jit(solution)/shard_map/ppermute | solution.py:678
  36.9 15.1 %collective-permute-start.14 = (bf16[576,512]{1,0:T(8,128)(2,1)S(1)}, bf16[576,512]{1,0:T(8,128)(2,1)S(1)}, u32[]{:S(2)}, u32[]{:S(2)}) collective-permute-start(bf16[576,512]{1,0:T(8,128)(2,1)S(1)} %get-tuple-element.332), channel_id=1, source_target_pairs={{0,2},{2,0},{4,6},{6,4},{8,10},{10,8},{12,14},{14,12},{16,18},{18,... | collective-permute-start | bytes 1769480 | tf_op jit(solution)/shard_map/ppermute | solution.py:678
  52.3 17.9 %collective-permute-start.18 = (bf16[672,512]{1,0:T(8,128)(2,1)S(1)}, bf16[672,512]{1,0:T(8,128)(2,1)S(1)}, u32[]{:S(2)}, u32[]{:S(2)}) collective-permute-start(bf16[672,512]{1,0:T(8,128)(2,1)S(1)} %get-tuple-element.382), channel_id=1, source_target_pairs={{0,2},{2,0},{4,6},{6,4},{8,10},{10,8},{12,14},{14,12},{16,18},{18,... | collective-permute-start | bytes 2064392 | tf_op jit(solution)/shard_map/ppermute | solution.py:678
  52.9 17.3 %collective-permute-start.20 = (bf16[672,512]{1,0:T(8,128)(2,1)S(1)}, bf16[672,512]{1,0:T(8,128)(2,1)S(1)}, u32[]{:S(2)}, u32[]{:S(2)}) collective-permute-start(bf16[672,512]{1,0:T(8,128)(2,1)S(1)} %get-tuple-element.384), channel_id=1, source_target_pairs={{0,4},{2,6},{4,0},{6,2},{8,12},{10,14},{12,8},{14,10},{16,20},{18,... | collective-permute-start | bytes 2064392 | tf_op jit(solution)/shard_map/ppermute | solution.py:678
  54.4 15.8 %collective-permute-start.21 = (bf16[576,512]{1,0:T(8,128)(2,1)S(1)}, bf16[576,512]{1,0:T(8,128)(2,1)S(1)}, u32[]{:S(2)}, u32[]{:S(2)}) collective-permute-start(bf16[576,512]{1,0:T(8,128)(2,1)S(1)} %get-tuple-element.385), channel_id=1, source_target_pairs={{0,8},{2,10},{4,12},{6,14},{8,0},{10,2},{12,4},{14,6},{16,24},{18,... | collective-permute-start | bytes 1769480 | tf_op jit(solution)/shard_map/ppermute | solution.py:678
  54.9 13.5 %collective-permute-start.19 = (bf16[96,512]{1,0:T(8,128)(2,1)S(1)}, bf16[96,512]{1,0:T(8,128)(2,1)S(1)}, u32[]{:S(2)}, u32[]{:S(2)}) collective-permute-start(bf16[96,512]{1,0:T(8,128)(2,1)S(1)} %get-tuple-element.383), channel_id=1, source_target_pairs={{0,16},{2,18},{4,20},{6,22},{8,24},{10,26},{12,28},{14,30},{16,0},... | collective-permute-start | bytes 294920 | tf_op jit(solution)/shard_map/ppermute | solution.py:678
  65.1 5.1 %collective-permute-start.22 = (f32[9,768]{1,0:T(8,128)S(1)}, f32[9,768]{1,0:T(8,128)S(1)}, u32[]{:S(2)}, u32[]{:S(2)}) collective-permute-start(f32[9,768]{1,0:T(8,128)S(1)} %get-tuple-element.408.refs_19_), channel_id=1, source_target_pairs={{0,2},{2,0},{4,6},{6,4},{8,10},{10,8},{12,14},{14,12},{16,18},{18,... | collective-permute-start | bytes 82952 | tf_op jit(solution)/shard_map/ppermute | solution.py:678
  70.5 10.0 %collective-permute-start.24 = (bf16[336,512]{1,0:T(8,128)(2,1)S(1)}, bf16[336,512]{1,0:T(8,128)(2,1)S(1)}, u32[]{:S(2)}, u32[]{:S(2)}) collective-permute-start(bf16[336,512]{1,0:T(8,128)(2,1)S(1)} %get-tuple-element.416), channel_id=1, source_target_pairs={{0,8},{2,10},{4,12},{6,14},{8,0},{10,2},{12,4},{14,6},{16,24},{18,... | collective-permute-start | bytes 1032200 | tf_op jit(solution)/shard_map/ppermute | solution.py:678
  73.2 6.7 %collective-permute-start.23 = (bf16[288,512]{1,0:T(8,128)(2,1)S(1)}, bf16[288,512]{1,0:T(8,128)(2,1)S(1)}, u32[]{:S(2)}, u32[]{:S(2)}) collective-permute-start(bf16[288,512]{1,0:T(8,128)(2,1)S(1)} %get-tuple-element.415), channel_id=1, source_target_pairs={{0,4},{2,6},{4,0},{6,2},{8,12},{10,14},{12,8},{14,10},{16,20},{18,... | collective-permute-start | bytes 884744 | tf_op jit(solution)/shard_map/ppermute | solution.py:678
  73.7 6.7 %collective-permute-start.25 = (bf16[288,512]{1,0:T(8,128)(2,1)S(1)}, bf16[288,512]{1,0:T(8,128)(2,1)S(1)}, u32[]{:S(2)}, u32[]{:S(2)}) collective-permute-start(bf16[288,512]{1,0:T(8,128)(2,1)S(1)} %get-tuple-element.417), channel_id=1, source_target_pairs={{0,2},{2,0},{4,6},{6,4},{8,10},{10,8},{12,14},{14,12},{16,18},{18,... | collective-permute-start | bytes 884744 | tf_op jit(solution)/shard_map/ppermute | solution.py:678
  75.2 5.3 %collective-permute-start.26 = (f32[9,768]{1,0:T(8,128)S(1)}, f32[9,768]{1,0:T(8,128)S(1)}, u32[]{:S(2)}, u32[]{:S(2)}) collective-permute-start(f32[9,768]{1,0:T(8,128)S(1)} %get-tuple-element.434.refs_15_), channel_id=1, source_target_pairs={{0,4},{2,6},{4,0},{6,2},{8,12},{10,14},{12,8},{14,10},{16,20},{18,... | collective-permute-start | bytes 82952 | tf_op jit(solution)/shard_map/ppermute | solution.py:678
  76.9 7.8 %collective-permute-start.30 = (bf16[96,512]{1,0:T(8,128)(2,1)S(1)}, bf16[96,512]{1,0:T(8,128)(2,1)S(1)}, u32[]{:S(2)}, u32[]{:S(2)}) collective-permute-start(bf16[96,512]{1,0:T(8,128)(2,1)S(1)} %get-tuple-element.457), channel_id=1, source_target_pairs={{0,16},{2,18},{4,20},{6,22},{8,24},{10,26},{12,28},{14,30},{16,0},... | collective-permute-start | bytes 294920 | tf_op jit(solution)/shard_map/ppermute | solution.py:678
  80.7 6.3 %collective-permute-start.27 = (bf16[96,512]{1,0:T(8,128)(2,1)S(1)}, bf16[96,512]{1,0:T(8,128)(2,1)S(1)}, u32[]{:S(2)}, u32[]{:S(2)}) collective-permute-start(bf16[96,512]{1,0:T(8,128)(2,1)S(1)} %get-tuple-element.441), channel_id=1, source_target_pairs={{0,8},{2,10},{4,12},{6,14},{8,0},{10,2},{12,4},{14,6},{16,24},{18,... | collective-permute-start | bytes 294920 | tf_op jit(solution)/shard_map/ppermute | solution.py:678
  86.6 8.2 %collective-permute-start.33 = (bf16[144,512]{1,0:T(8,128)(2,1)S(1)}, bf16[144,512]{1,0:T(8,128)(2,1)S(1)}, u32[]{:S(2)}, u32[]{:S(2)}) collective-permute-start(bf16[144,512]{1,0:T(8,128)(2,1)S(1)} %get-tuple-element.468), channel_id=1, source_target_pairs={{0,16},{2,18},{4,20},{6,22},{8,24},{10,26},{12,28},{14,30},{16,0},... | collective-permute-start | bytes 442376 | tf_op jit(solution)/shard_map/ppermute | solution.py:678
  88.9 10.1 %collective-permute-start.32 = (bf16[144,512]{1,0:T(8,128)(2,1)S(1)}, bf16[144,512]{1,0:T(8,128)(2,1)S(1)}, u32[]{:S(2)}, u32[]{:S(2)}) collective-permute-start(bf16[144,512]{1,0:T(8,128)(2,1)S(1)} %get-tuple-element.464), channel_id=1, source_target_pairs={{0,16},{2,18},{4,20},{6,22},{8,24},{10,26},{12,28},{14,30},{16,0},... | collective-permute-start | bytes 442376 | tf_op jit(solution)/shard_map/ppermute | solution.py:678
  91.1 8.0 %collective-permute-start.34 = (f32[9,768]{1,0:T(8,128)S(1)}, f32[9,768]{1,0:T(8,128)S(1)}, u32[]{:S(2)}, u32[]{:S(2)}) collective-permute-start(f32[9,768]{1,0:T(8,128)S(1)} %get-tuple-element.471.refs_13_), channel_id=1, source_target_pairs={{0,16},{2,18},{4,20},{6,22},{8,24},{10,26},{12,28},{14,30},{16,0},... | collective-permute-start | bytes 82952 | tf_op jit(solution)/shard_map/ppermute | solution.py:678
  (16 other events, 63.9 us)

commit v4 on v3

--- a/solution.py
+++ b/solution.py
@@ -321,7 +321,7 @@
 
 
 TOP_BITS = 4
-FC2_EARLY, FC1_EARLY, ATTN_EARLY = 1, 0, 0
+FC2_EARLY, FC1_EARLY, ATTN_EARLY = 0, 0, 0
 UNITS = 1 << TOP_BITS
 
 
@@ -331,7 +331,7 @@
 
 
 def order_of(part, early=0):
-    order = [(part + j) % 3 for j in range(3)] + [3]
+    order = [(part - j) % 3 for j in range(3)] + [3]
     return order[:2] + [3, order[2]] if part < early else order
 
 

time: 100 us -> 99.3 us (level)
  starting transfers between devices: 34.2 us -> 28.6 us
  waiting for transfers between devices: 27.5 us -> 32.1 us
    ppermute x23 -> x22, starting transfers between devices: 31.2 us -> 25.6 us  [swap(): lax.ppermute(value, 'dp', partners(count, bit + count.bit_length() - 1 -...]
    ppermute x23 -> x22, waiting for transfers between devices: 24.7 us -> 29.3 us  [swap(): lax.ppermute(value, 'dp', partners(count, bit + count.bit_length() - 1 -...]
  transfers between devices with their start and end apart: 35 -> 34, of which waited for: 16 -> 16; matrix products, arithmetic and copies ran while one was open for 0% -> 0% of each run, Pallas kernels for 36% -> 36%
where the time goes in v4:
time: 99.3 us; the launch traced here: 99.1 us
  Pallas kernels  37.3 us (38%)
  waiting for transfers between devices  32.1 us (32%)
  starting transfers between devices  28.6 us (29%)
  between operations  1.12 us (1%)
    pallas_call x23, Pallas kernels, call(): pl.pallas_call(body, out_shape=[(pltpu.HBM if i in far_out else pltpu.VME...  37.3 us
    ppermute x22, waiting for transfers between devices, swap(): lax.ppermute(value, 'dp', partners(count, bit + count.bit_length() - 1 -...  29.3 us
    ppermute x22, starting transfers between devices, swap(): lax.ppermute(value, 'dp', partners(count, bit + count.bit_length() - 1 -...  25.6 us
    ppermute x12, starting transfers between devices, other_core(): return lax.ppermute(value, 'head', [(0, 1), (1, 0)])  3 us
    ppermute x12, waiting for transfers between devices, other_core(): return lax.ppermute(value, 'head', [(0, 1), (1, 0)])  2.78 us
  transfers between devices with their start and end apart: 34, of which 16 were waited for; matrix products, arithmetic and copies ran while one was open for 0% of the time, Pallas kernels for 36%

profile of v4, /device:TPU:0, one launch (start us, length us, event | category | flops | bytes accessed | tf_op | source)
XLA Modules:
  0.0 99.1 jit_solution(6814626780109204512)
XLA Ops:
  1.3 2.7 %shard_map.263 = (s32[8,128]{1,0:T(8,128)S(1)}, s32[8,128]{1,0:T(8,128)S(1)}, bf16[336,768]{1,0:T(8,128)(2,1)S(1)}, bf16[336,768]{1,0:T(8,128)(2,1)S(1)}, bf16[3...) custom-call(s32[3,98]{1,0:T(4,128)} %refs_0_.1, ...), custom_call_target="tpu_custom_call" | custom-call | flops 1 | bytes 1 | tf_op jit(solution)/shard_map/pallas_call | solution.py:144
  6.6 4.0 %shard_map.264 = (bf16[336,1152]{1,0:T(8,128)(2,1)S(1)}, bf16[336,1152]{1,0:T(8,128)(2,1)S(1)}, bf16[336,384]{1,0:T(8,128)(2,1)S(1)}, bf16[336,384]{1,0:T(8,128)...) custom-call(s32[8,128]{1,0:T(8,128)S(1)} %get-tuple-element.250.refs_0_, ...), custom_call_target="tpu_custom_call" | custom-call | flops 1 | bytes 1 | tf_op jit(solution)/shard_map/pallas_call | solution.py:144
  17.0 2.5 %shard_map.269 = (bf16[384,512]{1,0:T(8,128)(2,1)S(1)}, bf16[384,512]{1,0:T(8,128)(2,1)S(1)}, bf16[384,512]{1,0:T(8,128)(2,1)S(1)}, f32[384,512]{1,0:T(8,128)S(1...) custom-call(bf16[336,768]{1,0:T(8,128)(2,1)S(1)} %get-tuple-element.249.refs_0_, ...), custom_call_target="tpu_custom_call" | custom-call | flops 1 | bytes 1 | tf_op jit(solution)/shard_map/pallas_call | solution.py:144
  19.4 2.7 %collective-permute-start.7 = (bf16[384,512]{1,0:T(8,128)(2,1)S(1)}, bf16[384,512]{1,0:T(8,128)(2,1)S(1)}, u32[]{:S(2)}, u32[]{:S(2)}) collective-permute-start(bf16[384,512]{1,0:T(8,128)(2,1)S(1)} %get-tuple-element.292), channel_id=1, source_target_pairs={{0,2},{2,0},{4,6},{6,4},{8,10},{10,8},{12,14},{14,12},{16,18},{18,... | collective-permute-start | bytes 1179656 | tf_op jit(solution)/shard_map/ppermute | solution.py:678
  23.6 1.6 %collective-permute-start.9 = (bf16[384,512]{1,0:T(8,128)(2,1)S(1)}, bf16[384,512]{1,0:T(8,128)(2,1)S(1)}, u32[]{:S(2)}, u32[]{:S(2)}) collective-permute-start(bf16[384,512]{1,0:T(8,128)(2,1)S(1)} %get-tuple-element.296), channel_id=1, source_target_pairs={{0,8},{2,10},{4,12},{6,14},{8,0},{10,2},{12,4},{14,6},{16,24},{18,... | collective-permute-start | bytes 1179656 | tf_op jit(solution)/shard_map/ppermute | solution.py:678
  25.2 2.5 %shard_map.270 = (bf16[336,768]{1,0:T(8,128)(2,1)S(1)}, f32[336,768]{1,0:T(8,128)S(1)}, f32[8,768]{1,0:T(8,128)S(1)}) custom-call(bf16[336,1536]{1,0:T(8,128)(2,1)S(1)} %get-tuple-element.284.refs_0_, bf16[768,1536]{1,0:T(8,128)(2,1)S(1)} %collective-permute-done.4.refs_1_, bf16[336,1536]{1,0:T(8,128)(2,1)S(1)} %get-tuple-element.299.refs_2_, ...), custom_call_target="tpu_custom_call" | custom-call | flops 1 | bytes 1 | tf_op jit(solution)/shard_map/pallas_call | solution.py:144
  27.7 2.5 %shard_map.271 = (bf16[384,512]{1,0:T(8,128)(2,1)S(1)}, bf16[384,512]{1,0:T(8,128)(2,1)S(1)}, bf16[384,512]{1,0:T(8,128)(2,1)S(1)}, f32[384,512]{1,0:T(8,128)S(1...) custom-call(bf16[336,768]{1,0:T(8,128)(2,1)S(1)} %get-tuple-element.261.refs_0_, ...), custom_call_target="tpu_custom_call" | custom-call | flops 1 | bytes 1 | tf_op jit(solution)/shard_map/pallas_call | solution.py:144
  30.2 1.8 %shard_map.272.refs_7_ = bf16[336,1152]{1,0:T(8,128)(2,1)S(1)} custom-call(s32[8,128]{1,0:T(8,128)S(1)} %get-tuple-element.250.refs_0_, bf16[336,768]{1,0:T(8,128)(2,1)S(1)} %get-tuple-element.332.refs_1_.refs_2_, bf16[384,768]{1,0:T(8,128)(2,1)S(1)} %collective-permute-done.2.refs_5_.refs_2_, bf16[336,1152]{1,0:T(8,128)(2,1)S(1)} %get-tuple-element.311.refs_3_), custom_call_target="tpu_custom_call" | custom-call | flops 1 | bytes 1 | tf_op jit(solution)/shard_map/pallas_call | solution.py:144
  34.7 1.6 %collective-permute-start.12 = (bf16[576,512]{1,0:T(8,128)(2,1)S(1)}, bf16[576,512]{1,0:T(8,128)(2,1)S(1)}, u32[]{:S(2)}, u32[]{:S(2)}) collective-permute-start(bf16[576,512]{1,0:T(8,128)(2,1)S(1)} %get-tuple-element.326), channel_id=1, source_target_pairs={{0,8},{2,10},{4,12},{6,14},{8,0},{10,2},{12,4},{14,6},{16,24},{18,... | collective-permute-start | bytes 1769480 | tf_op jit(solution)/shard_map/ppermute | solution.py:678
  37.4 1.8 %shard_map.274.refs_4_.refs_6_ = bf16[336,1152]{1,0:T(8,128)(2,1)S(1)} custom-call(s32[8,128]{1,0:T(8,128)S(1)} %get-tuple-element.250.refs_0_, bf16[336,768]{1,0:T(8,128)(2,1)S(1)} %get-tuple-element.332.refs_1_.refs_2_, bf16[384,768]{1,0:T(8,128)(2,1)S(1)} %get-tuple-element.254.refs_4_.refs_2_, bf16[336,1152]{1,0:T(8,128)(2,1)S(1)} %get-tuple-element.333.refs_3_), custom_call_target="tpu_custom_call" | custom-call | flops 1 | bytes 1 | tf_op jit(solution)/shard_map/pallas_call | solution.py:144
  39.3 3.7 %shard_map.275 = (bf16[384,512]{1,0:T(8,128)(2,1)S(1)}, bf16[384,512]{1,0:T(8,128)(2,1)S(1)}, bf16[384,512]{1,0:T(8,128)(2,1)S(1)}, f32[384,512]{1,0:T(8,128)S(1...) custom-call(bf16[336,768]{1,0:T(8,128)(2,1)S(1)} %get-tuple-element.252.refs_1_.refs_0_, ...), custom_call_target="tpu_custom_call" | custom-call | flops 1 | bytes 1 | tf_op jit(solution)/shard_map/pallas_call | solution.py:144
  43.0 7.4 %collective-permute-done.12.refs_2_.refs_9_ = bf16[576,512]{1,0:T(8,128)(2,1)S(1)} collective-permute-done((bf16[576,512]{1,0:T(8,128)(2,1)S(1)}, bf16[576,512]{1,0:T(8,128)(2,1)S(1)}, u32[]{:S(2)}, u32[]{:S(2)}) %collective-permute-start.12) | collective-permute-done | bytes 589856 | tf_op jit(solution)/shard_map/ppermute | solution.py:678
  54.8 2.1 %shard_map.277 = (f32[336,768]{1,0:T(8,128)S(1)}, f32[336,1]{1,0:T(8,128)S(1)}, f32[1,768]{1,0:T(1,128)S(1)}) custom-call(bf16[336,768]{1,0:T(8,128)(2,1)S(1)} %get-tuple-element.248.refs_6_.refs_4_.refs_0_.refs_3_, bf16[336,768]{1,0:T(8,128)(2,1)S(1)} %get-tuple-element.287.refs_6_.refs_1_, f32[336,1]{1,0:T(8,128)S(1)} %get-tuple-element.290.refs_2_, ...), custom_call_target="tpu_custom_call" | custom-call | flops 1 | bytes 1 | tf_op jit(solution)/shard_map/pallas_call | solution.py:144
  56.9 2.6 %shard_map.278 = (f32[336,768]{1,0:T(8,128)S(1)}, f32[9,768]{1,0:T(8,128)S(1)}, f32[9,768]{1,0:T(8,128)S(1)}) custom-call(bf16[3,768,384]{2,1,0:T(8,128)(2,1)S(1)} %get-tuple-element.245.refs_2_.refs_0_, f32[768]{0:T(1024)S(1)} %get-tuple-element.246.refs_1_, f32[768]{0:T(1024)S(1)} %get-tuple-element.247.refs_2_, ...), custom_call_target="tpu_custom_call" | custom-call | flops 1 | bytes 1 | tf_op jit(solution)/shard_map/pallas_call | solution.py:144
  60.8 1.6 %shard_map.279 = (bf16[3,197,768]{2,1,0:T(8,128)(2,1)}, f32[9,768]{1,0:T(8,128)S(1)}) custom-call(s32[8,128]{1,0:T(8,128)S(1)} %get-tuple-element.368.refs_0_, bf16[3,197,768]{2,1,0:T(8,128)(2,1)S(1)} %copy-done.2, f32[336,768]{1,0:T(8,128)S(1)} %get-tuple-element.371.refs_2_, f32[9,768]{1,0:T(8,128)S(1)} %get-tuple-element.372.refs_3_, ...), custom_call_target="tpu_custom_call" | custom-call | flops 1 | bytes 1 | tf_op jit(solution)/shard_map/pallas_call | solution.py:144
  62.9 1.6 %shard_map.280 = bf16[3,197,768]{2,1,0:T(8,128)(2,1)} custom-call(s32[8,128]{1,0:T(8,128)S(1)} %get-tuple-element.368.refs_0_, bf16[3,197,768]{2,1,0:T(8,128)(2,1)S(1)} %copy-done.3, f32[336,768]{1,0:T(8,128)S(1)} %get-tuple-element.382.refs_2_), custom_call_target="tpu_custom_call" | custom-call | flops 1 | bytes 1 | tf_op jit(solution)/shard_map/pallas_call | solution.py:144
  64.5 4.8 %collective-permute-done.18.refs_11_.refs_6_.refs_1_.refs_12_ = bf16[672,512]{1,0:T(8,128)(2,1)S(1)} collective-permute-done((bf16[672,512]{1,0:T(8,128)(2,1)S(1)}, bf16[672,512]{1,0:T(8,128)(2,1)S(1)}, u32[]{:S(2)}, u32[]{:S(2)}) %collective-permute-start.18) | collective-permute-done | bytes 688160 | tf_op jit(solution)/shard_map/ppermute | solution.py:678
  73.2 2.6 %collective-permute-start.29 = (bf16[144,512]{1,0:T(8,128)(2,1)S(1)}, bf16[144,512]{1,0:T(8,128)(2,1)S(1)}, u32[]{:S(2)}, u32[]{:S(2)}) collective-permute-start(bf16[144,512]{1,0:T(8,128)(2,1)S(1)} %get-tuple-element.450), channel_id=1, source_target_pairs={{0,16},{2,18},{4,20},{6,22},{8,24},{10,26},{12,28},{14,30},{16,0},... | collective-permute-start | bytes 442376 | tf_op jit(solution)/shard_map/ppermute | solution.py:678
  76.6 4.0 %collective-permute-done.22.refs_7_.refs_2_.refs_17_ = bf16[288,512]{1,0:T(8,128)(2,1)S(1)} collective-permute-done((bf16[288,512]{1,0:T(8,128)(2,1)S(1)}, bf16[288,512]{1,0:T(8,128)(2,1)S(1)}, u32[]{:S(2)}, u32[]{:S(2)}) %collective-permute-start.22) | collective-permute-done | bytes 294944 | tf_op jit(solution)/shard_map/ppermute | solution.py:678
  80.8 1.6 %collective-permute-start.26 = (bf16[96,512]{1,0:T(8,128)(2,1)S(1)}, bf16[96,512]{1,0:T(8,128)(2,1)S(1)}, u32[]{:S(2)}, u32[]{:S(2)}) collective-permute-start(bf16[96,512]{1,0:T(8,128)(2,1)S(1)} %get-tuple-element.434), channel_id=1, source_target_pairs={{0,4},{2,6},{4,0},{6,2},{8,12},{10,14},{12,8},{14,10},{16,20},{18,... | collective-permute-start | bytes 294920 | tf_op jit(solution)/shard_map/ppermute | solution.py:678
  85.8 2.3 %collective-permute-done.27.refs_7_.refs_8_ = bf16[96,512]{1,0:T(8,128)(2,1)S(1)} collective-permute-done((bf16[96,512]{1,0:T(8,128)(2,1)S(1)}, bf16[96,512]{1,0:T(8,128)(2,1)S(1)}, u32[]{:S(2)}, u32[]{:S(2)}) %collective-permute-start.27) | collective-permute-done | bytes 98336 | tf_op jit(solution)/shard_map/ppermute | solution.py:678
  90.0 1.9 %collective-permute-start.33 = (f32[9,768]{1,0:T(8,128)S(1)}, f32[9,768]{1,0:T(8,128)S(1)}, u32[]{:S(2)}, u32[]{:S(2)}) collective-permute-start(f32[9,768]{1,0:T(8,128)S(1)} %get-tuple-element.463.refs_13_), channel_id=1, source_target_pairs={{0,16},{2,18},{4,20},{6,22},{8,24},{10,26},{12,28},{14,30},{16,0},... | collective-permute-start | bytes 82952 | tf_op jit(solution)/shard_map/ppermute | solution.py:678
  91.9 3.5 %collective-permute-done.32.refs_15_ = bf16[144,512]{1,0:T(8,128)(2,1)S(1)} collective-permute-done((bf16[144,512]{1,0:T(8,128)(2,1)S(1)}, bf16[144,512]{1,0:T(8,128)(2,1)S(1)}, u32[]{:S(2)}, u32[]{:S(2)}) %collective-permute-start.32) | collective-permute-done | bytes 147488 | tf_op jit(solution)/shard_map/ppermute | solution.py:678
  96.4 1.7 %collective-permute-done.33.refs_14_ = f32[9,768]{1,0:T(8,128)S(1)} collective-permute-done((f32[9,768]{1,0:T(8,128)S(1)}, f32[9,768]{1,0:T(8,128)S(1)}, u32[]{:S(2)}, u32[]{:S(2)}) %collective-permute-start.33) | collective-permute-done | bytes 27680 | tf_op jit(solution)/shard_map/ppermute | solution.py:678
  (77 shorter events, 32.9 us)
Async XLA Ops:
  0.7 5.4 %collective-permute-start.1 = (bf16[3,768,384]{2,1,0:T(8,128)(2,1)}, bf16[3,768,384]{2,1,0:T(8,128)(2,1)S(1)}, u32[]{:S(2)}, u32[]{:S(2)}) collective-permute-start(bf16[3,768,384]{2,1,0:T(8,128)(2,1)} %refs_7_.2), channel_id=1, source_target_pairs={{0,1},{1,0},{2,3},{3,2},{4,5},{5,4},{6,7},{7,6},{8,9},{9,8},{10,11... | collective-permute-start | bytes 5308424 | tf_op jit(solution)/shard_map/ppermute | solution.py:670
  4.0 6.5 %collective-permute-start.3 = (bf16[336,768]{1,0:T(8,128)(2,1)S(1)}, bf16[336,768]{1,0:T(8,128)(2,1)S(1)}, u32[]{:S(2)}, u32[]{:S(2)}) collective-permute-start(bf16[336,768]{1,0:T(8,128)(2,1)S(1)} %get-tuple-element.249.refs_0_), channel_id=1, source_target_pairs={{0,1},{1,0},{2,3},{3,2},{4,5},{5,4},{6,7},{7,6},{8,9},{9,8},{10,11... | collective-permute-start | bytes 1548296 | tf_op jit(solution)/shard_map/ppermute | solution.py:670
  16.4 11.3 %collective-permute-start.10 = (bf16[336,1920]{1,0:T(8,128)(2,1)S(1)}, bf16[336,1920]{1,0:T(8,128)(2,1)S(1)}, u32[]{:S(2)}, u32[]{:S(2)}) collective-permute-start(bf16[336,1920]{1,0:T(8,128)(2,1)S(1)} %get-tuple-element.297), channel_id=1, source_target_pairs={{0,1},{1,0},{2,3},{3,2},{4,5},{5,4},{6,7},{7,6},{8,9},{9,8},{10,11... | collective-permute-start | bytes 3870728 | tf_op jit(solution)/shard_map/ppermute | solution.py:670
  16.6 11.1 %collective-permute-start.11 = (bf16[336,1536]{1,0:T(8,128)(2,1)S(1)}, bf16[336,1536]{1,0:T(8,128)(2,1)S(1)}, u32[]{:S(2)}, u32[]{:S(2)}) collective-permute-start(bf16[336,1536]{1,0:T(8,128)(2,1)S(1)} %get-tuple-element.284.refs_0_), channel_id=1, source_target_pairs={{0,1},{1,0},{2,3},{3,2},{4,5},{5,4},{6,7},{7,6},{8,9},{9,8},{10,11... | collective-permute-start | bytes 3096584 | tf_op jit(solution)/shard_map/ppermute | solution.py:670
  19.4 12.6 %collective-permute-start.7 = (bf16[384,512]{1,0:T(8,128)(2,1)S(1)}, bf16[384,512]{1,0:T(8,128)(2,1)S(1)}, u32[]{:S(2)}, u32[]{:S(2)}) collective-permute-start(bf16[384,512]{1,0:T(8,128)(2,1)S(1)} %get-tuple-element.292), channel_id=1, source_target_pairs={{0,2},{2,0},{4,6},{6,4},{8,10},{10,8},{12,14},{14,12},{16,18},{18,... | collective-permute-start | bytes 1179656 | tf_op jit(solution)/shard_map/ppermute | solution.py:678
  22.1 11.1 %collective-permute-start.8 = (bf16[384,512]{1,0:T(8,128)(2,1)S(1)}, bf16[384,512]{1,0:T(8,128)(2,1)S(1)}, u32[]{:S(2)}, u32[]{:S(2)}) collective-permute-start(bf16[384,512]{1,0:T(8,128)(2,1)S(1)} %get-tuple-element.294), channel_id=1, source_target_pairs={{0,4},{2,6},{4,0},{6,2},{8,12},{10,14},{12,8},{14,10},{16,20},{18,... | collective-permute-start | bytes 1179656 | tf_op jit(solution)/shard_map/ppermute | solution.py:678
  23.6 10.8 %collective-permute-start.9 = (bf16[384,512]{1,0:T(8,128)(2,1)S(1)}, bf16[384,512]{1,0:T(8,128)(2,1)S(1)}, u32[]{:S(2)}, u32[]{:S(2)}) collective-permute-start(bf16[384,512]{1,0:T(8,128)(2,1)S(1)} %get-tuple-element.296), channel_id=1, source_target_pairs={{0,8},{2,10},{4,12},{6,14},{8,0},{10,2},{12,4},{14,6},{16,24},{18,... | collective-permute-start | bytes 1179656 | tf_op jit(solution)/shard_map/ppermute | solution.py:678
  34.7 15.7 %collective-permute-start.12 = (bf16[576,512]{1,0:T(8,128)(2,1)S(1)}, bf16[576,512]{1,0:T(8,128)(2,1)S(1)}, u32[]{:S(2)}, u32[]{:S(2)}) collective-permute-start(bf16[576,512]{1,0:T(8,128)(2,1)S(1)} %get-tuple-element.326), channel_id=1, source_target_pairs={{0,8},{2,10},{4,12},{6,14},{8,0},{10,2},{12,4},{14,6},{16,24},{18,... | collective-permute-start | bytes 1769480 | tf_op jit(solution)/shard_map/ppermute | solution.py:678
  36.4 15.4 %collective-permute-start.13 = (bf16[576,512]{1,0:T(8,128)(2,1)S(1)}, bf16[576,512]{1,0:T(8,128)(2,1)S(1)}, u32[]{:S(2)}, u32[]{:S(2)}) collective-permute-start(bf16[576,512]{1,0:T(8,128)(2,1)S(1)} %get-tuple-element.327), channel_id=1, source_target_pairs={{0,2},{2,0},{4,6},{6,4},{8,10},{10,8},{12,14},{14,12},{16,18},{18,... | collective-permute-start | bytes 1769480 | tf_op jit(solution)/shard_map/ppermute | solution.py:678
  36.9 15.1 %collective-permute-start.14 = (bf16[576,512]{1,0:T(8,128)(2,1)S(1)}, bf16[576,512]{1,0:T(8,128)(2,1)S(1)}, u32[]{:S(2)}, u32[]{:S(2)}) collective-permute-start(bf16[576,512]{1,0:T(8,128)(2,1)S(1)} %get-tuple-element.328), channel_id=1, source_target_pairs={{0,4},{2,6},{4,0},{6,2},{8,12},{10,14},{12,8},{14,10},{16,20},{18,... | collective-permute-start | bytes 1769480 | tf_op jit(solution)/shard_map/ppermute | solution.py:678
  52.3 17.0 %collective-permute-start.18 = (bf16[672,512]{1,0:T(8,128)(2,1)S(1)}, bf16[672,512]{1,0:T(8,128)(2,1)S(1)}, u32[]{:S(2)}, u32[]{:S(2)}) collective-permute-start(bf16[672,512]{1,0:T(8,128)(2,1)S(1)} %get-tuple-element.377), channel_id=1, source_target_pairs={{0,2},{2,0},{4,6},{6,4},{8,10},{10,8},{12,14},{14,12},{16,18},{18,... | collective-permute-start | bytes 2064392 | tf_op jit(solution)/shard_map/ppermute | solution.py:678
  53.8 16.1 %collective-permute-start.19 = (bf16[672,512]{1,0:T(8,128)(2,1)S(1)}, bf16[672,512]{1,0:T(8,128)(2,1)S(1)}, u32[]{:S(2)}, u32[]{:S(2)}) collective-permute-start(bf16[672,512]{1,0:T(8,128)(2,1)S(1)} %get-tuple-element.378), channel_id=1, source_target_pairs={{0,4},{2,6},{4,0},{6,2},{8,12},{10,14},{12,8},{14,10},{16,20},{18,... | collective-permute-start | bytes 2064392 | tf_op jit(solution)/shard_map/ppermute | solution.py:678
  54.4 15.8 %collective-permute-start.20 = (bf16[672,512]{1,0:T(8,128)(2,1)S(1)}, bf16[672,512]{1,0:T(8,128)(2,1)S(1)}, u32[]{:S(2)}, u32[]{:S(2)}) collective-permute-start(bf16[672,512]{1,0:T(8,128)(2,1)S(1)} %get-tuple-element.379), channel_id=1, source_target_pairs={{0,8},{2,10},{4,12},{6,14},{8,0},{10,2},{12,4},{14,6},{16,24},{18,... | collective-permute-start | bytes 2064392 | tf_op jit(solution)/shard_map/ppermute | solution.py:678
  62.4 7.7 %collective-permute-start.21 = (f32[9,768]{1,0:T(8,128)S(1)}, f32[9,768]{1,0:T(8,128)S(1)}, u32[]{:S(2)}, u32[]{:S(2)}) collective-permute-start(f32[9,768]{1,0:T(8,128)S(1)} %get-tuple-element.401.refs_18_), channel_id=1, source_target_pairs={{0,2},{2,0},{4,6},{6,4},{8,10},{10,8},{12,14},{14,12},{16,18},{18,... | collective-permute-start | bytes 82952 | tf_op jit(solution)/shard_map/ppermute | solution.py:678
  70.4 10.2 %collective-permute-start.22 = (bf16[288,512]{1,0:T(8,128)(2,1)S(1)}, bf16[288,512]{1,0:T(8,128)(2,1)S(1)}, u32[]{:S(2)}, u32[]{:S(2)}) collective-permute-start(bf16[288,512]{1,0:T(8,128)(2,1)S(1)} %get-tuple-element.408), channel_id=1, source_target_pairs={{0,8},{2,10},{4,12},{6,14},{8,0},{10,2},{12,4},{14,6},{16,24},{18,... | collective-permute-start | bytes 884744 | tf_op jit(solution)/shard_map/ppermute | solution.py:678
  70.9 9.7 %collective-permute-start.23 = (bf16[288,512]{1,0:T(8,128)(2,1)S(1)}, bf16[288,512]{1,0:T(8,128)(2,1)S(1)}, u32[]{:S(2)}, u32[]{:S(2)}) collective-permute-start(bf16[288,512]{1,0:T(8,128)(2,1)S(1)} %get-tuple-element.409), channel_id=1, source_target_pairs={{0,4},{2,6},{4,0},{6,2},{8,12},{10,14},{12,8},{14,10},{16,20},{18,... | collective-permute-start | bytes 884744 | tf_op jit(solution)/shard_map/ppermute | solution.py:678
  72.5 8.2 %collective-permute-start.24 = (bf16[288,512]{1,0:T(8,128)(2,1)S(1)}, bf16[288,512]{1,0:T(8,128)(2,1)S(1)}, u32[]{:S(2)}, u32[]{:S(2)}) collective-permute-start(bf16[288,512]{1,0:T(8,128)(2,1)S(1)} %get-tuple-element.410), channel_id=1, source_target_pairs={{0,2},{2,0},{4,6},{6,4},{8,10},{10,8},{12,14},{14,12},{16,18},{18,... | collective-permute-start | bytes 884744 | tf_op jit(solution)/shard_map/ppermute | solution.py:678
  73.2 10.8 %collective-permute-start.29 = (bf16[144,512]{1,0:T(8,128)(2,1)S(1)}, bf16[144,512]{1,0:T(8,128)(2,1)S(1)}, u32[]{:S(2)}, u32[]{:S(2)}) collective-permute-start(bf16[144,512]{1,0:T(8,128)(2,1)S(1)} %get-tuple-element.450), channel_id=1, source_target_pairs={{0,16},{2,18},{4,20},{6,22},{8,24},{10,26},{12,28},{14,30},{16,0},... | collective-permute-start | bytes 442376 | tf_op jit(solution)/shard_map/ppermute | solution.py:678
  80.8 4.9 %collective-permute-start.26 = (bf16[96,512]{1,0:T(8,128)(2,1)S(1)}, bf16[96,512]{1,0:T(8,128)(2,1)S(1)}, u32[]{:S(2)}, u32[]{:S(2)}) collective-permute-start(bf16[96,512]{1,0:T(8,128)(2,1)S(1)} %get-tuple-element.434), channel_id=1, source_target_pairs={{0,4},{2,6},{4,0},{6,2},{8,12},{10,14},{12,8},{14,10},{16,20},{18,... | collective-permute-start | bytes 294920 | tf_op jit(solution)/shard_map/ppermute | solution.py:678
  82.4 5.6 %collective-permute-start.27 = (bf16[96,512]{1,0:T(8,128)(2,1)S(1)}, bf16[96,512]{1,0:T(8,128)(2,1)S(1)}, u32[]{:S(2)}, u32[]{:S(2)}) collective-permute-start(bf16[96,512]{1,0:T(8,128)(2,1)S(1)} %get-tuple-element.435), channel_id=1, source_target_pairs={{0,8},{2,10},{4,12},{6,14},{8,0},{10,2},{12,4},{14,6},{16,24},{18,... | collective-permute-start | bytes 294920 | tf_op jit(solution)/shard_map/ppermute | solution.py:678
  83.1 5.0 %collective-permute-start.28 = (bf16[96,512]{1,0:T(8,128)(2,1)S(1)}, bf16[96,512]{1,0:T(8,128)(2,1)S(1)}, u32[]{:S(2)}, u32[]{:S(2)}) collective-permute-start(bf16[96,512]{1,0:T(8,128)(2,1)S(1)} %get-tuple-element.436), channel_id=1, source_target_pairs={{0,2},{2,0},{4,6},{6,4},{8,10},{10,8},{12,14},{14,12},{16,18},{18,... | collective-permute-start | bytes 294920 | tf_op jit(solution)/shard_map/ppermute | solution.py:678
  84.6 10.9 %collective-permute-start.32 = (bf16[144,512]{1,0:T(8,128)(2,1)S(1)}, bf16[144,512]{1,0:T(8,128)(2,1)S(1)}, u32[]{:S(2)}, u32[]{:S(2)}) collective-permute-start(bf16[144,512]{1,0:T(8,128)(2,1)S(1)} %get-tuple-element.460), channel_id=1, source_target_pairs={{0,16},{2,18},{4,20},{6,22},{8,24},{10,26},{12,28},{14,30},{16,0},... | collective-permute-start | bytes 442376 | tf_op jit(solution)/shard_map/ppermute | solution.py:678
  88.9 9.1 %collective-permute-start.31 = (bf16[144,512]{1,0:T(8,128)(2,1)S(1)}, bf16[144,512]{1,0:T(8,128)(2,1)S(1)}, u32[]{:S(2)}, u32[]{:S(2)}) collective-permute-start(bf16[144,512]{1,0:T(8,128)(2,1)S(1)} %get-tuple-element.457), channel_id=1, source_target_pairs={{0,16},{2,18},{4,20},{6,22},{8,24},{10,26},{12,28},{14,30},{16,0},... | collective-permute-start | bytes 442376 | tf_op jit(solution)/shard_map/ppermute | solution.py:678
  90.0 8.0 %collective-permute-start.33 = (f32[9,768]{1,0:T(8,128)S(1)}, f32[9,768]{1,0:T(8,128)S(1)}, u32[]{:S(2)}, u32[]{:S(2)}) collective-permute-start(f32[9,768]{1,0:T(8,128)S(1)} %get-tuple-element.463.refs_13_), channel_id=1, source_target_pairs={{0,16},{2,18},{4,20},{6,22},{8,24},{10,26},{12,28},{14,30},{16,0},... | collective-permute-start | bytes 82952 | tf_op jit(solution)/shard_map/ppermute | solution.py:678
  (15 other events, 58.7 us)

commit v5 on v4

--- a/solution.py
+++ b/solution.py
@@ -16,7 +16,7 @@
 
 MIB = 1024 * 1024
 SIDES = 2
-FLOPS = 1
+FLOPS = 300_000_000
 UNIT_BLOCK = 512
 
 

time: 99.3 us -> 99.3 us (level)
  no operation moved by 1% of the time
where the time goes in v5:
time: 99.3 us; the launch traced here: 99.1 us
  Pallas kernels  37.3 us (38%)
  waiting for transfers between devices  32.1 us (32%)
  starting transfers between devices  28.6 us (29%)
  between operations  1.12 us (1%)
    pallas_call x23, Pallas kernels, call(): pl.pallas_call(body, out_shape=[(pltpu.HBM if i in far_out else pltpu.VME...  37.3 us
    ppermute x22, waiting for transfers between devices, swap(): lax.ppermute(value, 'dp', partners(count, bit + count.bit_length() - 1 -...  29.3 us
    ppermute x22, starting transfers between devices, swap(): lax.ppermute(value, 'dp', partners(count, bit + count.bit_length() - 1 -...  25.6 us
    ppermute x12, starting transfers between devices, other_core(): return lax.ppermute(value, 'head', [(0, 1), (1, 0)])  3 us
    ppermute x12, waiting for transfers between devices, other_core(): return lax.ppermute(value, 'head', [(0, 1), (1, 0)])  2.78 us
  transfers between devices with their start and end apart: 34, of which 16 were waited for; matrix products, arithmetic and copies ran while one was open for 0% of the time, Pallas kernels for 36%

profile of v5, /device:TPU:0, one launch (start us, length us, event | category | flops | bytes accessed | tf_op | source)
XLA Modules:
  0.0 99.1 jit_solution(4986456624620640043)
XLA Ops:
  1.3 2.7 %shard_map.263 = (s32[8,128]{1,0:T(8,128)S(1)}, s32[8,128]{1,0:T(8,128)S(1)}, bf16[336,768]{1,0:T(8,128)(2,1)S(1)}, bf16[336,768]{1,0:T(8,128)(2,1)S(1)}, bf16[3...) custom-call(s32[3,98]{1,0:T(4,128)} %refs_0_.1, ...), custom_call_target="tpu_custom_call" | custom-call | flops 300000000 | bytes 1 | tf_op jit(solution)/shard_map/pallas_call | solution.py:144
  6.6 4.0 %shard_map.264 = (bf16[336,1152]{1,0:T(8,128)(2,1)S(1)}, bf16[336,1152]{1,0:T(8,128)(2,1)S(1)}, bf16[336,384]{1,0:T(8,128)(2,1)S(1)}, bf16[336,384]{1,0:T(8,128)...) custom-call(s32[8,128]{1,0:T(8,128)S(1)} %get-tuple-element.250.refs_0_, ...), custom_call_target="tpu_custom_call" | custom-call | flops 300000000 | bytes 1 | tf_op jit(solution)/shard_map/pallas_call | solution.py:144
  17.0 2.5 %shard_map.269 = (bf16[384,512]{1,0:T(8,128)(2,1)S(1)}, bf16[384,512]{1,0:T(8,128)(2,1)S(1)}, bf16[384,512]{1,0:T(8,128)(2,1)S(1)}, f32[384,512]{1,0:T(8,128)S(1...) custom-call(bf16[336,768]{1,0:T(8,128)(2,1)S(1)} %get-tuple-element.249.refs_0_, ...), custom_call_target="tpu_custom_call" | custom-call | flops 300000000 | bytes 1 | tf_op jit(solution)/shard_map/pallas_call | solution.py:144
  19.4 2.7 %collective-permute-start.7 = (bf16[384,512]{1,0:T(8,128)(2,1)S(1)}, bf16[384,512]{1,0:T(8,128)(2,1)S(1)}, u32[]{:S(2)}, u32[]{:S(2)}) collective-permute-start(bf16[384,512]{1,0:T(8,128)(2,1)S(1)} %get-tuple-element.292), channel_id=1, source_target_pairs={{0,2},{2,0},{4,6},{6,4},{8,10},{10,8},{12,14},{14,12},{16,18},{18,... | collective-permute-start | bytes 1179656 | tf_op jit(solution)/shard_map/ppermute | solution.py:678
  23.6 1.6 %collective-permute-start.9 = (bf16[384,512]{1,0:T(8,128)(2,1)S(1)}, bf16[384,512]{1,0:T(8,128)(2,1)S(1)}, u32[]{:S(2)}, u32[]{:S(2)}) collective-permute-start(bf16[384,512]{1,0:T(8,128)(2,1)S(1)} %get-tuple-element.296), channel_id=1, source_target_pairs={{0,8},{2,10},{4,12},{6,14},{8,0},{10,2},{12,4},{14,6},{16,24},{18,... | collective-permute-start | bytes 1179656 | tf_op jit(solution)/shard_map/ppermute | solution.py:678
  25.2 2.5 %shard_map.270 = (bf16[336,768]{1,0:T(8,128)(2,1)S(1)}, f32[336,768]{1,0:T(8,128)S(1)}, f32[8,768]{1,0:T(8,128)S(1)}) custom-call(bf16[336,1536]{1,0:T(8,128)(2,1)S(1)} %get-tuple-element.284.refs_0_, bf16[768,1536]{1,0:T(8,128)(2,1)S(1)} %collective-permute-done.4.refs_1_, bf16[336,1536]{1,0:T(8,128)(2,1)S(1)} %get-tuple-element.299.refs_2_, ...), custom_call_target="tpu_custom_call" | custom-call | flops 300000000 | bytes 1 | tf_op jit(solution)/shard_map/pallas_call | solution.py:144
  27.7 2.5 %shard_map.271 = (bf16[384,512]{1,0:T(8,128)(2,1)S(1)}, bf16[384,512]{1,0:T(8,128)(2,1)S(1)}, bf16[384,512]{1,0:T(8,128)(2,1)S(1)}, f32[384,512]{1,0:T(8,128)S(1...) custom-call(bf16[336,768]{1,0:T(8,128)(2,1)S(1)} %get-tuple-element.261.refs_0_, ...), custom_call_target="tpu_custom_call" | custom-call | flops 300000000 | bytes 1 | tf_op jit(solution)/shard_map/pallas_call | solution.py:144
  30.2 1.8 %shard_map.272.refs_7_ = bf16[336,1152]{1,0:T(8,128)(2,1)S(1)} custom-call(s32[8,128]{1,0:T(8,128)S(1)} %get-tuple-element.250.refs_0_, bf16[336,768]{1,0:T(8,128)(2,1)S(1)} %get-tuple-element.332.refs_1_.refs_2_, bf16[384,768]{1,0:T(8,128)(2,1)S(1)} %collective-permute-done.2.refs_5_.refs_2_, bf16[336,1152]{1,0:T(8,128)(2,1)S(1)} %get-tuple-element.311.refs_3_), custom_call_target="tpu_custom_call" | custom-call | flops 300000000 | bytes 1 | tf_op jit(solution)/shard_map/pallas_call | solution.py:144
  34.7 1.6 %collective-permute-start.12 = (bf16[576,512]{1,0:T(8,128)(2,1)S(1)}, bf16[576,512]{1,0:T(8,128)(2,1)S(1)}, u32[]{:S(2)}, u32[]{:S(2)}) collective-permute-start(bf16[576,512]{1,0:T(8,128)(2,1)S(1)} %get-tuple-element.326), channel_id=1, source_target_pairs={{0,8},{2,10},{4,12},{6,14},{8,0},{10,2},{12,4},{14,6},{16,24},{18,... | collective-permute-start | bytes 1769480 | tf_op jit(solution)/shard_map/ppermute | solution.py:678
  37.4 1.8 %shard_map.274.refs_4_.refs_6_ = bf16[336,1152]{1,0:T(8,128)(2,1)S(1)} custom-call(s32[8,128]{1,0:T(8,128)S(1)} %get-tuple-element.250.refs_0_, bf16[336,768]{1,0:T(8,128)(2,1)S(1)} %get-tuple-element.332.refs_1_.refs_2_, bf16[384,768]{1,0:T(8,128)(2,1)S(1)} %get-tuple-element.254.refs_4_.refs_2_, bf16[336,1152]{1,0:T(8,128)(2,1)S(1)} %get-tuple-element.333.refs_3_), custom_call_target="tpu_custom_call" | custom-call | flops 300000000 | bytes 1 | tf_op jit(solution)/shard_map/pallas_call | solution.py:144
  39.3 3.7 %shard_map.275 = (bf16[384,512]{1,0:T(8,128)(2,1)S(1)}, bf16[384,512]{1,0:T(8,128)(2,1)S(1)}, bf16[384,512]{1,0:T(8,128)(2,1)S(1)}, f32[384,512]{1,0:T(8,128)S(1...) custom-call(bf16[336,768]{1,0:T(8,128)(2,1)S(1)} %get-tuple-element.252.refs_1_.refs_0_, ...), custom_call_target="tpu_custom_call" | custom-call | flops 300000000 | bytes 1 | tf_op jit(solution)/shard_map/pallas_call | solution.py:144
  43.0 7.4 %collective-permute-done.12.refs_2_.refs_9_ = bf16[576,512]{1,0:T(8,128)(2,1)S(1)} collective-permute-done((bf16[576,512]{1,0:T(8,128)(2,1)S(1)}, bf16[576,512]{1,0:T(8,128)(2,1)S(1)}, u32[]{:S(2)}, u32[]{:S(2)}) %collective-permute-start.12) | collective-permute-done | bytes 589856 | tf_op jit(solution)/shard_map/ppermute | solution.py:678
  54.8 2.1 %shard_map.277 = (f32[336,768]{1,0:T(8,128)S(1)}, f32[336,1]{1,0:T(8,128)S(1)}, f32[1,768]{1,0:T(1,128)S(1)}) custom-call(bf16[336,768]{1,0:T(8,128)(2,1)S(1)} %get-tuple-element.248.refs_6_.refs_4_.refs_0_.refs_3_, bf16[336,768]{1,0:T(8,128)(2,1)S(1)} %get-tuple-element.287.refs_6_.refs_1_, f32[336,1]{1,0:T(8,128)S(1)} %get-tuple-element.290.refs_2_, ...), custom_call_target="tpu_custom_call" | custom-call | flops 300000000 | bytes 1 | tf_op jit(solution)/shard_map/pallas_call | solution.py:144
  56.9 2.6 %shard_map.278 = (f32[336,768]{1,0:T(8,128)S(1)}, f32[9,768]{1,0:T(8,128)S(1)}, f32[9,768]{1,0:T(8,128)S(1)}) custom-call(bf16[3,768,384]{2,1,0:T(8,128)(2,1)S(1)} %get-tuple-element.245.refs_2_.refs_0_, f32[768]{0:T(1024)S(1)} %get-tuple-element.246.refs_1_, f32[768]{0:T(1024)S(1)} %get-tuple-element.247.refs_2_, ...), custom_call_target="tpu_custom_call" | custom-call | flops 300000000 | bytes 1 | tf_op jit(solution)/shard_map/pallas_call | solution.py:144
  60.8 1.6 %shard_map.279 = (bf16[3,197,768]{2,1,0:T(8,128)(2,1)}, f32[9,768]{1,0:T(8,128)S(1)}) custom-call(s32[8,128]{1,0:T(8,128)S(1)} %get-tuple-element.368.refs_0_, bf16[3,197,768]{2,1,0:T(8,128)(2,1)S(1)} %copy-done.2, f32[336,768]{1,0:T(8,128)S(1)} %get-tuple-element.371.refs_2_, f32[9,768]{1,0:T(8,128)S(1)} %get-tuple-element.372.refs_3_, ...), custom_call_target="tpu_custom_call" | custom-call | flops 300000000 | bytes 1 | tf_op jit(solution)/shard_map/pallas_call | solution.py:144
  62.9 1.6 %shard_map.280 = bf16[3,197,768]{2,1,0:T(8,128)(2,1)} custom-call(s32[8,128]{1,0:T(8,128)S(1)} %get-tuple-element.368.refs_0_, bf16[3,197,768]{2,1,0:T(8,128)(2,1)S(1)} %copy-done.3, f32[336,768]{1,0:T(8,128)S(1)} %get-tuple-element.382.refs_2_), custom_call_target="tpu_custom_call" | custom-call | flops 300000000 | bytes 1 | tf_op jit(solution)/shard_map/pallas_call | solution.py:144
  64.5 4.8 %collective-permute-done.18.refs_11_.refs_6_.refs_1_.refs_12_ = bf16[672,512]{1,0:T(8,128)(2,1)S(1)} collective-permute-done((bf16[672,512]{1,0:T(8,128)(2,1)S(1)}, bf16[672,512]{1,0:T(8,128)(2,1)S(1)}, u32[]{:S(2)}, u32[]{:S(2)}) %collective-permute-start.18) | collective-permute-done | bytes 688160 | tf_op jit(solution)/shard_map/ppermute | solution.py:678
  73.2 2.6 %collective-permute-start.29 = (bf16[144,512]{1,0:T(8,128)(2,1)S(1)}, bf16[144,512]{1,0:T(8,128)(2,1)S(1)}, u32[]{:S(2)}, u32[]{:S(2)}) collective-permute-start(bf16[144,512]{1,0:T(8,128)(2,1)S(1)} %get-tuple-element.450), channel_id=1, source_target_pairs={{0,16},{2,18},{4,20},{6,22},{8,24},{10,26},{12,28},{14,30},{16,0},... | collective-permute-start | bytes 442376 | tf_op jit(solution)/shard_map/ppermute | solution.py:678
  76.6 4.0 %collective-permute-done.22.refs_7_.refs_2_.refs_17_ = bf16[288,512]{1,0:T(8,128)(2,1)S(1)} collective-permute-done((bf16[288,512]{1,0:T(8,128)(2,1)S(1)}, bf16[288,512]{1,0:T(8,128)(2,1)S(1)}, u32[]{:S(2)}, u32[]{:S(2)}) %collective-permute-start.22) | collective-permute-done | bytes 294944 | tf_op jit(solution)/shard_map/ppermute | solution.py:678
  80.8 1.6 %collective-permute-start.26 = (bf16[96,512]{1,0:T(8,128)(2,1)S(1)}, bf16[96,512]{1,0:T(8,128)(2,1)S(1)}, u32[]{:S(2)}, u32[]{:S(2)}) collective-permute-start(bf16[96,512]{1,0:T(8,128)(2,1)S(1)} %get-tuple-element.434), channel_id=1, source_target_pairs={{0,4},{2,6},{4,0},{6,2},{8,12},{10,14},{12,8},{14,10},{16,20},{18,... | collective-permute-start | bytes 294920 | tf_op jit(solution)/shard_map/ppermute | solution.py:678
  85.8 2.3 %collective-permute-done.27.refs_7_.refs_8_ = bf16[96,512]{1,0:T(8,128)(2,1)S(1)} collective-permute-done((bf16[96,512]{1,0:T(8,128)(2,1)S(1)}, bf16[96,512]{1,0:T(8,128)(2,1)S(1)}, u32[]{:S(2)}, u32[]{:S(2)}) %collective-permute-start.27) | collective-permute-done | bytes 98336 | tf_op jit(solution)/shard_map/ppermute | solution.py:678
  90.0 1.9 %collective-permute-start.33 = (f32[9,768]{1,0:T(8,128)S(1)}, f32[9,768]{1,0:T(8,128)S(1)}, u32[]{:S(2)}, u32[]{:S(2)}) collective-permute-start(f32[9,768]{1,0:T(8,128)S(1)} %get-tuple-element.463.refs_13_), channel_id=1, source_target_pairs={{0,16},{2,18},{4,20},{6,22},{8,24},{10,26},{12,28},{14,30},{16,0},... | collective-permute-start | bytes 82952 | tf_op jit(solution)/shard_map/ppermute | solution.py:678
  91.9 3.5 %collective-permute-done.32.refs_15_ = bf16[144,512]{1,0:T(8,128)(2,1)S(1)} collective-permute-done((bf16[144,512]{1,0:T(8,128)(2,1)S(1)}, bf16[144,512]{1,0:T(8,128)(2,1)S(1)}, u32[]{:S(2)}, u32[]{:S(2)}) %collective-permute-start.32) | collective-permute-done | bytes 147488 | tf_op jit(solution)/shard_map/ppermute | solution.py:678
  96.4 1.7 %collective-permute-done.33.refs_14_ = f32[9,768]{1,0:T(8,128)S(1)} collective-permute-done((f32[9,768]{1,0:T(8,128)S(1)}, f32[9,768]{1,0:T(8,128)S(1)}, u32[]{:S(2)}, u32[]{:S(2)}) %collective-permute-start.33) | collective-permute-done | bytes 27680 | tf_op jit(solution)/shard_map/ppermute | solution.py:678
  (77 shorter events, 32.9 us)
Async XLA Ops:
  0.7 5.4 %collective-permute-start.1 = (bf16[3,768,384]{2,1,0:T(8,128)(2,1)}, bf16[3,768,384]{2,1,0:T(8,128)(2,1)S(1)}, u32[]{:S(2)}, u32[]{:S(2)}) collective-permute-start(bf16[3,768,384]{2,1,0:T(8,128)(2,1)} %refs_7_.2), channel_id=1, source_target_pairs={{0,1},{1,0},{2,3},{3,2},{4,5},{5,4},{6,7},{7,6},{8,9},{9,8},{10,11... | collective-permute-start | bytes 5308424 | tf_op jit(solution)/shard_map/ppermute | solution.py:670
  4.0 6.5 %collective-permute-start.3 = (bf16[336,768]{1,0:T(8,128)(2,1)S(1)}, bf16[336,768]{1,0:T(8,128)(2,1)S(1)}, u32[]{:S(2)}, u32[]{:S(2)}) collective-permute-start(bf16[336,768]{1,0:T(8,128)(2,1)S(1)} %get-tuple-element.249.refs_0_), channel_id=1, source_target_pairs={{0,1},{1,0},{2,3},{3,2},{4,5},{5,4},{6,7},{7,6},{8,9},{9,8},{10,11... | collective-permute-start | bytes 1548296 | tf_op jit(solution)/shard_map/ppermute | solution.py:670
  16.4 11.3 %collective-permute-start.10 = (bf16[336,1920]{1,0:T(8,128)(2,1)S(1)}, bf16[336,1920]{1,0:T(8,128)(2,1)S(1)}, u32[]{:S(2)}, u32[]{:S(2)}) collective-permute-start(bf16[336,1920]{1,0:T(8,128)(2,1)S(1)} %get-tuple-element.297), channel_id=1, source_target_pairs={{0,1},{1,0},{2,3},{3,2},{4,5},{5,4},{6,7},{7,6},{8,9},{9,8},{10,11... | collective-permute-start | bytes 3870728 | tf_op jit(solution)/shard_map/ppermute | solution.py:670
  16.6 11.1 %collective-permute-start.11 = (bf16[336,1536]{1,0:T(8,128)(2,1)S(1)}, bf16[336,1536]{1,0:T(8,128)(2,1)S(1)}, u32[]{:S(2)}, u32[]{:S(2)}) collective-permute-start(bf16[336,1536]{1,0:T(8,128)(2,1)S(1)} %get-tuple-element.284.refs_0_), channel_id=1, source_target_pairs={{0,1},{1,0},{2,3},{3,2},{4,5},{5,4},{6,7},{7,6},{8,9},{9,8},{10,11... | collective-permute-start | bytes 3096584 | tf_op jit(solution)/shard_map/ppermute | solution.py:670
  19.4 12.6 %collective-permute-start.7 = (bf16[384,512]{1,0:T(8,128)(2,1)S(1)}, bf16[384,512]{1,0:T(8,128)(2,1)S(1)}, u32[]{:S(2)}, u32[]{:S(2)}) collective-permute-start(bf16[384,512]{1,0:T(8,128)(2,1)S(1)} %get-tuple-element.292), channel_id=1, source_target_pairs={{0,2},{2,0},{4,6},{6,4},{8,10},{10,8},{12,14},{14,12},{16,18},{18,... | collective-permute-start | bytes 1179656 | tf_op jit(solution)/shard_map/ppermute | solution.py:678
  22.1 11.1 %collective-permute-start.8 = (bf16[384,512]{1,0:T(8,128)(2,1)S(1)}, bf16[384,512]{1,0:T(8,128)(2,1)S(1)}, u32[]{:S(2)}, u32[]{:S(2)}) collective-permute-start(bf16[384,512]{1,0:T(8,128)(2,1)S(1)} %get-tuple-element.294), channel_id=1, source_target_pairs={{0,4},{2,6},{4,0},{6,2},{8,12},{10,14},{12,8},{14,10},{16,20},{18,... | collective-permute-start | bytes 1179656 | tf_op jit(solution)/shard_map/ppermute | solution.py:678
  23.6 10.8 %collective-permute-start.9 = (bf16[384,512]{1,0:T(8,128)(2,1)S(1)}, bf16[384,512]{1,0:T(8,128)(2,1)S(1)}, u32[]{:S(2)}, u32[]{:S(2)}) collective-permute-start(bf16[384,512]{1,0:T(8,128)(2,1)S(1)} %get-tuple-element.296), channel_id=1, source_target_pairs={{0,8},{2,10},{4,12},{6,14},{8,0},{10,2},{12,4},{14,6},{16,24},{18,... | collective-permute-start | bytes 1179656 | tf_op jit(solution)/shard_map/ppermute | solution.py:678
  34.7 15.7 %collective-permute-start.12 = (bf16[576,512]{1,0:T(8,128)(2,1)S(1)}, bf16[576,512]{1,0:T(8,128)(2,1)S(1)}, u32[]{:S(2)}, u32[]{:S(2)}) collective-permute-start(bf16[576,512]{1,0:T(8,128)(2,1)S(1)} %get-tuple-element.326), channel_id=1, source_target_pairs={{0,8},{2,10},{4,12},{6,14},{8,0},{10,2},{12,4},{14,6},{16,24},{18,... | collective-permute-start | bytes 1769480 | tf_op jit(solution)/shard_map/ppermute | solution.py:678
  36.4 15.4 %collective-permute-start.13 = (bf16[576,512]{1,0:T(8,128)(2,1)S(1)}, bf16[576,512]{1,0:T(8,128)(2,1)S(1)}, u32[]{:S(2)}, u32[]{:S(2)}) collective-permute-start(bf16[576,512]{1,0:T(8,128)(2,1)S(1)} %get-tuple-element.327), channel_id=1, source_target_pairs={{0,2},{2,0},{4,6},{6,4},{8,10},{10,8},{12,14},{14,12},{16,18},{18,... | collective-permute-start | bytes 1769480 | tf_op jit(solution)/shard_map/ppermute | solution.py:678
  36.9 15.1 %collective-permute-start.14 = (bf16[576,512]{1,0:T(8,128)(2,1)S(1)}, bf16[576,512]{1,0:T(8,128)(2,1)S(1)}, u32[]{:S(2)}, u32[]{:S(2)}) collective-permute-start(bf16[576,512]{1,0:T(8,128)(2,1)S(1)} %get-tuple-element.328), channel_id=1, source_target_pairs={{0,4},{2,6},{4,0},{6,2},{8,12},{10,14},{12,8},{14,10},{16,20},{18,... | collective-permute-start | bytes 1769480 | tf_op jit(solution)/shard_map/ppermute | solution.py:678
  52.3 17.0 %collective-permute-start.18 = (bf16[672,512]{1,0:T(8,128)(2,1)S(1)}, bf16[672,512]{1,0:T(8,128)(2,1)S(1)}, u32[]{:S(2)}, u32[]{:S(2)}) collective-permute-start(bf16[672,512]{1,0:T(8,128)(2,1)S(1)} %get-tuple-element.377), channel_id=1, source_target_pairs={{0,2},{2,0},{4,6},{6,4},{8,10},{10,8},{12,14},{14,12},{16,18},{18,... | collective-permute-start | bytes 2064392 | tf_op jit(solution)/shard_map/ppermute | solution.py:678
  53.8 16.1 %collective-permute-start.19 = (bf16[672,512]{1,0:T(8,128)(2,1)S(1)}, bf16[672,512]{1,0:T(8,128)(2,1)S(1)}, u32[]{:S(2)}, u32[]{:S(2)}) collective-permute-start(bf16[672,512]{1,0:T(8,128)(2,1)S(1)} %get-tuple-element.378), channel_id=1, source_target_pairs={{0,4},{2,6},{4,0},{6,2},{8,12},{10,14},{12,8},{14,10},{16,20},{18,... | collective-permute-start | bytes 2064392 | tf_op jit(solution)/shard_map/ppermute | solution.py:678
  54.4 15.8 %collective-permute-start.20 = (bf16[672,512]{1,0:T(8,128)(2,1)S(1)}, bf16[672,512]{1,0:T(8,128)(2,1)S(1)}, u32[]{:S(2)}, u32[]{:S(2)}) collective-permute-start(bf16[672,512]{1,0:T(8,128)(2,1)S(1)} %get-tuple-element.379), channel_id=1, source_target_pairs={{0,8},{2,10},{4,12},{6,14},{8,0},{10,2},{12,4},{14,6},{16,24},{18,... | collective-permute-start | bytes 2064392 | tf_op jit(solution)/shard_map/ppermute | solution.py:678
  62.4 7.7 %collective-permute-start.21 = (f32[9,768]{1,0:T(8,128)S(1)}, f32[9,768]{1,0:T(8,128)S(1)}, u32[]{:S(2)}, u32[]{:S(2)}) collective-permute-start(f32[9,768]{1,0:T(8,128)S(1)} %get-tuple-element.401.refs_18_), channel_id=1, source_target_pairs={{0,2},{2,0},{4,6},{6,4},{8,10},{10,8},{12,14},{14,12},{16,18},{18,... | collective-permute-start | bytes 82952 | tf_op jit(solution)/shard_map/ppermute | solution.py:678
  70.4 10.2 %collective-permute-start.22 = (bf16[288,512]{1,0:T(8,128)(2,1)S(1)}, bf16[288,512]{1,0:T(8,128)(2,1)S(1)}, u32[]{:S(2)}, u32[]{:S(2)}) collective-permute-start(bf16[288,512]{1,0:T(8,128)(2,1)S(1)} %get-tuple-element.408), channel_id=1, source_target_pairs={{0,8},{2,10},{4,12},{6,14},{8,0},{10,2},{12,4},{14,6},{16,24},{18,... | collective-permute-start | bytes 884744 | tf_op jit(solution)/shard_map/ppermute | solution.py:678
  70.9 9.7 %collective-permute-start.23 = (bf16[288,512]{1,0:T(8,128)(2,1)S(1)}, bf16[288,512]{1,0:T(8,128)(2,1)S(1)}, u32[]{:S(2)}, u32[]{:S(2)}) collective-permute-start(bf16[288,512]{1,0:T(8,128)(2,1)S(1)} %get-tuple-element.409), channel_id=1, source_target_pairs={{0,4},{2,6},{4,0},{6,2},{8,12},{10,14},{12,8},{14,10},{16,20},{18,... | collective-permute-start | bytes 884744 | tf_op jit(solution)/shard_map/ppermute | solution.py:678
  72.5 8.2 %collective-permute-start.24 = (bf16[288,512]{1,0:T(8,128)(2,1)S(1)}, bf16[288,512]{1,0:T(8,128)(2,1)S(1)}, u32[]{:S(2)}, u32[]{:S(2)}) collective-permute-start(bf16[288,512]{1,0:T(8,128)(2,1)S(1)} %get-tuple-element.410), channel_id=1, source_target_pairs={{0,2},{2,0},{4,6},{6,4},{8,10},{10,8},{12,14},{14,12},{16,18},{18,... | collective-permute-start | bytes 884744 | tf_op jit(solution)/shard_map/ppermute | solution.py:678
  73.2 10.8 %collective-permute-start.29 = (bf16[144,512]{1,0:T(8,128)(2,1)S(1)}, bf16[144,512]{1,0:T(8,128)(2,1)S(1)}, u32[]{:S(2)}, u32[]{:S(2)}) collective-permute-start(bf16[144,512]{1,0:T(8,128)(2,1)S(1)} %get-tuple-element.450), channel_id=1, source_target_pairs={{0,16},{2,18},{4,20},{6,22},{8,24},{10,26},{12,28},{14,30},{16,0},... | collective-permute-start | bytes 442376 | tf_op jit(solution)/shard_map/ppermute | solution.py:678
  80.8 4.9 %collective-permute-start.26 = (bf16[96,512]{1,0:T(8,128)(2,1)S(1)}, bf16[96,512]{1,0:T(8,128)(2,1)S(1)}, u32[]{:S(2)}, u32[]{:S(2)}) collective-permute-start(bf16[96,512]{1,0:T(8,128)(2,1)S(1)} %get-tuple-element.434), channel_id=1, source_target_pairs={{0,4},{2,6},{4,0},{6,2},{8,12},{10,14},{12,8},{14,10},{16,20},{18,... | collective-permute-start | bytes 294920 | tf_op jit(solution)/shard_map/ppermute | solution.py:678
  82.4 5.6 %collective-permute-start.27 = (bf16[96,512]{1,0:T(8,128)(2,1)S(1)}, bf16[96,512]{1,0:T(8,128)(2,1)S(1)}, u32[]{:S(2)}, u32[]{:S(2)}) collective-permute-start(bf16[96,512]{1,0:T(8,128)(2,1)S(1)} %get-tuple-element.435), channel_id=1, source_target_pairs={{0,8},{2,10},{4,12},{6,14},{8,0},{10,2},{12,4},{14,6},{16,24},{18,... | collective-permute-start | bytes 294920 | tf_op jit(solution)/shard_map/ppermute | solution.py:678
  83.1 5.0 %collective-permute-start.28 = (bf16[96,512]{1,0:T(8,128)(2,1)S(1)}, bf16[96,512]{1,0:T(8,128)(2,1)S(1)}, u32[]{:S(2)}, u32[]{:S(2)}) collective-permute-start(bf16[96,512]{1,0:T(8,128)(2,1)S(1)} %get-tuple-element.436), channel_id=1, source_target_pairs={{0,2},{2,0},{4,6},{6,4},{8,10},{10,8},{12,14},{14,12},{16,18},{18,... | collective-permute-start | bytes 294920 | tf_op jit(solution)/shard_map/ppermute | solution.py:678
  84.6 10.9 %collective-permute-start.32 = (bf16[144,512]{1,0:T(8,128)(2,1)S(1)}, bf16[144,512]{1,0:T(8,128)(2,1)S(1)}, u32[]{:S(2)}, u32[]{:S(2)}) collective-permute-start(bf16[144,512]{1,0:T(8,128)(2,1)S(1)} %get-tuple-element.460), channel_id=1, source_target_pairs={{0,16},{2,18},{4,20},{6,22},{8,24},{10,26},{12,28},{14,30},{16,0},... | collective-permute-start | bytes 442376 | tf_op jit(solution)/shard_map/ppermute | solution.py:678
  88.9 9.1 %collective-permute-start.31 = (bf16[144,512]{1,0:T(8,128)(2,1)S(1)}, bf16[144,512]{1,0:T(8,128)(2,1)S(1)}, u32[]{:S(2)}, u32[]{:S(2)}) collective-permute-start(bf16[144,512]{1,0:T(8,128)(2,1)S(1)} %get-tuple-element.457), channel_id=1, source_target_pairs={{0,16},{2,18},{4,20},{6,22},{8,24},{10,26},{12,28},{14,30},{16,0},... | collective-permute-start | bytes 442376 | tf_op jit(solution)/shard_map/ppermute | solution.py:678
  90.0 8.0 %collective-permute-start.33 = (f32[9,768]{1,0:T(8,128)S(1)}, f32[9,768]{1,0:T(8,128)S(1)}, u32[]{:S(2)}, u32[]{:S(2)}) collective-permute-start(f32[9,768]{1,0:T(8,128)S(1)} %get-tuple-element.463.refs_13_), channel_id=1, source_target_pairs={{0,16},{2,18},{4,20},{6,22},{8,24},{10,26},{12,28},{14,30},{16,0},... | collective-permute-start | bytes 82952 | tf_op jit(solution)/shard_map/ppermute | solution.py:678
  (15 other events, 58.7 us)
